TPU v7x, 128 devices: a whole 4x4x4 slice. The times are simulated.
128 devices in a mesh: gx: 4 (over y), gy: 4 (over z_lo, core), ta: 8 (over x, z_hi).
Axes of the slice: x: 4, y: 4, z: 4 (z_hi: 2, z_lo: 2; z = z_hi * 2 + z_lo), core: 2. Of those that a mesh axis runs over, the one named last changes fastest.
Arguments:
- tokens: bfloat16 [4, 4, 16, 128, 512], P('gx', 'gy', 'ta'), may hold values from -6 to 6
- norm_gain: float32 [512], replicated, may hold values from 0.1 to 1.9
- w_query: bfloat16 [512, 512], replicated, may hold values from -0.25 to 0.25
- w_key: bfloat16 [512, 512], replicated, may hold values from -0.25 to 0.25
- w_value: bfloat16 [512, 512], replicated, may hold values from -0.25 to 0.25
- w_proj: bfloat16 [512, 512], replicated, may hold values from -0.25 to 0.25
- temper: float32 [8], replicated, may hold values from 1 to 3
- neighbours: int32 [4, 4, 16, 27], P('gx', 'gy', 'ta'), may hold values from 0 to 255, as said below
- valid_mask: int32 [4, 4, 16, 27], P('gx', 'gy', 'ta'), may hold values from 0 to 1, as said below
- cotangent: bfloat16 [4, 4, 16, 128, 512], P('gx', 'gy', 'ta'), may hold values from -6 to 6
Outputs:
- layer_out: bfloat16 [4, 4, 16, 128, 512], P('gx', 'gy', 'ta')
- grad_tokens: float32 [4, 4, 16, 128, 512], P('gx', 'gy', 'ta')
- grad_gain: float32 [512], replicated
- grad_query: float32 [512, 512], replicated
- grad_key: float32 [512, 512], replicated
- grad_value: float32 [512, 512], replicated
- grad_proj: float32 [512, 512], replicated
- grad_temper: float32 [8], replicated
Inputs may be any that keep to these rules, and one draw needn't show every extreme that they name: `neighbours`: row (a, b, c) names the 27 blocks (i, j, k) with i - a, j - b, k - c each in -1, 0, 1 modulo 4, 4, 16, each once, in any order; block (i, j, k) is numbered (i * 4 + j) * 16 + k. `valid_mask`: the entry that names the row's own block is 1.
All inputs are finite; a program needn't handle non-finite values.
Results may differ from a plain program's by a relative error of at most 0.013.
The roundings to bfloat16 on the way count: a program that leaves them out, or rounds other values in their place, can miss the bound.
Values may be sent and summed in bfloat16 or wider, within the bound.
No kernel may reach another device: no remote copies, remote signals or barrier semaphores. Data moves between devices by JAX's collectives and lax.ppermute only.
A program may use at most 192 MiB of HBM per device.

v0:
```python
import jax
import jax.numpy as jnp
from jax import lax
from jax.sharding import PartitionSpec as P

NORM_EPS = 1e-05
HEAD_EPS = 1e-06


def extended(block, sides, width):
    for axis, dim in sides:
        count = lax.axis_size(axis)
        forward = [(i, i + 1) for i in range(count - 1)]
        forward.append((count - 1, 0))
        backward = [(target, source) for source, target in forward]
        low = lax.ppermute(
            lax.slice_in_dim(block, block.shape[dim] - width, None, axis=dim), axis, forward
        )
        high = lax.ppermute(lax.slice_in_dim(block, 0, width, axis=dim), axis, backward)
        block = jnp.concatenate([low, block, high], axis=dim)
    return block


def norm_rows(tokens):
    values = tokens.astype(jnp.float32)
    factor = lax.rsqrt(jnp.mean(values * values, axis=-1, keepdims=True) + NORM_EPS)
    return (values * factor, factor)


def norm_heads(joined, head_count):
    split_shape = joined.shape[:-1] + (head_count, joined.shape[-1] // head_count)
    shaped = joined.reshape(split_shape)
    factor = lax.rsqrt(jnp.mean(shaped * shaped, axis=-1, keepdims=True) + HEAD_EPS)
    return ((shaped * factor).reshape(joined.shape), factor)


def back_heads(normed, factor, upstream, head_count):
    split_shape = normed.shape[:-1] + (head_count, normed.shape[-1] // head_count)
    unit_rows = normed.reshape(split_shape)
    slope_rows = upstream.reshape(split_shape)
    result = factor * (
        slope_rows - unit_rows * jnp.mean(unit_rows * slope_rows, axis=-1, keepdims=True)
    )
    return result.reshape(normed.shape)


def project(inputs, weight):
    return jnp.dot(inputs, weight, preferred_element_type=jnp.float32)


def contract(left_rows, right_rows):
    return lax.dot_general(
        left_rows, right_rows, (((1,), (1,)), ((), ())), preferred_element_type=jnp.float32
    )


def outer_sum(left_rows, right_rows):
    return lax.dot_general(
        left_rows, right_rows, (((0,), (0,)), ((), ())), preferred_element_type=jnp.float32
    )


def local(
    tokens, norm_gain, w_query, w_key, w_value, w_proj, temper, neighbours, valid_mask, cotangent
):
    head_count = temper.shape[0]
    model_width = tokens.shape[-1]
    head_size = model_width // head_count
    block_rows = tokens.shape[3]
    local_t = tokens.shape[2]
    slot_count = neighbours.shape[-1]
    padded_t = local_t + 2
    score_scale = head_size ** (-0.5)
    span_x = lax.axis_size("gx")
    span_y = lax.axis_size("gy")
    span_t = local_t * lax.axis_size("ta")
    anchor_x = lax.axis_index("gx")
    anchor_y = lax.axis_index("gy")
    anchor_t = lax.axis_index("ta") * local_t
    head_ids = jnp.arange(head_count, dtype=jnp.int32)
    local_ids = jnp.arange(local_t, dtype=jnp.int32)
    unit_in, factor = norm_rows(tokens)
    hidden = (unit_in * norm_gain).astype(jnp.bfloat16)
    query_f, query_factor = norm_heads(project(hidden, w_query), head_count)
    key_f, key_factor = norm_heads(project(hidden, w_key), head_count)
    query_n = query_f.astype(jnp.bfloat16)
    key_n = key_f.astype(jnp.bfloat16)
    value_n = project(hidden, w_value).astype(jnp.bfloat16)
    back_mixed = project(cotangent, w_proj.T).astype(jnp.bfloat16)
    margin = extended(
        jnp.concatenate([key_n, value_n], axis=-1), (("gx", 0), ("gy", 1), ("ta", 2)), 1
    )
    key_pad = margin[..., :model_width]
    value_pad = margin[..., model_width:]
    key_flat = key_pad.reshape(9 * padded_t, block_rows, model_width)
    value_flat = value_pad.reshape(9 * padded_t, block_rows, model_width)

    def query_block(packed):
        query_blk, back_blk, block_ids, keep_row, local_pos = packed
        along_t = block_ids % span_t
        along_y = block_ids // span_t % span_y
        along_x = block_ids // (span_t * span_y)
        step_x = (along_x - anchor_x + 1) % span_x
        step_y = (along_y - anchor_y + 1) % span_y
        step_t = (along_t - anchor_t - local_pos + 1) % span_t + local_pos
        slot_rows = (step_x * 3 + step_y) * padded_t + step_t
        keys_all = key_flat[slot_rows].reshape(slot_count * block_rows, model_width)
        values_all = value_flat[slot_rows].reshape(slot_count * block_rows, model_width)
        key_keep = jnp.repeat(keep_row.astype(jnp.float32), block_rows)

        def query_one_head(head_id):
            query_h = lax.dynamic_slice_in_dim(query_blk, head_id * head_size, head_size, 1)
            back_h = lax.dynamic_slice_in_dim(back_blk, head_id * head_size, head_size, 1)
            key_h = lax.dynamic_slice_in_dim(keys_all, head_id * head_size, head_size, 1)
            value_h = lax.dynamic_slice_in_dim(values_all, head_id * head_size, head_size, 1)
            temp_h = temper[head_id]
            scores = contract(query_h, key_h) * score_scale
            weights = jnp.exp(temp_h * scores) * key_keep
            totals = jnp.sum(weights, axis=1)
            probs = weights / totals[:, None]
            probs_b = probs.astype(jnp.bfloat16)
            mixed_h = jnp.dot(probs_b, value_h, preferred_element_type=jnp.float32)
            slopes = contract(back_h, value_h)
            inners = jnp.sum(probs * slopes, axis=1)
            score_grad = probs * (slopes - inners[:, None])
            temper_part = jnp.sum(score_grad * scores)
            scaled = (score_grad * (temp_h * score_scale)).astype(jnp.bfloat16)
            query_grad = jnp.dot(scaled, key_h, preferred_element_type=jnp.float32)
            return (mixed_h, query_grad, totals, inners, temper_part)

        results = lax.map(query_one_head, head_ids)
        mixed_h, query_grad, totals, inners, temper_part = results[:5]
        mixed_blk = (
            jnp.transpose(mixed_h, (1, 0, 2)).reshape(block_rows, model_width).astype(jnp.bfloat16)
        )
        grad_blk = jnp.transpose(query_grad, (1, 0, 2)).reshape(block_rows, model_width)
        outs = (mixed_blk, grad_blk, jnp.stack([totals, inners]), temper_part)
        return (outs, None, None)

    scan_inputs = (query_n[0, 0], back_mixed[0, 0], neighbours[0, 0], valid_mask[0, 0], local_ids)
    mixed_all, query_grads, moments, temper_parts = lax.map(
        lambda packed: query_block(packed)[0], scan_inputs
    )
    joined = extended(
        jnp.concatenate([query_n, back_mixed], axis=-1), (("gx", 0), ("gy", 1), ("ta", 2)), 1
    )
    query_pad = joined[..., :model_width]
    back_pad = joined[..., model_width:]
    stats_pad = extended(
        moments.reshape((1, 1) + moments.shape), (("gx", 0), ("gy", 1), ("ta", 2)), 1
    )
    lists_pad = extended(
        jnp.concatenate([neighbours, valid_mask], axis=-1), (("gx", 0), ("gy", 1), ("ta", 2)), 1
    )
    query_flat = query_pad.reshape(9 * padded_t, block_rows, model_width)
    back_flat = back_pad.reshape(9 * padded_t, block_rows, model_width)
    stats_flat = stats_pad.reshape((9 * padded_t,) + moments.shape[1:])
    lists_flat = lists_pad.reshape(9 * padded_t, 2 * slot_count)
    window = (
        jnp.arange(9, dtype=jnp.int32)[:, None] * padded_t + jnp.arange(3, dtype=jnp.int32)[None, :]
    ).reshape(-1)

    def key_block(packed):
        key_blk, value_blk, local_pos = packed
        slot_rows = window + local_pos
        own_number = (anchor_x * span_y + anchor_y) * span_t + anchor_t + local_pos
        listed = lists_flat[slot_rows]
        attends = jnp.sum(
            jnp.where(listed[:, :slot_count] == own_number, listed[:, slot_count:], 0), axis=1
        )
        query_keep = jnp.repeat(attends.astype(jnp.float32), block_rows)
        queries_all = query_flat[slot_rows].reshape(-1, model_width)
        backs_all = back_flat[slot_rows].reshape(-1, model_width)
        picked = stats_flat[slot_rows]
        totals_all = jnp.transpose(picked[:, 0], (1, 0, 2)).reshape(head_count, -1)
        inners_all = jnp.transpose(picked[:, 1], (1, 0, 2)).reshape(head_count, -1)

        def key_one_head(head_id):
            query_h = lax.dynamic_slice_in_dim(queries_all, head_id * head_size, head_size, 1)
            back_h = lax.dynamic_slice_in_dim(backs_all, head_id * head_size, head_size, 1)
            key_h = lax.dynamic_slice_in_dim(key_blk, head_id * head_size, head_size, 1)
            value_h = lax.dynamic_slice_in_dim(value_blk, head_id * head_size, head_size, 1)
            temp_h = temper[head_id]
            scores = contract(query_h, key_h) * score_scale
            probs = jnp.exp(temp_h * scores) * query_keep[:, None] / totals_all[head_id][:, None]
            probs_b = probs.astype(jnp.bfloat16)
            slopes = contract(back_h, value_h)
            score_grad = probs * (slopes - inners_all[head_id][:, None])
            scaled = (score_grad * (temp_h * score_scale)).astype(jnp.bfloat16)
            key_grad = outer_sum(scaled, query_h)
            value_grad = outer_sum(probs_b, back_h)
            return (key_grad, value_grad)

        key_grad, value_grad = lax.map(key_one_head, head_ids)
        key_out = jnp.transpose(key_grad, (1, 0, 2)).reshape(block_rows, model_width)
        value_out = jnp.transpose(value_grad, (1, 0, 2)).reshape(block_rows, model_width)
        return (key_out, value_out)

    key_grads, value_grads = lax.map(key_block, (key_n[0, 0], value_n[0, 0], local_ids))
    layer_out = project(mixed_all, w_proj).astype(jnp.bfloat16).reshape(tokens.shape)
    query_d = back_heads(
        query_f, query_factor, query_grads.reshape(tokens.shape), head_count
    ).astype(jnp.bfloat16)
    key_d = back_heads(key_f, key_factor, key_grads.reshape(tokens.shape), head_count).astype(
        jnp.bfloat16
    )
    value_d = value_grads.reshape(tokens.shape).astype(jnp.bfloat16)
    hidden_rows = hidden.reshape(-1, model_width)
    back_hidden = (
        project(query_d, w_query.T) + project(key_d, w_key.T) + project(value_d, w_value.T)
    )
    slope_in = back_hidden * norm_gain
    grad_tokens = factor * (
        slope_in - unit_in * jnp.mean(slope_in * unit_in, axis=-1, keepdims=True)
    )
    gain_part = jnp.sum((back_hidden * unit_in).reshape(-1, model_width), axis=0)
    grad_query, grad_key, grad_value, grad_proj, grad_gain, grad_temper = lax.psum(
        (
            outer_sum(hidden_rows, query_d.reshape(-1, model_width)),
            outer_sum(hidden_rows, key_d.reshape(-1, model_width)),
            outer_sum(hidden_rows, value_d.reshape(-1, model_width)),
            outer_sum(mixed_all.reshape(-1, model_width), cotangent.reshape(-1, model_width)),
            gain_part,
            jnp.sum(temper_parts, axis=0),
        ),
        ("gx", "gy", "ta"),
    )
    return (
        layer_out,
        grad_tokens,
        grad_gain,
        grad_query,
        grad_key,
        grad_value,
        grad_proj,
        grad_temper,
    )


def solution(mesh):
    placed = (
        P("gx", "gy", "ta", None, None),
        P(),
        P(),
        P(),
        P(),
        P(),
        P(),
        P("gx", "gy", "ta", None),
        P("gx", "gy", "ta", None),
        P("gx", "gy", "ta", None, None),
    )
    return jax.shard_map(
        local,
        mesh=mesh,
        in_specs=placed,
        out_specs=(
            P("gx", "gy", "ta", None, None),
            P("gx", "gy", "ta", None, None),
            P(),
            P(),
            P(),
            P(),
            P(),
            P(),
        ),
        check_vma=False,
    )
```

profile of v0, /device:TPU:1, one launch (start us, length us, event | category | flops | bytes accessed | tf_op | source)
XLA Modules:
  0.0 1014.8 jit_solution(3526147688756526316)
XLA Ops:
  17.5 11.1 %collective-permute-done = bf16[1,1,2,128,1024]{4,3,2,1,0:T(8,128)(2,1)S(1)} collective-permute-done((bf16[1,1,2,128,1024]{4,3,2,1,0:T(8,128)(2,1)}, bf16[1,1,2,128,1024]{4,3,2,1,0:T(8,128)(2,1)S(1)}, u32[]{:S(2)}, u32[]{:S(2)}) %collective-permute-start) | collective-permute-done | bytes 524320 | tf_op jit(solution)/shard_map/ppermute | solution.py:16
  42.1 11.8 %collective-permute-done.6 = bf16[1,1,2,128,1024]{4,3,2,1,0:T(8,128)(2,1)S(1)} collective-permute-done((bf16[1,1,2,128,1024]{4,3,2,1,0:T(8,128)(2,1)S(1)}, bf16[1,1,2,128,1024]{4,3,2,1,0:T(8,128)(2,1)S(1)}, u32[]{:S(2)}, u32[]{:S(2)}) %collective-permute-start.6) | collective-permute-done | bytes 524320 | tf_op jit(solution)/shard_map/ppermute | solution.py:16
  56.5 10.6 %collective-permute-done.2 = bf16[3,1,2,128,1024]{4,3,2,1,0:T(8,128)(2,1)} collective-permute-done((bf16[3,1,2,128,1024]{4,3,2,1,0:T(8,128)(2,1)}, bf16[3,1,2,128,1024]{4,3,2,1,0:T(8,128)(2,1)}, u32[]{:S(2)}, u32[]{:S(2)}) %collective-permute-start.2) | collective-permute-done | bytes 1572896 | tf_op jit(solution)/shard_map/ppermute | solution.py:16
  70.3 3.4 pad_maximum_fusion.2
  90.1 111.9 %collective-permute-done.14 = s32[3,1,2,54]{3,2,1,0:T(2,128)S(1)} collective-permute-done((s32[3,1,2,54]{3,2,1,0:T(2,128)S(1)}, s32[3,1,2,54]{3,2,1,0:T(2,128)S(1)}, u32[]{:S(2)}, u32[]{:S(2)}) %collective-permute-start.14) | collective-permute-done | bytes 1328 | tf_op jit(solution)/shard_map/ppermute | solution.py:16
  201.9 4.1 collective-permute-done.15
  217.0 3.4 pad_maximum_fusion.3
  224.4 3.7 collective-permute-start.11
  228.2 8.6 pad_maximum_fusion
  236.8 8.6 fusion.110
  246.2 289.6 %while.106 = (s32[]{:T(128)}, bf16[2,128,512]{1,2,0:T(8,128)(2,1)}, f32[2,128,512]{1,2,0:T(8,128)}, f32[2,2,8,128]{3,2,1,0:T(8,128)S(1)}, f32[2,8]{1,0:T(2,128)S...) while((s32[]{:T(128)}, bf16[2,128,512]{1,2,0:T(8,128)(2,1)}, ...), condition=%wide.region_9.10_spmd.clone, body=%wide.region_3.9_spmd.clone.sunk | while | flops 238441568 | bytes 40497868 | solution.py:141
  247.5 5.0 gather_fusion.4
  252.5 4.9 gather_fusion.5
  257.5 132.1 %while.109 = (s32[]{:T(128)}, bf16[8,128,64]{1,2,0:T(8,128)(2,1)S(1)}, f32[8,128,64]{1,2,0:T(8,128)S(1)}, f32[8,128]{1,0:T(8,128)S(1)}, f32[8,128]{1,0:T(8,128)S...) while((s32[]{:T(128)}, ...), condition=%wide.region_8.8_spmd.clone, body=%wide.region_4.7_spmd.clone.sunk | while | flops 238436096 | bytes 25008588 | solution.py:131
  392.3 5.0 gather_fusion.4
  397.3 4.9 gather_fusion.5
  402.3 132.1 %while.109 = (s32[]{:T(128)}, bf16[8,128,64]{1,2,0:T(8,128)(2,1)S(1)}, f32[8,128,64]{1,2,0:T(8,128)S(1)}, f32[8,128]{1,0:T(8,128)S(1)}, f32[8,128]{1,0:T(8,128)S...) while((s32[]{:T(128)}, ...), condition=%wide.region_8.8_spmd.clone, body=%wide.region_4.7_spmd.clone.sunk | while | flops 238436096 | bytes 25008588 | solution.py:131
  538.6 7.7 pad_maximum_fusion.1
  546.3 8.5 fusion.109
  564.7 5.1 collective-permute-start.23
  573.1 263.4 %while.108 = (s32[]{:T(128)}, f32[2,128,512]{1,2,0:T(8,128)}, bf16[2,128,512]{1,2,0:T(8,128)(2,1)}, s32[2]{0:T(128)S(1)}, bf16[36,128,512]{2,1,0:T(8,128)(2,1)},...) while((s32[]{:T(128)}, f32[2,128,512]{1,2,0:T(8,128)}, ...), condition=%wide.region_15.16_spmd.clone, body=%wide.region_11.15_spmd.clone.sunk | while | flops 230034704 | bytes 25472284 | solution.py:199
  577.5 5.0 gather_fusion
  582.6 4.9 gather_fusion.2
  588.2 113.4 %while.110 = (s32[]{:T(128)}, f32[8,128,64]{1,2,0:T(8,128)}, bf16[8,128,64]{1,2,0:T(8,128)(2,1)}, s32[8]{0:T(128)S(1)}, bf16[3456,512]{1,0:T(8,128)(2,1)}, /*ind...) while((s32[]{:T(128)}, f32[8,128,64]{1,2,0:T(8,128)}, ...), condition=%wide.region_14.14_spmd.clone, body=%wide.region_13.13_spmd.clone.sunk | while | flops 230031360 | bytes 9096589 | solution.py:194
  592.8 3.3 fusion.158
  596.1 3.6 fusion.159
  610.3 3.6 fusion.159
  621.1 3.3 fusion.158
  624.4 3.6 fusion.159
  638.6 3.6 fusion.159
  652.8 3.6 fusion.159
  667.0 3.6 fusion.159
  681.2 3.6 fusion.159
  692.0 3.3 fusion.158
  695.3 3.6 fusion.159
  709.2 5.0 gather_fusion
  714.3 4.9 gather_fusion.2
  719.9 113.4 %while.110 = (s32[]{:T(128)}, f32[8,128,64]{1,2,0:T(8,128)}, bf16[8,128,64]{1,2,0:T(8,128)(2,1)}, s32[8]{0:T(128)S(1)}, bf16[3456,512]{1,0:T(8,128)(2,1)}, /*ind...) while((s32[]{:T(128)}, f32[8,128,64]{1,2,0:T(8,128)}, ...), condition=%wide.region_14.14_spmd.clone, body=%wide.region_13.13_spmd.clone.sunk | while | flops 230031360 | bytes 9096589 | solution.py:194
  727.8 3.6 fusion.159
  741.9 3.6 fusion.159
  756.1 3.6 fusion.159
  770.3 3.6 fusion.159
  784.5 3.6 fusion.159
  798.7 3.6 fusion.159
  812.8 3.6 fusion.159
  827.0 3.6 fusion.159
  848.6 66.4 %all-reduce = (f32[512]{0:T(512)}, f32[8]{0:T(128)}) all-reduce(f32[512]{0:T(512)S(1)} %get-tuple-element.752, f32[8]{0:T(128)S(1)} %reduce_sum.117), channel_id=1, replica_groups=mesh['gx'=4,'gy'=4,'ta'=8] {'gx','gy','ta'}, use_global_device_ids=true, to_apply=%region_19.20 | all-reduce | flops 520 | bytes 4160 | tf_op jit(solution)/shard_map/psum | solution.py:217
  916.0 85.3 %all-reduce.4.cloned.1.call-done = (f32[512,512]{1,0:T(8,128)}, f32[512,512]{1,0:T(8,128)}, f32[512,512]{1,0:T(8,128)}, f32[512,512]{1,0:T(8,128)}) async-done(((f32[512,512]{1,0:T(8,128)}, f32[512,512]{1,0:T(8,128)}, f32[512,512]{1,0:T(8,128)}, f32[512,512]{1,0:T(8,128)}), (f32[512,512]{1,0:T(8,128)}, f32[512,512]{1,0:T(8,128)}, f32[512,512]{1,0:T(8,128)}, ...) | async-done | bytes 4194320 | tf_op jit(solution)/shard_map/psum | solution.py:217
  (563 shorter events, 436.8 us)
Async XLA Ops:
  7.2 994.1 %all-reduce.4.cloned.1.call-start = ((), (), s32[]{:S(2)}) async-start(), calls=%async_computation | async-start | bytes 8388608 | tf_op jit(solution)/shard_map/psum | solution.py:217
  8.4 8.5 copy-start.38
  12.1 216.1 %copy-start.5 = (bf16[2,128,512]{2,1,0:T(8,128)(2,1)}, bf16[2,128,512]{2,1,0:T(8,128)(2,1)S(1)}, u32[]{:S(2)}) copy-start(bf16[2,128,512]{2,1,0:T(8,128)(2,1)S(1)} %get-tuple-element.1504) | copy-start | bytes 786436
  12.4 215.7 %copy-start.7 = (bf16[2,128,512]{2,1,0:T(8,128)(2,1)}, bf16[2,128,512]{2,1,0:T(8,128)(2,1)S(1)}, u32[]{:S(2)}) copy-start(bf16[2,128,512]{2,1,0:T(8,128)(2,1)S(1)} %convolution_convert_fusion.1) | copy-start | bytes 786436
  13.3 15.3 %collective-permute-start = (bf16[1,1,2,128,1024]{4,3,2,1,0:T(8,128)(2,1)}, bf16[1,1,2,128,1024]{4,3,2,1,0:T(8,128)(2,1)S(1)}, u32[]{:S(2)}, u32[]{:S(2)}) collective-permute-start(bf16[1,1,2,128,1024]{4,3,2,1,0:T(8,128)(2,1)} %pad_maximum_fusion.6), channel_id=1, source_target_pairs={{0,32},{32,64},{64,96},{96,0},{1,33},{33,65},{65,97},{97,1},{2,34}... | collective-permute-start | bytes 1572872 | tf_op jit(solution)/shard_map/ppermute | solution.py:16
  15.5 13.1 %collective-permute-start.1 = (bf16[1,1,2,128,1024]{4,3,2,1,0:T(8,128)(2,1)}, bf16[1,1,2,128,1024]{4,3,2,1,0:T(8,128)(2,1)S(1)}, u32[]{:S(2)}, u32[]{:S(2)}) collective-permute-start(bf16[1,1,2,128,1024]{4,3,2,1,0:T(8,128)(2,1)} %pad_maximum_fusion.6), channel_id=1, source_target_pairs={{32,0},{64,32},{96,64},{0,96},{33,1},{65,33},{97,65},{1,97},{34,2}... | collective-permute-start | bytes 1572872 | tf_op jit(solution)/shard_map/ppermute | solution.py:19
  17.5 16.4 %copy-start.17 = (f32[2,128,512]{1,2,0:T(8,128)}, f32[2,128,512]{1,2,0:T(8,128)S(1)}, u32[]{:S(2)}) copy-start(f32[2,128,512]{1,2,0:T(8,128)S(1)} %copy.28) | copy-start | bytes 1572868
  28.6 10.6 %copy-start.11 = (bf16[1,1,2,128,1024]{4,3,2,1,0:T(8,128)(2,1)}, bf16[1,1,2,128,1024]{4,3,2,1,0:T(8,128)(2,1)S(1)}, u32[]{:S(2)}) copy-start(bf16[1,1,2,128,1024]{4,3,2,1,0:T(8,128)(2,1)S(1)} %collective-permute-done.1) | copy-start | bytes 1572868
  30.0 37.1 %collective-permute-start.2 = (bf16[3,1,2,128,1024]{4,3,2,1,0:T(8,128)(2,1)}, bf16[3,1,2,128,1024]{4,3,2,1,0:T(8,128)(2,1)}, u32[]{:S(2)}, u32[]{:S(2)}) collective-permute-start(bf16[3,1,2,128,1024]{4,3,2,1,0:T(8,128)(2,1)} %pad_maximum_fusion.4), channel_id=1, source_target_pairs={{0,8},{8,16},{16,24},{24,0},{1,9},{9,17},{17,25},{25,1},{2,10},{10... | collective-permute-start | bytes 4718600 | tf_op jit(solution)/shard_map/ppermute | solution.py:16
  32.9 37.4 %collective-permute-start.3 = (bf16[3,1,2,128,1024]{4,3,2,1,0:T(8,128)(2,1)}, bf16[3,1,2,128,1024]{4,3,2,1,0:T(8,128)(2,1)}, u32[]{:S(2)}, u32[]{:S(2)}) collective-permute-start(bf16[3,1,2,128,1024]{4,3,2,1,0:T(8,128)(2,1)} %pad_maximum_fusion.4), channel_id=1, source_target_pairs={{8,0},{16,8},{24,16},{0,24},{9,1},{17,9},{25,17},{1,25},{10,2},{18... | collective-permute-start | bytes 4718600 | tf_op jit(solution)/shard_map/ppermute | solution.py:19
  39.2 31.0 %copy-start.12 = (bf16[1,1,2,128,1024]{4,3,2,1,0:T(8,128)(2,1)S(1)}, bf16[1,1,2,128,1024]{4,3,2,1,0:T(8,128)(2,1)}, u32[]{:S(2)}) copy-start(bf16[1,1,2,128,1024]{4,3,2,1,0:T(8,128)(2,1)} %copy-done.11) | copy-start | bytes 1572868
  39.3 14.6 %collective-permute-start.6 = (bf16[1,1,2,128,1024]{4,3,2,1,0:T(8,128)(2,1)S(1)}, bf16[1,1,2,128,1024]{4,3,2,1,0:T(8,128)(2,1)S(1)}, u32[]{:S(2)}, u32[]{:S(2)}) collective-permute-start(bf16[1,1,2,128,1024]{4,3,2,1,0:T(8,128)(2,1)S(1)} %pad_maximum_fusion.7), channel_id=1, source_target_pairs={{0,32},{32,64},{64,96},{96,0},{1,33},{33,65},{65,97},{97,1},{2,34}... | collective-permute-start | bytes 1572872 | tf_op jit(solution)/shard_map/ppermute | solution.py:16
  40.7 13.2 %collective-permute-start.7 = (bf16[1,1,2,128,1024]{4,3,2,1,0:T(8,128)(2,1)S(1)}, bf16[1,1,2,128,1024]{4,3,2,1,0:T(8,128)(2,1)S(1)}, u32[]{:S(2)}, u32[]{:S(2)}) collective-permute-start(bf16[1,1,2,128,1024]{4,3,2,1,0:T(8,128)(2,1)S(1)} %pad_maximum_fusion.7), channel_id=1, source_target_pairs={{32,0},{64,32},{96,64},{0,96},{33,1},{65,33},{97,65},{1,97},{34,2}... | collective-permute-start | bytes 1572872 | tf_op jit(solution)/shard_map/ppermute | solution.py:19
  53.9 163.1 %copy-start.9 = (bf16[1,1,2,128,1024]{4,3,2,1,0:T(8,128)(2,1)}, bf16[1,1,2,128,1024]{4,3,2,1,0:T(8,128)(2,1)S(1)}, u32[]{:S(2)}) copy-start(bf16[1,1,2,128,1024]{4,3,2,1,0:T(8,128)(2,1)S(1)} %collective-permute-done.6) | copy-start | bytes 1572868
  53.9 163.1 %copy-start.10 = (bf16[1,1,2,128,1024]{4,3,2,1,0:T(8,128)(2,1)}, bf16[1,1,2,128,1024]{4,3,2,1,0:T(8,128)(2,1)S(1)}, u32[]{:S(2)}) copy-start(bf16[1,1,2,128,1024]{4,3,2,1,0:T(8,128)(2,1)S(1)} %collective-permute-done.7) | copy-start | bytes 1572868
  55.4 161.5 %collective-permute-start.8 = (bf16[3,1,2,128,1024]{4,3,2,1,0:T(8,128)(2,1)}, bf16[3,1,2,128,1024]{4,3,2,1,0:T(8,128)(2,1)}, u32[]{:S(2)}, u32[]{:S(2)}) collective-permute-start(bf16[3,1,2,128,1024]{4,3,2,1,0:T(8,128)(2,1)} %pad_maximum_fusion.5), channel_id=1, source_target_pairs={{0,8},{8,16},{16,24},{24,0},{1,9},{9,17},{17,25},{25,1},{2,10},{10... | collective-permute-start | bytes 4718600 | tf_op jit(solution)/shard_map/ppermute | solution.py:16
  56.5 160.5 %collective-permute-start.9 = (bf16[3,1,2,128,1024]{4,3,2,1,0:T(8,128)(2,1)}, bf16[3,1,2,128,1024]{4,3,2,1,0:T(8,128)(2,1)}, u32[]{:S(2)}, u32[]{:S(2)}) collective-permute-start(bf16[3,1,2,128,1024]{4,3,2,1,0:T(8,128)(2,1)} %pad_maximum_fusion.5), channel_id=1, source_target_pairs={{8,0},{16,8},{24,16},{0,24},{9,1},{17,9},{25,17},{1,25},{10,2},{18... | collective-permute-start | bytes 4718600 | tf_op jit(solution)/shard_map/ppermute | solution.py:19
  73.7 8.2 copy-start.40
  73.7 8.2 copy-start.41
  76.4 151.8 %collective-permute-start.4 = (bf16[3,3,1,128,1024]{4,3,2,1,0:T(8,128)(2,1)}, bf16[3,3,1,128,1024]{4,3,2,1,0:T(8,128)(2,1)}, u32[]{:S(2)}, u32[]{:S(2)}) collective-permute-start(bf16[3,3,1,128,1024]{4,3,2,1,0:T(8,128)(2,1)} %get-tuple-element.890), channel_id=1, source_target_pairs={{0,1},{1,2},{2,3},{3,4},{4,5},{5,6},{6,7},{7,0},{8,9},{9,10},{10,1... | collective-permute-start | bytes 7077896 | tf_op jit(solution)/shard_map/ppermute | solution.py:16
  79.7 148.5 %collective-permute-start.5 = (bf16[3,3,1,128,1024]{4,3,2,1,0:T(8,128)(2,1)}, bf16[3,3,1,128,1024]{4,3,2,1,0:T(8,128)(2,1)}, u32[]{:S(2)}, u32[]{:S(2)}) collective-permute-start(bf16[3,3,1,128,1024]{4,3,2,1,0:T(8,128)(2,1)} %get-tuple-element.891), channel_id=1, source_target_pairs={{1,0},{2,1},{3,2},{4,3},{5,4},{6,5},{7,6},{0,7},{9,8},{10,9},{11,1... | collective-permute-start | bytes 7077896 | tf_op jit(solution)/shard_map/ppermute | solution.py:19
  81.9 4.0 collective-permute-start.12
  86.0 2.8 collective-permute-start.13
  88.9 113.1 %collective-permute-start.14 = (s32[3,1,2,54]{3,2,1,0:T(2,128)S(1)}, s32[3,1,2,54]{3,2,1,0:T(2,128)S(1)}, u32[]{:S(2)}, u32[]{:S(2)}) collective-permute-start(s32[3,1,2,54]{3,2,1,0:T(2,128)S(1)} %pad_add_fusion.2), channel_id=1, source_target_pairs={{0,8},{8,16},{16,24},{24,0},{1,9},{9,17},{17,25},{25,1},{2,10},{10... | collective-permute-start | bytes 3896 | tf_op jit(solution)/shard_map/ppermute | solution.py:16
  201.9 4.1 collective-permute-start.15
  206.1 6.1 collective-permute-start.16
  212.3 4.0 collective-permute-start.17
  223.0 315.6 %collective-permute-start.10 = (bf16[3,3,1,128,1024]{4,3,2,1,0:T(8,128)(2,1)}, bf16[3,3,1,128,1024]{4,3,2,1,0:T(8,128)(2,1)}, u32[]{:S(2)}, u32[]{:S(2)}) collective-permute-start(bf16[3,3,1,128,1024]{4,3,2,1,0:T(8,128)(2,1)} %get-tuple-element.888), channel_id=1, source_target_pairs={{0,1},{1,2},{2,3},{3,4},{4,5},{5,6},{6,7},{7,0},{8,9},{9,10},{10,1... | collective-permute-start | bytes 7077896 | tf_op jit(solution)/shard_map/ppermute | solution.py:16
  224.4 314.2 %collective-permute-start.11 = (bf16[3,3,1,128,1024]{4,3,2,1,0:T(8,128)(2,1)}, bf16[3,3,1,128,1024]{4,3,2,1,0:T(8,128)(2,1)}, u32[]{:S(2)}, u32[]{:S(2)}) collective-permute-start(bf16[3,3,1,128,1024]{4,3,2,1,0:T(8,128)(2,1)} %get-tuple-element.889), channel_id=1, source_target_pairs={{1,0},{2,1},{3,2},{4,3},{5,4},{6,5},{7,6},{0,7},{9,8},{10,9},{11,1... | collective-permute-start | bytes 7077896 | tf_op jit(solution)/shard_map/ppermute | solution.py:19
  236.8 9.4 copy-start.43
  535.8 22.1 %collective-permute-start.18 = (f32[1,1,2,2,8,128]{5,4,3,2,1,0:T(8,128)S(1)}, f32[1,1,2,2,8,128]{5,4,3,2,1,0:T(8,128)S(1)}, u32[]{:S(2)}, u32[]{:S(2)}) collective-permute-start(f32[1,1,2,2,8,128]{5,4,3,2,1,0:T(8,128)S(1)} %bitcast.281), channel_id=1, source_target_pairs={{0,32},{32,64},{64,96},{96,0},{1,33},{33,65},{65,97},{97,1},{2,34}... | collective-permute-start | bytes 49160 | tf_op jit(solution)/shard_map/ppermute | solution.py:16
  537.2 20.7 %collective-permute-start.19 = (f32[1,1,2,2,8,128]{5,4,3,2,1,0:T(8,128)S(1)}, f32[1,1,2,2,8,128]{5,4,3,2,1,0:T(8,128)S(1)}, u32[]{:S(2)}, u32[]{:S(2)}) collective-permute-start(f32[1,1,2,2,8,128]{5,4,3,2,1,0:T(8,128)S(1)} %bitcast.282), channel_id=1, source_target_pairs={{32,0},{64,32},{96,64},{0,96},{33,1},{65,33},{97,65},{1,97},{34,2}... | collective-permute-start | bytes 49160 | tf_op jit(solution)/shard_map/ppermute | solution.py:19
  546.3 8.6 copy-start.20
  546.3 9.6 copy-start.18
  546.3 9.6 copy-start.37
  556.0 13.8 %copy-start.4 = (bf16[1,1,2,128,512]{4,3,2,1,0:T(8,128)(2,1)S(1)}, bf16[1,1,2,128,512]{4,3,2,1,0:T(8,128)(2,1)}, u32[]{:S(2)}) copy-start(bf16[1,1,2,128,512]{4,3,2,1,0:T(8,128)(2,1)} %param.18) | copy-start | bytes 786436
  556.0 13.8 %copy-start.33 = (f32[512]{0:T(512)S(1)}, f32[512]{0:T(512)}, u32[]{:S(2)}) copy-start(f32[512]{0:T(512)} %param.19) | copy-start | bytes 6148
  556.0 13.8 %copy-start.39 = (f32[2,128]{1,0:T(2,128)S(1)}, f32[2,128]{1,0:T(2,128)}, u32[]{:S(2)}) copy-start(f32[2,128]{1,0:T(2,128)} %copy-done.38) | copy-start | bytes 3076
  556.3 16.8 %copy-start.2 = (s32[36,54]{1,0:T(8,128)S(1)}, s32[36,54]{1,0:T(8,128)}, u32[]{:S(2)}) copy-start(s32[36,54]{1,0:T(8,128)} %reshape.687) | copy-start | bytes 23332
  556.3 16.8 %copy-start.6 = (bf16[2,128,512]{2,1,0:T(8,128)(2,1)S(1)}, bf16[2,128,512]{2,1,0:T(8,128)(2,1)}, u32[]{:S(2)}) copy-start(bf16[2,128,512]{2,1,0:T(8,128)(2,1)} %copy-done.5) | copy-start | bytes 786436
  556.3 16.8 %copy-start.8 = (bf16[2,128,512]{2,1,0:T(8,128)(2,1)S(1)}, bf16[2,128,512]{2,1,0:T(8,128)(2,1)}, u32[]{:S(2)}) copy-start(bf16[2,128,512]{2,1,0:T(8,128)(2,1)} %copy-done.7) | copy-start | bytes 786436
  556.3 16.8 %copy-start.42 = (s32[9]{0:T(128)S(1)}, s32[9]{0:T(128)}, u32[]{:S(2)}) copy-start(s32[9]{0:T(128)} %iota_multiply_fusion) | copy-start | bytes 112
  557.7 15.4 %copy-start.21 = (bf16[2,128,512]{2,1,0:T(8,128)(2,1)}, bf16[2,128,512]{2,1,0:T(8,128)(2,1)S(1)}, u32[]{:S(2)}) copy-start(bf16[2,128,512]{2,1,0:T(8,128)(2,1)S(1)} %multiply_convert_fusion.3) | copy-start | bytes 786436
  558.0 5.3 collective-permute-start.20
  561.0 3.6 collective-permute-start.21
  564.6 6.9 collective-permute-start.22
  564.7 6.8 collective-permute-start.23
  573.1 265.6 %copy-start.35 = (f32[2,128,8]{1,2,0:T(8,128)S(1)}, f32[2,128,8]{1,2,0:T(8,128)}, u32[]{:S(2)}) copy-start(f32[2,128,8]{1,2,0:T(8,128)} %copy-done.34) | copy-start | bytes 24580
  (36 other events, 94.5 us)
Sparse Core Ops, SparseCore 0:
  845.5 155.8 all-reduce.3
where the time goes:
time: 1020 us; the launch traced here: 1010 us
  matrix products  305 us (30%)
  waiting for transfers between devices  247 us (24%)
  local copies, waits for them, and re-layouts  172 us (17%)
  loops' own time  105 us (10%)
  blocking collectives  66.4 us (7%)
  other arithmetic  62.9 us (6%)
  starting transfers between devices  41.2 us (4%)
  between operations  14.6 us (1%)
    ppermute x12, waiting for transfers between devices, extended(): lax.ppermute(lax.slice_in_dim(block, block.shape[dim] - width, None, axis...  151 us
    dot_general x48, matrix products, contract(): lax.dot_general(left_rows, right_rows, (((1,), (1,)), ((), ())), preferre...  113 us
    dot_general x36, matrix products, outer_sum(): lax.dot_general(left_rows, right_rows, (((0,), (0,)), ((), ())), preferre...  107 us
    psum x1, waiting for transfers between devices, local(): lax.psum((outer_sum(hidden_rows, query_d.reshape(-1, model_width)), outer...  85.3 us
    psum x1, blocking collectives, local(): lax.psum((outer_sum(hidden_rows, query_d.reshape(-1, model_width)), outer...  66.4 us
    another operation x2, loops' own time, key_block(): key_grad, value_grad = lax.map(key_one_head, head_ids)  52.2 us
    another operation x2, loops' own time, query_block(): results = lax.map(query_one_head, head_ids)  51.3 us
    dot_general x16, matrix products, query_one_head(): query_grad = jnp.dot(scaled, key_h, preferred_element_type=jnp.float32)  43.6 us
  transfers between devices with their start and end apart: 25, of which 13 were waited for; matrix products, arithmetic and copies ran while one was open for 28% of the time, Pallas kernels for 0%

commit v1 on v0

v1 whole, which is shorter than its diff:
```python
import math

import jax
import jax.numpy as jnp
from jax import lax
from jax.experimental import pallas as pl
from jax.experimental.pallas import tpu as pltpu
from jax.sharding import Mesh, PartitionSpec as P

NORM_EPS = 1e-05
HEAD_EPS = 1e-06
D = 512
H = 8
DH = 64
BLK = 128
NB = 27
ROWS = 256
SCALE = DH**-0.5
BF = jnp.bfloat16
F32 = jnp.float32
ZLINE = ("zl", "cr", "zh")
PLANE = ("gx", "tx")
ALL = ("gx", "zl", "cr", "tx", "zh")
VMEM_LIMIT = 56 * 1024 * 1024


def params():
    return pltpu.CompilerParams(vmem_limit_bytes=VMEM_LIMIT)


def dot_nn(left, right):
    return jnp.dot(left, right, preferred_element_type=F32)


def dot_nt(left, right):
    return lax.dot_general(left, right, (((1,), (1,)), ((), ())), preferred_element_type=F32)


def dot_tn(left, right):
    return lax.dot_general(left, right, (((0,), (0,)), ((), ())), preferred_element_type=F32)


def head(values, index):
    return values[:, index * DH : (index + 1) * DH]


def normed_hidden(tok_ref, gain_ref):
    values = tok_ref[...].astype(F32)
    factor = lax.rsqrt(jnp.mean(values * values, axis=-1, keepdims=True) + NORM_EPS)
    unit = values * factor
    return unit, factor, (unit * gain_ref[...]).astype(BF)


def project_kernel(tok, gain, cot, keep, wq, wk, wv, wp, kv_out, qb_out, qf_out, kf_out):
    _, _, hidden = normed_hidden(tok, gain)
    key_f = dot_nn(hidden, wk[...])
    value = dot_nn(hidden, wv[...]).astype(BF)
    kf_out[...] = key_f
    for h in range(H):
        part = head(key_f, h)
        factor = lax.rsqrt(jnp.mean(part * part, axis=-1, keepdims=True) + HEAD_EPS)
        kv_out[h] = jnp.concatenate([(part * factor).astype(BF), head(value, h)], axis=1)
    query_f = dot_nn(hidden, wq[...])
    back = dot_nt(cot[...], wp[...]).astype(BF)
    qf_out[...] = query_f
    for h in range(H):
        part = head(query_f, h)
        factor = lax.rsqrt(jnp.mean(part * part, axis=-1, keepdims=True) + HEAD_EPS)
        qb_out[h, :ROWS] = jnp.concatenate([(part * factor).astype(BF), head(back, h)], axis=1)
        qb_out[h, ROWS:] = keep[...]


def attend_kernel(
    coef, keep, own, xm, xp, tm, tp, cmm, cmp, cpm, cpp, qb,
    mq_out, own_out, xm_out, xp_out, tm_out, tp_out, cmm_out, cmp_out, cpm_out, cpp_out,
    kvall, kvt, acc, wbuf, sems,
):
    moves = [
        (cmm, 0, 0), (xm, 0, None), (cmp, 0, 5),
        (tm, 1, 0), (own, 1, None), (tp, 1, 5),
        (cpm, 2, 0), (xp, 2, None), (cpp, 2, 5),
    ]
    copies = []
    for number, (src, dx, slot) in enumerate(moves):
        dst = kvall.at[dx, :, pl.ds(1, 4)] if slot is None else kvall.at[dx, :, slot]
        copies.append(pltpu.make_async_copy(src, dst, sems.at[number]))
    for copy in copies:
        copy.start()
    acc[...] = jnp.zeros_like(acc)
    for copy in copies:
        copy.wait()
    for dx in range(3):
        for y in range(4):
            for t in range(6):
                kvt[dx, y, :, t * BLK : (t + 1) * BLK] = kvall[dx, y, t].T

    exp_coef = coef[0]
    grad_coef = coef[1]
    lane = lax.broadcasted_iota(jnp.int32, (BLK, 2 * DH), 1)
    low = (lane < DH).astype(F32).astype(BF)
    high = (lane >= DH).astype(F32).astype(BF)

    def fold(values):
        return jnp.sum(values.reshape(-1, 8, BLK), axis=0)

    def one_block(number, carry):
        y = number // 4
        t = number % 4
        rows = pl.multiple_of((t % 2) * BLK, BLK)
        both = qb[y * 2 + t // 2, pl.ds(rows, BLK), :]
        spread = jnp.concatenate([both * low, both * high], axis=0)
        total = jnp.zeros((8, BLK), F32)
        inner = jnp.zeros((8, BLK), F32)
        for g in range(9):
            dx, dy = g // 3, g % 3
            yy = (y + dy + 3) % 4
            keys = kvall[dx, yy, pl.ds(t, 3)].reshape(3 * BLK, 2 * DH)
            pair = dot_nt(keys, spread)
            for k in range(3):
                score = pair[k * BLK : (k + 1) * BLK, :BLK]
                slope = pair[k * BLK : (k + 1) * BLK, BLK:]
                weight = jnp.exp2(score * exp_coef) * keep[number * NB + g * 3 + k]
                total = total + fold(weight)
                inner = inner + fold(weight * slope)
                base = (g * 3 + k) * BLK
                wbuf[base : base + BLK, :BLK] = weight
                wbuf[base : base + BLK, BLK:] = slope
        total_row = jnp.sum(total, axis=0, keepdims=True)
        inverse = 1.0 / total_row
        inner_row = jnp.sum(inner, axis=0, keepdims=True) * inverse
        out = jnp.zeros((2 * DH, 2 * BLK), F32)
        for g in range(9):
            dx, dy = g // 3, g % 3
            yy = (y + dy + 3) % 4
            base = g * 3 * BLK
            prob = wbuf[base : base + 3 * BLK, :BLK] * inverse
            slope = wbuf[base : base + 3 * BLK, BLK:]
            scaled = (prob * (slope - inner_row)) * grad_coef
            mixed = jnp.concatenate([scaled.astype(BF), prob.astype(BF)], axis=1)
            update = dot_nn(mixed, spread)
            acc[dx, yy, pl.ds(t, 3)] += update.reshape(3, BLK, 2 * DH)
            lanes = pl.multiple_of(t * BLK, BLK)
            out = out + dot_nn(kvt[dx, yy, :, pl.ds(lanes, 3 * BLK)], mixed)
        mq_out[number] = jnp.concatenate([out[DH:, BLK:].T, out[:DH, :BLK].T], axis=1).astype(BF)
        return carry

    lax.fori_loop(0, 16, one_block, 0)
    own_out[...] = acc[1, :, 1:5]
    for out_ref, dx in ((xm_out, 0), (xp_out, 2)):
        out_ref[...] = acc[dx, :, 1:5].astype(BF)
    for out_ref, dx, slot in (
        (tm_out, 1, 0), (tp_out, 1, 5), (cmm_out, 0, 0),
        (cmp_out, 0, 5), (cpm_out, 2, 0), (cpp_out, 2, 5),
    ):
        out_ref[...] = acc[dx, :, slot].astype(BF)


def gather_kernel(own, rx0, rx2, lo0, lo1, lo2, hi0, hi1, hi2, out):
    total = own[...] + rx0[...].astype(F32) + rx2[...].astype(F32)
    first = lo0[...].astype(F32) + lo1[...].astype(F32) + lo2[...].astype(F32)
    last = hi0[...].astype(F32) + hi1[...].astype(F32) + hi2[...].astype(F32)
    out[:, 1:3] = total[:, 1:3].astype(BF)
    out[:, 0] = (total[:, 0] + first).astype(BF)
    out[:, 3] = (total[:, 3] + last).astype(BF)


def finish_kernel(
    tok, gain, cot, mq, kv, qf, kf, wq, wk, wv, wp, layer_out, grad_tok, parts
):
    unit, factor_in, hidden = normed_hidden(tok, gain)
    mixed = jnp.concatenate([mq[h][:, :DH] for h in range(H)], axis=1)
    layer_out[...] = dot_nn(mixed, wp[...]).astype(BF)
    query_grad = jnp.concatenate([mq[h][:, DH:] for h in range(H)], axis=1)
    key_grad = jnp.concatenate([kv[h][:, :DH] for h in range(H)], axis=1)
    value_d = jnp.concatenate([kv[h][:, DH:] for h in range(H)], axis=1)

    def back(flat, upstream):
        pieces, units = [], []
        for h in range(H):
            part = head(flat, h)
            slope = head(upstream, h).astype(F32)
            factor = lax.rsqrt(jnp.mean(part * part, axis=-1, keepdims=True) + HEAD_EPS)
            normed = part * factor
            pieces.append(
                (slope - normed * jnp.mean(normed * slope, axis=-1, keepdims=True)) * factor
            )
            units.append(normed)
        return jnp.concatenate(pieces, axis=1).astype(BF), jnp.concatenate(units, axis=1)

    query_d, query_n = back(qf[...], query_grad)
    key_d, _ = back(kf[...], key_grad)
    temper_part = jnp.sum(
        query_n.astype(BF).astype(F32) * query_grad.astype(F32), axis=0, keepdims=True
    )
    back_hidden = dot_nt(query_d, wq[...]) + dot_nt(key_d, wk[...]) + dot_nt(value_d, wv[...])
    slope_in = back_hidden * gain[...]
    grad_tok[...] = factor_in * (
        slope_in - unit * jnp.mean(slope_in * unit, axis=-1, keepdims=True)
    )
    gain_part = jnp.sum(back_hidden * unit, axis=0, keepdims=True)
    extras = jnp.concatenate(
        [gain_part[:, c * 128 : (c + 1) * 128] for c in range(4)]
        + [temper_part[:, c * 128 : (c + 1) * 128] for c in range(4)],
        axis=0,
    )
    parts[:, 64:72] = jnp.broadcast_to(extras.astype(BF)[None], (128, 8, 128))
    left = (hidden, hidden, hidden, mixed)
    right = (query_d, key_d, value_d, cot[...])
    for w in range(4):
        grad = dot_tn(left[w], right[w]).astype(BF)
        for c in range(4):
            parts[w * 32 : (w + 1) * 32, c * 16 : (c + 1) * 16] = grad[
                :, c * 128 : (c + 1) * 128
            ].reshape(32, 16, 128)


def whole(shape, dtype):
    return jax.ShapeDtypeStruct(shape, dtype)


def exchange(block, dx, dt):
    pairs = [
        (a * 4 + b, ((a + dx) % 4) * 4 + (b + dt) % 4) for a in range(4) for b in range(4)
    ]
    return lax.ppermute(block, PLANE, pairs)


def local(
    tokens, norm_gain, w_query, w_key, w_value, w_proj, temper, neighbours, valid_mask, cotangent
):
    tok = tokens.reshape(ROWS, D)
    cot = cotangent.reshape(ROWS, D)
    gain = norm_gain.reshape(1, D)
    place_x = lax.axis_index("gx")
    place_y = lax.axis_index("zl") * 2 + lax.axis_index("cr")
    place_t = (lax.axis_index("tx") * 2 + lax.axis_index("zh")) * 2 + jnp.arange(2)[:, None]
    ids = neighbours.reshape(2, NB)
    step_t = (ids % 16 - place_t + 1) % 16
    step_y = (ids // 16 % 4 - place_y + 1) % 4
    step_x = (ids // 64 - place_x + 1) % 4
    slots = step_x * 9 + step_y * 3 + step_t
    kept = jnp.sum(
        jnp.where(
            slots[:, :, None] == jnp.arange(128)[None, None, :],
            valid_mask.reshape(2, NB)[:, :, None],
            0,
        ),
        axis=1,
    )
    keep_rows = jnp.pad(kept.astype(BF), ((0, 14), (0, 0)))

    kv_send, qb_send, query_f, key_f = pl.pallas_call(
        project_kernel,
        out_shape=(
            whole((H, ROWS, 2 * DH), BF),
            whole((H, ROWS + 16, 2 * DH), BF),
            whole((ROWS, D), F32),
            whole((ROWS, D), F32),
        ),
        compiler_params=params(),
    )(tok, gain, cot, keep_rows, w_query, w_key, w_value, w_proj)

    own = lax.all_to_all(kv_send, ZLINE, 0, 0, tiled=True).reshape(4, 4, BLK, 2 * DH)
    late, early = own[:, 3], own[:, 0]
    xm = exchange(own, 1, 0)
    xp = exchange(own, -1, 0)
    tm = exchange(late, 0, 1)
    tp = exchange(early, 0, -1)
    cmm = exchange(late, 1, 1)
    cmp = exchange(early, 1, -1)
    cpm = exchange(late, -1, 1)
    cpp = exchange(early, -1, -1)
    qb = lax.all_to_all(qb_send, ZLINE, 0, 0, tiled=True)
    keep = qb[:, ROWS : ROWS + 2, :NB].astype(F32).reshape(16 * NB)
    head_id = (lax.axis_index("zl") * 2 + lax.axis_index("cr")) * 2 + lax.axis_index("zh")
    temp = temper[head_id] * SCALE
    coef = jnp.stack([temp * math.log2(math.e), temp])

    any_spec = pl.BlockSpec(memory_space=pl.ANY)
    smem = pl.BlockSpec(memory_space=pltpu.SMEM)
    vmem = pl.BlockSpec(memory_space=pltpu.VMEM)
    full = (4, 4, BLK, 2 * DH)
    edge = (4, BLK, 2 * DH)
    outs = pl.pallas_call(
        attend_kernel,
        out_shape=(
            whole((16, BLK, 2 * DH), BF), whole(full, F32), whole(full, BF), whole(full, BF),
        ) + tuple(whole(edge, BF) for _ in range(6)),
        in_specs=[smem, smem] + [any_spec] * 9 + [vmem],
        out_specs=tuple([vmem] * 10),
        scratch_shapes=[
            pltpu.VMEM((3, 4, 6, BLK, 2 * DH), BF),
            pltpu.VMEM((3, 4, 2 * DH, 6 * BLK), BF),
            pltpu.VMEM((3, 4, 6, BLK, 2 * DH), F32),
            pltpu.VMEM((NB * BLK, 2 * BLK), F32),
            pltpu.SemaphoreType.DMA((9,)),
        ],
        compiler_params=params(),
    )(coef, keep, own, xm, xp, tm, tp, cmm, cmp, cpm, cpp, qb)
    mq_send, own_grad, gxm, gxp, gtm, gtp, gmm, gmp, gpm, gpp = outs
    rx0 = exchange(gxm, -1, 0)
    rx2 = exchange(gxp, 1, 0)
    hi0 = exchange(gtm, 0, -1)
    lo0 = exchange(gtp, 0, 1)
    hi1 = exchange(gmm, -1, -1)
    lo1 = exchange(gmp, -1, 1)
    hi2 = exchange(gpm, 1, -1)
    lo2 = exchange(gpp, 1, 1)
    mq = lax.all_to_all(mq_send.reshape(H, ROWS, 2 * DH), ZLINE, 0, 0, tiled=True)
    kv_grad = pl.pallas_call(
        gather_kernel, out_shape=whole(full, BF), compiler_params=params()
    )(own_grad, rx0, rx2, lo0, lo1, lo2, hi0, hi1, hi2)
    kv = lax.all_to_all(kv_grad.reshape(H, ROWS, 2 * DH), ZLINE, 0, 0, tiled=True)

    layer_out, grad_tokens, parts = pl.pallas_call(
        finish_kernel,
        out_shape=(whole((ROWS, D), BF), whole((ROWS, D), F32), whole((128, 72, 128), BF)),
        compiler_params=params(),
    )(tok, gain, cot, mq, kv, query_f, key_f, w_query, w_key, w_value, w_proj)

    arrived = lax.all_to_all(parts, ALL, 0, 0, tiled=True)
    summed = jnp.sum(arrived.astype(F32), axis=0)
    grad_gain = summed[64:68].reshape(D)
    grad_temper = jnp.sum(summed[68:72].reshape(H, DH), axis=1) / temper
    share = jnp.broadcast_to(summed[:64].astype(BF)[None], (128, 64, 128))
    shares = lax.all_to_all(share, ALL, 0, 0, tiled=True)
    grads = jnp.transpose(shares.reshape(4, 32, 4, 16, 128), (0, 1, 3, 2, 4))
    grads = grads.reshape(4, D, D).astype(F32)
    return (
        layer_out.reshape(tokens.shape),
        grad_tokens.reshape(tokens.shape),
        grad_gain,
        grads[0],
        grads[1],
        grads[2],
        grads[3],
        grad_temper,
    )


def solution(mesh):
    fine = Mesh(mesh.devices.reshape(4, 2, 2, 4, 2), ALL)
    lattice = ("gx", ("zl", "cr"), ("tx", "zh"))
    blocks = P(*lattice, None, None)
    lists = P(*lattice, None)
    return jax.shard_map(
        local,
        mesh=fine,
        in_specs=(blocks, P(), P(), P(), P(), P(), P(), lists, lists, blocks),
        out_specs=(blocks, blocks, P(), P(), P(), P(), P(), P()),
        check_vma=False,
    )
```

time: 1020 us -> 230 us (0.23)
  matrix products: 305 us -> 0 us
  waiting for transfers between devices: 247 us -> 50.2 us
  local copies, waits for them, and re-layouts: 172 us -> 13.2 us
  loops' own time: 105 us -> 0 us
  other arithmetic: 62.9 us -> 2.99 us
  Pallas kernels: 0 us -> 54.4 us
  between operations: 14.6 us -> 2.22 us
    dot_general x124 -> x0, matrix products: 305 us -> none  [the longest x48 113 us: contract(): lax.dot_general(left_rows, right_rows, (((1,), (1,)), ((), ())), preferre...]
    ppermute x24 -> x16, waiting for transfers between devices: 162 us -> 20.8 us  [exchange(): return lax.ppermute(block, PLANE, pairs)]
    another operation x6 -> x0, loops' own time: 105 us -> none  [the longest x2 52.2 us: key_block(): key_grad, value_grad = lax.map(key_one_head, head_ids)]
    psum x1 -> x0, waiting for transfers between devices: 85.3 us -> none  [local(): lax.psum((outer_sum(hidden_rows, query_d.reshape(-1, model_width)), outer...]
    all_to_all x0 -> x3, blocking collectives: none -> 68.9 us  [the longest x1 37.3 us: local(): arrived = lax.all_to_all(parts, ALL, 0, 0, tiled=True)]
    psum x1 -> x0, blocking collectives: 66.4 us -> none  [local(): lax.psum((outer_sum(hidden_rows, query_d.reshape(-1, model_width)), outer...]
    pallas_call x0 -> x4, Pallas kernels: none -> 54.4 us  [the longest x1 36.9 us: local(): pl.pallas_call(attend_kernel, out_shape=(whole((16, BLK, 2 * DH), BF), wh...]
    gather x12 -> x0, local copies, waits for them, and re-layouts: 43.9 us -> none  [the longest x2 10 us: key_block(): queries_all = query_flat[slot_rows].reshape(-1, model_width)]
  transfers between devices with their start and end apart: 25 -> 19, of which waited for: 13 -> 8; matrix products, arithmetic and copies ran while one was open for 28% -> 1% of each run, Pallas kernels for 0% -> 1%
where the time goes in v1:
time: 230 us; the launch traced here: 229 us
  blocking collectives  68.9 us (30%)
  Pallas kernels  54.4 us (24%)
  waiting for transfers between devices  50.2 us (22%)
  starting transfers between devices  37.3 us (16%)
  local copies, waits for them, and re-layouts  13.2 us (6%)
  other arithmetic  2.99 us (1%)
    all_to_all x1, blocking collectives, local(): arrived = lax.all_to_all(parts, ALL, 0, 0, tiled=True)  37.3 us
    pallas_call x1, Pallas kernels, local(): pl.pallas_call(attend_kernel, out_shape=(whole((16, BLK, 2 * DH), BF), wh...  36.9 us
    all_to_all x1, waiting for transfers between devices, local(): shares = lax.all_to_all(share, ALL, 0, 0, tiled=True)  29.4 us
    ppermute x16, starting transfers between devices, exchange(): return lax.ppermute(block, PLANE, pairs)  21.9 us
    ppermute x16, waiting for transfers between devices, exchange(): return lax.ppermute(block, PLANE, pairs)  20.8 us
    all_to_all x1, blocking collectives, local(): lax.all_to_all(kv_send, ZLINE, 0, 0, tiled=True).reshape(4, 4, BLK, 2 * DH)  16.2 us
    all_to_all x1, blocking collectives, local(): lax.all_to_all(kv_grad.reshape(H, ROWS, 2 * DH), ZLINE, 0, 0, tiled=True)  15.4 us
    pallas_call x1, Pallas kernels, local(): pl.pallas_call(finish_kernel, out_shape=(whole((ROWS, D), BF), whole((ROW...  8.99 us
  transfers between devices with their start and end apart: 19, of which 8 were waited for; matrix products, arithmetic and copies ran while one was open for 1% of the time, Pallas kernels for 1%

profile of v1, /device:TPU:1, one launch (start us, length us, event | category | flops | bytes accessed | tf_op | source)
XLA Modules:
  0.0 229.1 jit_solution(3741492765019000850)
XLA Ops:
  0.7 0.8 fusion.1
  1.5 0.8 copy.30
  2.4 0.6 pad.4.keep
  3.0 5.6 %shard_map.161 = (bf16[8,256,128]{2,1,0:T(8,128)(2,1)}, bf16[8,272,128]{2,1,0:T(8,128)(2,1)}, f32[256,512]{1,0:T(8,128)}, f32[256,512]{1,0:T(8,128)}) custom-call(bf16[256,512]{1,0:T(8,128)(2,1)} %bitcast.67, f32[1,512]{1,0:T(1,128)} %bitcast.72, bf16[256,512]{1,0:T(8,128)(2,1)} %bitcast.69, bf16[16,128]{1,0:T(8,128)(2,1)} %pad.4.keep, bf16[512,512]{1,0:T(8,128)(2,1)} %wq.3, ...), custom_call_target="tpu_custom_call" | custom-call | tf_op jit(solution)/shard_map/pallas_call | solution.py:252
  8.7 16.2 %all_to_all.30 = bf16[8,256,128]{2,1,0:T(8,128)(2,1)S(1)} all-to-all(bf16[8,256,128]{2,1,0:T(8,128)(2,1)} %get-tuple-element.26), channel_id=1, replica_groups=mesh['gx'=4,'zl'=2,'cr'=2,'tx'=4,'zh'=2] {'zl','cr','zh'}, dimensions={0} | all-to-all | bytes 1048576 | tf_op jit(solution)/shard_map/all_to_all | solution.py:263
  24.8 3.5 %all-to-all-start = ((bf16[8,272,128]{2,1,0:T(8,128)(2,1)}), bf16[8,272,128]{2,1,0:T(8,128)(2,1)S(1)}, u32[]{:S(2)}, u32[]{:S(2)}) async-start(bf16[8,272,128]{2,1,0:T(8,128)(2,1)} %get-tuple-element.25), calls=%async_computation | async-start | bytes 1114112 | tf_op jit(solution)/shard_map/all_to_all | solution.py:273
  28.3 2.8 %collective-permute-start.1 = (bf16[4,4,128,128]{3,2,1,0:T(8,128)(2,1)S(1)}, bf16[4,4,128,128]{3,2,1,0:T(8,128)(2,1)S(1)}, u32[]{:S(2)}, u32[]{:S(2)}) collective-permute-start(bf16[4,4,128,128]{3,2,1,0:T(8,128)(2,1)S(1)} %bitcast.62), channel_id=1, source_target_pairs={{0,96},{2,98},{4,100},{6,102},{32,0},{34,2},{36,4},{38,6},{64,32},... | collective-permute-start | bytes 1572872 | tf_op jit(solution)/shard_map/ppermute | solution.py:225
  31.2 4.9 %collective-permute-start.7 = (bf16[4,128,128]{2,1,0:T(8,128)(2,1)S(1)}, bf16[4,128,128]{2,1,0:T(8,128)(2,1)S(1)}, u32[]{:S(2)}, u32[]{:S(2)}) collective-permute-start(bf16[4,128,128]{2,1,0:T(8,128)(2,1)S(1)} %get-tuple-element.46), channel_id=1, source_target_pairs={{0,102},{2,96},{4,98},{6,100},{32,6},{34,0},{36,2},{38,4},{64,38},... | collective-permute-start | bytes 393224 | tf_op jit(solution)/shard_map/ppermute | solution.py:225
  36.1 0.5 collective-permute-start.3
  36.7 0.6 dynamic_slice.3
  38.5 0.6 pad_maximum_fusion.coef
  39.1 3.6 %collective-permute-start.6 = (bf16[4,128,128]{2,1,0:T(8,128)(2,1)S(1)}, bf16[4,128,128]{2,1,0:T(8,128)(2,1)S(1)}, u32[]{:S(2)}, u32[]{:S(2)}) collective-permute-start(bf16[4,128,128]{2,1,0:T(8,128)(2,1)S(1)} %get-tuple-element.47), channel_id=1, source_target_pairs={{0,98},{2,100},{4,102},{6,96},{32,2},{34,4},{36,6},{38,0},{64,34},... | collective-permute-start | bytes 393224 | tf_op jit(solution)/shard_map/ppermute | solution.py:225
  43.1 0.9 collective-permute-done.3.tp
  44.0 1.0 collective-permute-start.2
  45.0 0.8 reshape.220.keep
  45.8 4.6 %collective-permute-done.4.cmm = bf16[4,128,128]{2,1,0:T(8,128)(2,1)S(1)} collective-permute-done((bf16[4,128,128]{2,1,0:T(8,128)(2,1)S(1)}, bf16[4,128,128]{2,1,0:T(8,128)(2,1)S(1)}, u32[]{:S(2)}, u32[]{:S(2)}) %collective-permute-start.4) | collective-permute-done | bytes 131104 | tf_op jit(solution)/shard_map/ppermute | solution.py:225
  50.4 1.2 collective-permute-done.2.tm
  51.6 0.6 copy-done.12
  52.4 0.8 copy-done.4
  53.2 36.9 %shard_map.162 = (bf16[16,128,128]{2,1,0:T(8,128)(2,1)}, f32[4,4,128,128]{3,2,1,0:T(8,128)}, bf16[4,4,128,128]{3,2,1,0:T(8,128)(2,1)}, bf16[4,4,128,128]{3,2,1,0...) custom-call(f32[2]{0:T(128)} %pad_maximum_fusion.coef, ...), custom_call_target="tpu_custom_call" | custom-call | tf_op jit(solution)/shard_map/pallas_call | solution.py:284
  90.2 0.9 collective-permute-start.8
  91.0 0.7 collective-permute-start.9
  91.7 7.6 %all-to-all-start.2 = ((bf16[8,256,128]{2,1,0:T(8,128)(2,1)}), bf16[8,256,128]{2,1,0:T(8,128)(2,1)S(1)}, u32[]{:S(2)}, u32[]{:S(2)}) async-start(bf16[8,256,128]{2,1,0:T(8,128)(2,1)} %bitcast.71), calls=%async_computation.2 | async-start | bytes 1048576 | tf_op jit(solution)/shard_map/all_to_all | solution.py:309
  99.3 3.3 %collective-permute-start.11 = (bf16[4,128,128]{2,1,0:T(8,128)(2,1)}, bf16[4,128,128]{2,1,0:T(8,128)(2,1)S(1)}, u32[]{:S(2)}, u32[]{:S(2)}) collective-permute-start(bf16[4,128,128]{2,1,0:T(8,128)(2,1)} %get-tuple-element.32), channel_id=1, source_target_pairs={{0,98},{2,100},{4,102},{6,96},{32,2},{34,4},{36,6},{38,0},{64,34},... | collective-permute-start | bytes 393224 | tf_op jit(solution)/shard_map/ppermute | solution.py:225
  102.6 3.2 %collective-permute-done.10.lo0 = bf16[4,128,128]{2,1,0:T(8,128)(2,1)S(1)} collective-permute-done((bf16[4,128,128]{2,1,0:T(8,128)(2,1)}, bf16[4,128,128]{2,1,0:T(8,128)(2,1)S(1)}, u32[]{:S(2)}, u32[]{:S(2)}) %collective-permute-start.10) | collective-permute-done | bytes 131104 | tf_op jit(solution)/shard_map/ppermute | solution.py:225
  106.1 2.0 collective-permute-done.11.lo1
  108.1 3.5 %collective-permute-start.14 = (bf16[4,128,128]{2,1,0:T(8,128)(2,1)}, bf16[4,128,128]{2,1,0:T(8,128)(2,1)S(1)}, u32[]{:S(2)}, u32[]{:S(2)}) collective-permute-start(bf16[4,128,128]{2,1,0:T(8,128)(2,1)} %get-tuple-element.35), channel_id=1, source_target_pairs={{0,102},{2,96},{4,98},{6,100},{32,6},{34,0},{36,2},{38,4},{64,38},... | collective-permute-start | bytes 393224 | tf_op jit(solution)/shard_map/ppermute | solution.py:225
  111.7 2.4 %collective-permute-done.12.lo2 = bf16[4,128,128]{2,1,0:T(8,128)(2,1)S(1)} collective-permute-done((bf16[4,128,128]{2,1,0:T(8,128)(2,1)}, bf16[4,128,128]{2,1,0:T(8,128)(2,1)S(1)}, u32[]{:S(2)}, u32[]{:S(2)}) %collective-permute-start.12) | collective-permute-done | bytes 131104 | tf_op jit(solution)/shard_map/ppermute | solution.py:225
  114.1 6.5 %collective-permute-done.15.hi2 = bf16[4,128,128]{2,1,0:T(8,128)(2,1)S(1)} collective-permute-done((bf16[4,128,128]{2,1,0:T(8,128)(2,1)}, bf16[4,128,128]{2,1,0:T(8,128)(2,1)S(1)}, u32[]{:S(2)}, u32[]{:S(2)}) %collective-permute-start.15) | collective-permute-done | bytes 131104 | tf_op jit(solution)/shard_map/ppermute | solution.py:225
  120.6 0.6 copy-done.18
  121.6 2.8 %shard_map.163 = bf16[4,4,128,128]{3,2,1,0:T(8,128)(2,1)} custom-call(f32[4,4,128,128]{3,2,1,0:T(8,128)} %get-tuple-element.28.own, bf16[4,4,128,128]{3,2,1,0:T(8,128)(2,1)} %copy-done.5, bf16[4,4,128,128]{3,2,1,0:T(8,128)(2,1)} %copy-done.6, bf16[4,128,128]{2,1,0:T(8,128)(2,1)} %copy-done.13, bf16[4,128,128]{2,1,0:T(8,128)(2,1)} %copy-done.14, ...), custom_call_target="tpu_custom_call" | custom-call | tf_op jit(solution)/shard_map/pallas_call | solution.py:310
  124.4 15.4 %all_to_all.31.kv = bf16[8,256,128]{2,1,0:T(8,128)(2,1)} all-to-all(bf16[8,256,128]{2,1,0:T(8,128)(2,1)} %bitcast.66), channel_id=1, replica_groups=mesh['gx'=4,'zl'=2,'cr'=2,'tx'=4,'zh'=2] {'zl','cr','zh'}, dimensions={0} | all-to-all | bytes 1048576 | tf_op jit(solution)/shard_map/all_to_all | solution.py:313
  139.8 9.0 %shard_map.164 = (bf16[256,512]{1,0:T(8,128)(2,1)}, f32[256,512]{1,0:T(8,128)}, bf16[128,72,128]{2,1,0:T(8,128)(2,1)}) custom-call(bf16[256,512]{1,0:T(8,128)(2,1)} %bitcast.68, f32[1,512]{1,0:T(1,128)} %bitcast.73, bf16[256,512]{1,0:T(8,128)(2,1)} %bitcast.70, bf16[8,256,128]{2,1,0:T(8,128)(2,1)} %copy-done.2, bf16[8,256,128]{2,1,0:T(8,128)(2,1)} %all_to_all.31.kv, ...), custom_call_target="tpu_custom_call" | custom-call | tf_op jit(solution)/shard_map/pallas_call | solution.py:315
  148.8 37.3 %all_to_all.32 = bf16[128,72,128]{2,1,0:T(8,128)(2,1)S(1)} all-to-all(bf16[128,72,128]{2,1,0:T(8,128)(2,1)} %get-tuple-element.41), channel_id=1, replica_groups=mesh['gx'=4,'zl'=2,'cr'=2,'tx'=4,'zh'=2] {'gx','zl','cr','tx','zh'}, dimensions={0} | all-to-all | bytes 4718592 | tf_op jit(solution)/shard_map/all_to_all | solution.py:321
  186.2 0.4 convert_reduce_fusion
  186.5 1.9 broadcast_in_dim.26
  188.4 4.3 %all-to-all-start.5 = ((bf16[128,64,128]{2,1,0:T(8,128)(2,1)}), bf16[128,64,128]{2,1,0:T(8,128)(2,1)S(1)}, u32[]{:S(2)}, u32[]{:S(2)}) async-start(bf16[128,64,128]{2,1,0:T(8,128)(2,1)} %broadcast_in_dim.26), calls=%async_computation.5 | async-start | bytes 4194304 | tf_op jit(solution)/shard_map/all_to_all | solution.py:326
  192.7 0.6 fusion.14
  193.5 0.5 div.30
  194.0 29.4 %all-to-all-done.5 = bf16[128,64,128]{2,1,0:T(8,128)(2,1)S(1)} async-done(((bf16[128,64,128]{2,1,0:T(8,128)(2,1)}), bf16[128,64,128]{2,1,0:T(8,128)(2,1)S(1)}, u32[]{:S(2)}, u32[]{:S(2)}) %all-to-all-start.5) | async-done | bytes 2097184 | tf_op jit(solution)/shard_map/all_to_all | solution.py:326
  223.4 0.5 convert_bitcast_fusion
  223.8 0.6 fusion.13
  224.4 0.4 copy.36
  224.9 0.4 copy.35
  225.3 0.4 copy.34
  225.7 0.4 copy.33
  226.2 1.5 copy_bitcast_fusion
  227.6 1.5 copy_bitcast_fusion.2
  (64 shorter events, 1.8 us)
Async XLA Ops:
  3.0 33.6 %copy-start.19 = (f32[8]{0:T(128)S(1)}, f32[8]{0:T(128)}, u32[]{:S(2)}) copy-start(f32[8]{0:T(128)} %param.16) | copy-start | bytes 100
  24.8 26.7 %copy-start = (bf16[8,256,128]{2,1,0:T(8,128)(2,1)}, bf16[8,256,128]{2,1,0:T(8,128)(2,1)S(1)}, u32[]{:S(2)}) copy-start(bf16[8,256,128]{2,1,0:T(8,128)(2,1)S(1)} %all_to_all.30) | copy-start | bytes 1572868
  24.8 20.1 %all-to-all-start = ((bf16[8,272,128]{2,1,0:T(8,128)(2,1)}), bf16[8,272,128]{2,1,0:T(8,128)(2,1)S(1)}, u32[]{:S(2)}, u32[]{:S(2)}) async-start(bf16[8,272,128]{2,1,0:T(8,128)(2,1)} %get-tuple-element.25), calls=%async_computation | async-start | bytes 1114112 | tf_op jit(solution)/shard_map/all_to_all | solution.py:273
  28.3 23.2 %collective-permute-start.1 = (bf16[4,4,128,128]{3,2,1,0:T(8,128)(2,1)S(1)}, bf16[4,4,128,128]{3,2,1,0:T(8,128)(2,1)S(1)}, u32[]{:S(2)}, u32[]{:S(2)}) collective-permute-start(bf16[4,4,128,128]{3,2,1,0:T(8,128)(2,1)S(1)} %bitcast.62), channel_id=1, source_target_pairs={{0,96},{2,98},{4,100},{6,102},{32,0},{34,2},{36,4},{38,6},{64,32},... | collective-permute-start | bytes 1572872 | tf_op jit(solution)/shard_map/ppermute | solution.py:225
  31.1 20.4 %collective-permute-start = (bf16[4,4,128,128]{3,2,1,0:T(8,128)(2,1)S(1)}, bf16[4,4,128,128]{3,2,1,0:T(8,128)(2,1)S(1)}, u32[]{:S(2)}, u32[]{:S(2)}) collective-permute-start(bf16[4,4,128,128]{3,2,1,0:T(8,128)(2,1)S(1)} %bitcast.63), channel_id=1, source_target_pairs={{0,32},{2,34},{4,36},{6,38},{32,64},{34,66},{36,68},{38,70},{64,96... | collective-permute-start | bytes 1572872 | tf_op jit(solution)/shard_map/ppermute | solution.py:225
  31.2 8.0 %collective-permute-start.7 = (bf16[4,128,128]{2,1,0:T(8,128)(2,1)S(1)}, bf16[4,128,128]{2,1,0:T(8,128)(2,1)S(1)}, u32[]{:S(2)}, u32[]{:S(2)}) collective-permute-start(bf16[4,128,128]{2,1,0:T(8,128)(2,1)S(1)} %get-tuple-element.46), channel_id=1, source_target_pairs={{0,102},{2,96},{4,98},{6,100},{32,6},{34,0},{36,2},{38,4},{64,38},... | collective-permute-start | bytes 393224 | tf_op jit(solution)/shard_map/ppermute | solution.py:225
  36.1 6.6 %collective-permute-start.5 = (bf16[4,128,128]{2,1,0:T(8,128)(2,1)S(1)}, bf16[4,128,128]{2,1,0:T(8,128)(2,1)S(1)}, u32[]{:S(2)}, u32[]{:S(2)}) collective-permute-start(bf16[4,128,128]{2,1,0:T(8,128)(2,1)S(1)} %get-tuple-element.46), channel_id=1, source_target_pairs={{0,38},{2,32},{4,34},{6,36},{32,70},{34,64},{36,66},{38,68},{64,10... | collective-permute-start | bytes 393224 | tf_op jit(solution)/shard_map/ppermute | solution.py:225
  36.1 7.8 %collective-permute-start.3 = (bf16[4,128,128]{2,1,0:T(8,128)(2,1)S(1)}, bf16[4,128,128]{2,1,0:T(8,128)(2,1)S(1)}, u32[]{:S(2)}, u32[]{:S(2)}) collective-permute-start(bf16[4,128,128]{2,1,0:T(8,128)(2,1)S(1)} %get-tuple-element.46), channel_id=1, source_target_pairs={{0,6},{2,0},{4,2},{6,4},{32,38},{34,32},{36,34},{38,36},{64,70},{6... | collective-permute-start | bytes 393224 | tf_op jit(solution)/shard_map/ppermute | solution.py:225
  39.1 12.5 %copy-start.7 = (bf16[4,128,128]{2,1,0:T(8,128)(2,1)}, bf16[4,128,128]{2,1,0:T(8,128)(2,1)S(1)}, u32[]{:S(2)}) copy-start(bf16[4,128,128]{2,1,0:T(8,128)(2,1)S(1)} %collective-permute-done.7.cpp) | copy-start | bytes 393220
  39.1 6.6 %collective-permute-start.6 = (bf16[4,128,128]{2,1,0:T(8,128)(2,1)S(1)}, bf16[4,128,128]{2,1,0:T(8,128)(2,1)S(1)}, u32[]{:S(2)}, u32[]{:S(2)}) collective-permute-start(bf16[4,128,128]{2,1,0:T(8,128)(2,1)S(1)} %get-tuple-element.47), channel_id=1, source_target_pairs={{0,98},{2,100},{4,102},{6,96},{32,2},{34,4},{36,6},{38,0},{64,34},... | collective-permute-start | bytes 393224 | tf_op jit(solution)/shard_map/ppermute | solution.py:225
  42.7 8.9 %copy-start.8 = (bf16[4,128,128]{2,1,0:T(8,128)(2,1)}, bf16[4,128,128]{2,1,0:T(8,128)(2,1)S(1)}, u32[]{:S(2)}) copy-start(bf16[4,128,128]{2,1,0:T(8,128)(2,1)S(1)} %collective-permute-done.5.cmp) | copy-start | bytes 393220
  42.7 7.7 %collective-permute-start.4 = (bf16[4,128,128]{2,1,0:T(8,128)(2,1)S(1)}, bf16[4,128,128]{2,1,0:T(8,128)(2,1)S(1)}, u32[]{:S(2)}, u32[]{:S(2)}) collective-permute-start(bf16[4,128,128]{2,1,0:T(8,128)(2,1)S(1)} %get-tuple-element.47), channel_id=1, source_target_pairs={{0,34},{2,36},{4,38},{6,32},{32,66},{34,68},{36,70},{38,64},{64,98... | collective-permute-start | bytes 393224 | tf_op jit(solution)/shard_map/ppermute | solution.py:225
  44.0 7.7 %copy-start.9 = (bf16[4,128,128]{2,1,0:T(8,128)(2,1)}, bf16[4,128,128]{2,1,0:T(8,128)(2,1)S(1)}, u32[]{:S(2)}) copy-start(bf16[4,128,128]{2,1,0:T(8,128)(2,1)S(1)} %collective-permute-done.3.tp) | copy-start | bytes 393220
  44.0 7.6 %collective-permute-start.2 = (bf16[4,128,128]{2,1,0:T(8,128)(2,1)S(1)}, bf16[4,128,128]{2,1,0:T(8,128)(2,1)S(1)}, u32[]{:S(2)}, u32[]{:S(2)}) collective-permute-start(bf16[4,128,128]{2,1,0:T(8,128)(2,1)S(1)} %get-tuple-element.47), channel_id=1, source_target_pairs={{0,2},{2,4},{4,6},{6,0},{32,34},{34,36},{36,38},{38,32},{64,66},{6... | collective-permute-start | bytes 393224 | tf_op jit(solution)/shard_map/ppermute | solution.py:225
  45.0 6.6 %copy-start.1 = (bf16[8,272,128]{2,1,0:T(8,128)(2,1)}, bf16[8,272,128]{2,1,0:T(8,128)(2,1)S(1)}, u32[]{:S(2)}) copy-start(bf16[8,272,128]{2,1,0:T(8,128)(2,1)S(1)} %all-to-all-done.qb) | copy-start | bytes 1671172
  45.7 5.9 %copy-start.10 = (bf16[4,128,128]{2,1,0:T(8,128)(2,1)}, bf16[4,128,128]{2,1,0:T(8,128)(2,1)S(1)}, u32[]{:S(2)}) copy-start(bf16[4,128,128]{2,1,0:T(8,128)(2,1)S(1)} %collective-permute-done.6.cpm) | copy-start | bytes 393220
  50.4 1.3 copy-start.11
  51.6 0.7 copy-start.12
  51.6 0.8 copy-start.3
  52.4 0.8 copy-start.4
  90.2 30.4 %collective-permute-start.8 = (bf16[4,4,128,128]{3,2,1,0:T(8,128)(2,1)}, bf16[4,4,128,128]{3,2,1,0:T(8,128)(2,1)S(1)}, u32[]{:S(2)}, u32[]{:S(2)}) collective-permute-start(bf16[4,4,128,128]{3,2,1,0:T(8,128)(2,1)} %get-tuple-element.29), channel_id=1, source_target_pairs={{0,96},{2,98},{4,100},{6,102},{32,0},{34,2},{36,4},{38,6},{64,32},... | collective-permute-start | bytes 1572872 | tf_op jit(solution)/shard_map/ppermute | solution.py:225
  91.0 29.6 %collective-permute-start.9 = (bf16[4,4,128,128]{3,2,1,0:T(8,128)(2,1)}, bf16[4,4,128,128]{3,2,1,0:T(8,128)(2,1)S(1)}, u32[]{:S(2)}, u32[]{:S(2)}) collective-permute-start(bf16[4,4,128,128]{3,2,1,0:T(8,128)(2,1)} %get-tuple-element.30), channel_id=1, source_target_pairs={{0,32},{2,34},{4,36},{6,38},{32,64},{34,66},{36,68},{38,70},{64,96... | collective-permute-start | bytes 1572872 | tf_op jit(solution)/shard_map/ppermute | solution.py:225
  91.7 32.7 %all-to-all-start.2 = ((bf16[8,256,128]{2,1,0:T(8,128)(2,1)}), bf16[8,256,128]{2,1,0:T(8,128)(2,1)S(1)}, u32[]{:S(2)}, u32[]{:S(2)}) async-start(bf16[8,256,128]{2,1,0:T(8,128)(2,1)} %bitcast.71), calls=%async_computation.2 | async-start | bytes 1048576 | tf_op jit(solution)/shard_map/all_to_all | solution.py:309
  99.3 6.5 %collective-permute-start.10 = (bf16[4,128,128]{2,1,0:T(8,128)(2,1)}, bf16[4,128,128]{2,1,0:T(8,128)(2,1)S(1)}, u32[]{:S(2)}, u32[]{:S(2)}) collective-permute-start(bf16[4,128,128]{2,1,0:T(8,128)(2,1)} %get-tuple-element.31), channel_id=1, source_target_pairs={{0,2},{2,4},{4,6},{6,0},{32,34},{34,36},{36,38},{38,32},{64,66},{6... | collective-permute-start | bytes 393224 | tf_op jit(solution)/shard_map/ppermute | solution.py:225
  99.3 8.9 %collective-permute-start.11 = (bf16[4,128,128]{2,1,0:T(8,128)(2,1)}, bf16[4,128,128]{2,1,0:T(8,128)(2,1)S(1)}, u32[]{:S(2)}, u32[]{:S(2)}) collective-permute-start(bf16[4,128,128]{2,1,0:T(8,128)(2,1)} %get-tuple-element.32), channel_id=1, source_target_pairs={{0,98},{2,100},{4,102},{6,96},{32,2},{34,4},{36,6},{38,0},{64,34},... | collective-permute-start | bytes 393224 | tf_op jit(solution)/shard_map/ppermute | solution.py:225
  102.6 11.4 %collective-permute-start.12 = (bf16[4,128,128]{2,1,0:T(8,128)(2,1)}, bf16[4,128,128]{2,1,0:T(8,128)(2,1)S(1)}, u32[]{:S(2)}, u32[]{:S(2)}) collective-permute-start(bf16[4,128,128]{2,1,0:T(8,128)(2,1)} %get-tuple-element.33), channel_id=1, source_target_pairs={{0,34},{2,36},{4,38},{6,32},{32,66},{34,68},{36,70},{38,64},{64,98... | collective-permute-start | bytes 393224 | tf_op jit(solution)/shard_map/ppermute | solution.py:225
  105.8 14.8 %copy-start.13 = (bf16[4,128,128]{2,1,0:T(8,128)(2,1)}, bf16[4,128,128]{2,1,0:T(8,128)(2,1)S(1)}, u32[]{:S(2)}) copy-start(bf16[4,128,128]{2,1,0:T(8,128)(2,1)S(1)} %collective-permute-done.10.lo0) | copy-start | bytes 393220
  105.8 8.2 %collective-permute-start.13 = (bf16[4,128,128]{2,1,0:T(8,128)(2,1)}, bf16[4,128,128]{2,1,0:T(8,128)(2,1)S(1)}, u32[]{:S(2)}, u32[]{:S(2)}) collective-permute-start(bf16[4,128,128]{2,1,0:T(8,128)(2,1)} %get-tuple-element.34), channel_id=1, source_target_pairs={{0,6},{2,0},{4,2},{6,4},{32,38},{34,32},{36,34},{38,36},{64,70},{6... | collective-permute-start | bytes 393224 | tf_op jit(solution)/shard_map/ppermute | solution.py:225
  108.1 12.5 %copy-start.14 = (bf16[4,128,128]{2,1,0:T(8,128)(2,1)}, bf16[4,128,128]{2,1,0:T(8,128)(2,1)S(1)}, u32[]{:S(2)}) copy-start(bf16[4,128,128]{2,1,0:T(8,128)(2,1)S(1)} %collective-permute-done.11.lo1) | copy-start | bytes 393220
  108.1 5.9 %collective-permute-start.14 = (bf16[4,128,128]{2,1,0:T(8,128)(2,1)}, bf16[4,128,128]{2,1,0:T(8,128)(2,1)S(1)}, u32[]{:S(2)}, u32[]{:S(2)}) collective-permute-start(bf16[4,128,128]{2,1,0:T(8,128)(2,1)} %get-tuple-element.35), channel_id=1, source_target_pairs={{0,102},{2,96},{4,98},{6,100},{32,6},{34,0},{36,2},{38,4},{64,38},... | collective-permute-start | bytes 393224 | tf_op jit(solution)/shard_map/ppermute | solution.py:225
  114.0 6.6 %copy-start.15 = (bf16[4,128,128]{2,1,0:T(8,128)(2,1)}, bf16[4,128,128]{2,1,0:T(8,128)(2,1)S(1)}, u32[]{:S(2)}) copy-start(bf16[4,128,128]{2,1,0:T(8,128)(2,1)S(1)} %collective-permute-done.12.lo2) | copy-start | bytes 393220
  114.0 6.6 %collective-permute-start.15 = (bf16[4,128,128]{2,1,0:T(8,128)(2,1)}, bf16[4,128,128]{2,1,0:T(8,128)(2,1)S(1)}, u32[]{:S(2)}, u32[]{:S(2)}) collective-permute-start(bf16[4,128,128]{2,1,0:T(8,128)(2,1)} %get-tuple-element.36), channel_id=1, source_target_pairs={{0,38},{2,32},{4,34},{6,36},{32,70},{34,64},{36,66},{38,68},{64,10... | collective-permute-start | bytes 393224 | tf_op jit(solution)/shard_map/ppermute | solution.py:225
  114.0 6.6 %copy-start.16 = (bf16[4,128,128]{2,1,0:T(8,128)(2,1)}, bf16[4,128,128]{2,1,0:T(8,128)(2,1)S(1)}, u32[]{:S(2)}) copy-start(bf16[4,128,128]{2,1,0:T(8,128)(2,1)S(1)} %collective-permute-done.13.hi0) | copy-start | bytes 393220
  114.0 6.6 %copy-start.17 = (bf16[4,128,128]{2,1,0:T(8,128)(2,1)}, bf16[4,128,128]{2,1,0:T(8,128)(2,1)S(1)}, u32[]{:S(2)}) copy-start(bf16[4,128,128]{2,1,0:T(8,128)(2,1)S(1)} %collective-permute-done.14.hi1) | copy-start | bytes 393220
  120.6 0.7 copy-start.18
  120.6 0.8 copy-start.5
  120.6 1.0 copy-start.6
  124.4 15.4 %copy-start.2 = (bf16[8,256,128]{2,1,0:T(8,128)(2,1)}, bf16[8,256,128]{2,1,0:T(8,128)(2,1)S(1)}, u32[]{:S(2)}) copy-start(bf16[8,256,128]{2,1,0:T(8,128)(2,1)S(1)} %all-to-all-done.2.mq) | copy-start | bytes 1572868
  188.4 34.9 %all-to-all-start.5 = ((bf16[128,64,128]{2,1,0:T(8,128)(2,1)}), bf16[128,64,128]{2,1,0:T(8,128)(2,1)S(1)}, u32[]{:S(2)}, u32[]{:S(2)}) async-start(bf16[128,64,128]{2,1,0:T(8,128)(2,1)} %broadcast_in_dim.26), calls=%async_computation.5 | async-start | bytes 4194304 | tf_op jit(solution)/shard_map/all_to_all | solution.py:326

commit v2 on v1

v2 whole, which is shorter than its diff:
```python
import math

import jax
import jax.numpy as jnp
from jax import lax
from jax.experimental import pallas as pl
from jax.experimental.pallas import tpu as pltpu
from jax.sharding import Mesh, PartitionSpec as P

NORM_EPS = 1e-05
HEAD_EPS = 1e-06
D = 512
H = 8
DH = 64
BLK = 128
NB = 27
ROWS = 256
SCALE = DH**-0.5
BF = jnp.bfloat16
F32 = jnp.float32
ZLINE = ("zl", "cr", "zh")
PLANE = ("gx", "tx")
CORES = ("gx", "zl", "tx", "zh")
ALL = ("gx", "zl", "cr", "tx", "zh")
VMEM_LIMIT = 56 * 1024 * 1024


def params():
    return pltpu.CompilerParams(vmem_limit_bytes=VMEM_LIMIT)


def dot_nn(left, right):
    return jnp.dot(left, right, preferred_element_type=F32)


def dot_nt(left, right):
    return lax.dot_general(left, right, (((1,), (1,)), ((), ())), preferred_element_type=F32)


def dot_tn(left, right):
    return lax.dot_general(left, right, (((0,), (0,)), ((), ())), preferred_element_type=F32)


def head(values, index):
    return values[:, index * DH : (index + 1) * DH]


def normed_hidden(tokens, gain):
    values = tokens.astype(F32)
    factor = lax.rsqrt(jnp.mean(values * values, axis=-1, keepdims=True) + NORM_EPS)
    unit = values * factor
    return unit, factor, (unit * gain).astype(BF)


def high_low(values):
    upper = values.astype(BF).astype(F32)
    return upper, values - upper


def project_kernel(
    place, tok, gain, cot, neighbours, valid, wq, wk, wv, wp, kv_out, qb_out
):
    _, _, hidden = normed_hidden(tok[...], gain[...])
    lane = lax.broadcasted_iota(jnp.int32, (ROWS, 128), 1)
    factors = jnp.zeros((ROWS, 128), F32)
    key_f = dot_nn(hidden, wk[...])
    value = dot_nn(hidden, wv[...]).astype(BF)
    for h in range(H):
        part = head(key_f, h)
        factor = lax.rsqrt(jnp.mean(part * part, axis=-1, keepdims=True) + HEAD_EPS)
        factors = jnp.where(lane == H + h, factor, factors)
        kv_out[h] = jnp.concatenate([(part * factor).astype(BF), head(value, h)], axis=1)
    query_f = dot_nn(hidden, wq[...])
    back = dot_nt(cot[...], wp[...]).astype(BF)
    for h in range(H):
        part = head(query_f, h)
        factor = lax.rsqrt(jnp.mean(part * part, axis=-1, keepdims=True) + HEAD_EPS)
        factors = jnp.where(lane == h, factor, factors)
        qb_out[h, :ROWS] = jnp.concatenate([(part * factor).astype(BF), head(back, h)], axis=1)
    ids = neighbours[...]
    keep = valid[...]
    own_t = place[2] + lax.broadcasted_iota(jnp.int32, (2, NB), 0)
    step_t = jnp.bitwise_and(ids - own_t + 1, 15)
    step_y = jnp.bitwise_and(jnp.right_shift(ids, 4) - place[1] + 1, 3)
    step_x = jnp.bitwise_and(jnp.right_shift(ids, 6) - place[0] + 1, 3)
    slots = step_x * 9 + step_y * 3 + step_t
    short = lax.broadcasted_iota(jnp.int32, (2, 128), 1)
    kept = jnp.zeros((2, 128), F32)
    for slot in range(NB):
        hit = short == slots[:, slot : slot + 1]
        kept = kept + jnp.where(hit, keep[:, slot : slot + 1].astype(F32), 0.0)
    turned = factors.T
    for h in range(H):
        rows = [kept]
        for which in (h, H + h):
            line = turned[which : which + 1]
            for piece in high_low(line):
                rows += [piece[:, :BLK], piece[:, BLK:]]
        rows.append(jnp.zeros((6, 128), F32))
        qb_out[h, ROWS:] = jnp.concatenate(rows, axis=0).astype(BF)


def factor_rows(extra, base, which):
    first = extra[base : base + 1] + extra[base + 2 : base + 3]
    second = extra[base + 1 : base + 2] + extra[base + 3 : base + 4]
    return jnp.where(which == 0, first, second)


def attend_kernel(
    coef, keep, own, xm, xp, tm, tp, cmm, cmp, cpm, cpp, qb,
    mq_out, mqt_out, own_out, xm_out, xp_out, tm_out, tp_out, cmm_out, cmp_out, cpm_out, cpp_out,
    kvall, kvt, acc, wbuf, sems,
):
    moves = [
        (cmm, 0, 0), (xm, 0, None), (cmp, 0, 5),
        (tm, 1, 0), (own, 1, None), (tp, 1, 5),
        (cpm, 2, 0), (xp, 2, None), (cpp, 2, 5),
    ]
    copies = []
    for number, (src, dx, slot) in enumerate(moves):
        dst = kvall.at[dx, :, pl.ds(1, 4)] if slot is None else kvall.at[dx, :, slot]
        copies.append(pltpu.make_async_copy(src, dst, sems.at[number]))
    for copy in copies:
        copy.start()
    acc[...] = jnp.zeros_like(acc)
    for copy in copies:
        copy.wait()
    for dx in range(3):
        for y in range(4):
            for t in range(6):
                kvt[dx, y, :, t * BLK : (t + 1) * BLK] = kvall[dx, y, t].T

    exp_coef = coef[0]
    grad_coef = coef[1]
    lane = lax.broadcasted_iota(jnp.int32, (BLK, 2 * DH), 1)
    low = (lane < DH).astype(F32).astype(BF)
    high = (lane >= DH).astype(F32).astype(BF)

    def fold(values):
        return jnp.sum(values.reshape(-1, 8, BLK), axis=0)

    def one_block(number, carry):
        y = number // 4
        t = number % 4
        rows = pl.multiple_of((t % 2) * BLK, BLK)
        both = qb[y * 2 + t // 2, pl.ds(rows, BLK), :]
        spread = jnp.concatenate([both * low, both * high], axis=0)
        total = jnp.zeros((8, BLK), F32)
        inner = jnp.zeros((8, BLK), F32)
        for g in range(9):
            dx, dy = g // 3, g % 3
            yy = (y + dy + 3) % 4
            keys = kvall[dx, yy, pl.ds(t, 3)].reshape(3 * BLK, 2 * DH)
            pair = dot_nt(keys, spread)
            for k in range(3):
                score = pair[k * BLK : (k + 1) * BLK, :BLK]
                slope = pair[k * BLK : (k + 1) * BLK, BLK:]
                weight = jnp.exp2(score * exp_coef) * keep[number * NB + g * 3 + k]
                total = total + fold(weight)
                inner = inner + fold(weight * slope)
                base = (g * 3 + k) * BLK
                wbuf[base : base + BLK, :BLK] = weight
                wbuf[base : base + BLK, BLK:] = slope
        total_row = jnp.sum(total, axis=0, keepdims=True)
        inverse = 1.0 / total_row
        inner_row = jnp.sum(inner, axis=0, keepdims=True) * inverse
        out = jnp.zeros((2 * DH, 2 * BLK), F32)
        for g in range(9):
            dx, dy = g // 3, g % 3
            yy = (y + dy + 3) % 4
            base = g * 3 * BLK
            prob = wbuf[base : base + 3 * BLK, :BLK] * inverse
            slope = wbuf[base : base + 3 * BLK, BLK:]
            scaled = (prob * (slope - inner_row)) * grad_coef
            mixed = jnp.concatenate([scaled.astype(BF), prob.astype(BF)], axis=1)
            update = dot_nn(mixed, spread)
            acc[dx, yy, pl.ds(t, 3)] += update.reshape(3, BLK, 2 * DH)
            lanes = pl.multiple_of(t * BLK, BLK)
            out = out + dot_nn(kvt[dx, yy, :, pl.ds(lanes, 3 * BLK)], mixed)
        extra = qb[y * 2 + t // 2, ROWS:, :].astype(F32)
        factor = factor_rows(extra, 2, t % 2)
        query_t = both.astype(F32).T[:DH]
        grad_t = out[:DH, :BLK]
        inside = jnp.sum(query_t * grad_t, axis=0, keepdims=True)
        query_d = (grad_t - query_t * (inside * (1.0 / DH))) * factor
        joined = jnp.concatenate([out[DH:, BLK:], query_d], axis=0)
        mq_out[y * 2 + t // 2, pl.ds(rows, BLK), :] = joined.T.astype(BF)
        mqt_out[number] = joined.astype(BF)
        return carry + inside

    inside = lax.fori_loop(0, 16, one_block, jnp.zeros((1, BLK), F32))
    upper, lower = high_low(jnp.broadcast_to(jnp.sum(inside, axis=1, keepdims=True), (1, BLK)))
    tail = jnp.concatenate([upper, lower, jnp.zeros((14, BLK), F32)], axis=0).astype(BF)
    for chunk in range(H):
        mq_out[chunk, ROWS:, :] = tail
    own_out[...] = acc[1, :, 1:5]
    for out_ref, dx in ((xm_out, 0), (xp_out, 2)):
        out_ref[...] = acc[dx, :, 1:5].astype(BF)
    for out_ref, dx, slot in (
        (tm_out, 1, 0), (tp_out, 1, 5), (cmm_out, 0, 0),
        (cmp_out, 0, 5), (cpm_out, 2, 0), (cpp_out, 2, 5),
    ):
        out_ref[...] = acc[dx, :, slot].astype(BF)


def head_kernel(
    own, rx0, rx2, lo0, lo1, lo2, hi0, hi1, hi2, kv, qb, mqt, mq, tok, cot, gain,
    kv_out, parts_out, turned,
):
    for b in range(16):
        y, t = b // 4, b % 4
        total = own[y, t] + rx0[y, t].astype(F32) + rx2[y, t].astype(F32)
        if t == 0:
            total = total + lo0[y].astype(F32) + lo1[y].astype(F32) + lo2[y].astype(F32)
        if t == 3:
            total = total + hi0[y].astype(F32) + hi1[y].astype(F32) + hi2[y].astype(F32)
        total_t = total.T
        key_t = kv[y, t].astype(F32).T[:DH]
        extra = qb[y * 2 + t // 2, ROWS:, :].astype(F32)
        factor = factor_rows(extra, 6, t % 2)
        grad_t = total_t[:DH]
        inside = jnp.sum(key_t * grad_t, axis=0, keepdims=True) * (1.0 / DH)
        joined = jnp.concatenate([(grad_t - key_t * inside) * factor, total_t[DH:]], axis=0)
        turned[:, b * BLK : (b + 1) * BLK] = joined.astype(BF)
        kv_out[b] = joined.T.astype(BF)
    query_part = jnp.zeros((DH, D), F32)
    proj_part = jnp.zeros((DH, D), F32)
    both_part = jnp.zeros((2 * DH, D), F32)
    for c in range(4):
        lines = slice(c * 512, (c + 1) * 512)
        _, _, hidden = normed_hidden(tok[lines], gain[...])
        mixed_t = jnp.concatenate([mqt[c * 4 + k] for k in range(4)], axis=1)
        proj_part = proj_part + dot_nn(mixed_t[:DH], cot[lines])
        query_part = query_part + dot_nn(mixed_t[DH:], hidden)
        both_part = both_part + dot_nn(turned[:, lines], hidden)
    upper = jnp.concatenate([mq[h, ROWS : ROWS + 1].astype(F32) for h in range(H)], axis=0)
    lower = jnp.concatenate([mq[h, ROWS + 1 : ROWS + 2].astype(F32) for h in range(H)], axis=0)
    extra = jnp.concatenate([upper, lower, upper, lower], axis=1).astype(BF)
    joined = jnp.concatenate([query_part, both_part, proj_part], axis=0).astype(BF)
    for g in range(16):
        parts_out[g, :16] = joined[g * 16 : (g + 1) * 16]
        parts_out[g, 16:] = extra


def sum_kernel(arrived, share_out, temper_out):
    total = jnp.zeros((24, D), F32)
    for g in range(16):
        total = total + arrived[g].astype(F32)
    temper_out[...] = total[16:, :128] + total[16:, 128:256]
    share = total[:16].astype(BF)
    for k in range(64):
        share_out[k] = share


def output_kernel(core, near, far, gain, wq, wk, wv, gq, gk, gv, gp, gg, turned):
    for which, source in ((core[0], near), (1 - core[0], far)):
        for m in range(4):
            for zl in range(2):
                for tx in range(4):
                    for zh in range(2):
                        piece = source[m * 16 + zl * 8 + tx * 2 + zh]
                        start = pl.multiple_of(zl * 256 + which * 128 + zh * 64 + tx * 16, 16)
                        turned[m, pl.ds(start, 16), :] = piece
    gp[...] = turned[3].astype(F32)
    total = jnp.zeros((D, 1), F32)
    for m, (out, weight) in enumerate(((gq, wq), (gk, wk), (gv, wv))):
        value = turned[m].T.astype(F32)
        out[...] = value
        total = total + jnp.sum(value * weight[...].astype(F32), axis=1, keepdims=True)
    line = jnp.broadcast_to(total, (D, 128)).T
    gg[...] = line[:1] / gain[...]


def finish_kernel(tok, gain, mq, kv, wq, wk, wv, wp, layer_out, grad_tok):
    unit, factor_in, _ = normed_hidden(tok[...], gain[...])
    mixed = jnp.concatenate([mq[h, :ROWS, :DH] for h in range(H)], axis=1)
    layer_out[...] = dot_nn(mixed, wp[...]).astype(BF)
    query_d = jnp.concatenate([mq[h, :ROWS, DH:] for h in range(H)], axis=1)
    key_d = jnp.concatenate([kv[h][:, :DH] for h in range(H)], axis=1)
    value_d = jnp.concatenate([kv[h][:, DH:] for h in range(H)], axis=1)
    back_hidden = dot_nt(query_d, wq[...]) + dot_nt(key_d, wk[...]) + dot_nt(value_d, wv[...])
    slope_in = back_hidden * gain[...]
    grad_tok[...] = factor_in * (
        slope_in - unit * jnp.mean(slope_in * unit, axis=-1, keepdims=True)
    )


def whole(shape, dtype):
    return jax.ShapeDtypeStruct(shape, dtype)


def exchange(block, dx, dt):
    pairs = [
        (a * 4 + b, ((a + dx) % 4) * 4 + (b + dt) % 4) for a in range(4) for b in range(4)
    ]
    return lax.ppermute(block, PLANE, pairs)


def local(
    tokens, norm_gain, w_query, w_key, w_value, w_proj, temper, neighbours, valid_mask, cotangent
):
    tok = tokens.reshape(ROWS, D)
    cot = cotangent.reshape(ROWS, D)
    gain = norm_gain.reshape(1, D)
    tok_all = lax.all_gather(tok, ZLINE, axis=0, tiled=True)
    cot_all = lax.all_gather(cot, ZLINE, axis=0, tiled=True)
    core = lax.axis_index("cr")
    place = jnp.stack(
        [
            lax.axis_index("gx"),
            lax.axis_index("zl") * 2 + core,
            (lax.axis_index("tx") * 2 + lax.axis_index("zh")) * 2,
        ]
    )
    any_spec = pl.BlockSpec(memory_space=pl.ANY)
    smem = pl.BlockSpec(memory_space=pltpu.SMEM)
    vmem = pl.BlockSpec(memory_space=pltpu.VMEM)

    kv_send, qb_send = pl.pallas_call(
        project_kernel,
        out_shape=(whole((H, ROWS, 2 * DH), BF), whole((H, ROWS + 16, 2 * DH), BF)),
        in_specs=[smem] + [vmem] * 9,
        out_specs=(vmem, vmem),
        compiler_params=params(),
    )(
        place, tok, gain, cot, neighbours.reshape(2, NB), valid_mask.reshape(2, NB),
        w_query, w_key, w_value, w_proj,
    )

    own = lax.all_to_all(kv_send, ZLINE, 0, 0, tiled=True).reshape(4, 4, BLK, 2 * DH)
    late, early = own[:, 3], own[:, 0]
    xm = exchange(own, 1, 0)
    xp = exchange(own, -1, 0)
    tm = exchange(late, 0, 1)
    tp = exchange(early, 0, -1)
    cmm = exchange(late, 1, 1)
    cmp = exchange(early, 1, -1)
    cpm = exchange(late, -1, 1)
    cpp = exchange(early, -1, -1)
    qb = lax.all_to_all(qb_send, ZLINE, 0, 0, tiled=True)
    keep = qb[:, ROWS : ROWS + 2, :NB].astype(F32).reshape(16 * NB)
    head_id = (lax.axis_index("zl") * 2 + core) * 2 + lax.axis_index("zh")
    temp = temper[head_id] * SCALE
    coef = jnp.stack([temp * math.log2(math.e), temp])

    full = (4, 4, BLK, 2 * DH)
    edge = (4, BLK, 2 * DH)
    outs = pl.pallas_call(
        attend_kernel,
        out_shape=(
            whole((H, ROWS + 16, 2 * DH), BF), whole((16, 2 * DH, BLK), BF), whole(full, F32), whole(full, BF), whole(full, BF),
        ) + tuple(whole(edge, BF) for _ in range(6)),
        in_specs=[smem, smem] + [any_spec] * 9 + [vmem],
        out_specs=tuple([vmem] * 11),
        scratch_shapes=[
            pltpu.VMEM((3, 4, 6, BLK, 2 * DH), BF),
            pltpu.VMEM((3, 4, 2 * DH, 6 * BLK), BF),
            pltpu.VMEM((3, 4, 6, BLK, 2 * DH), F32),
            pltpu.VMEM((NB * BLK, 2 * BLK), F32),
            pltpu.SemaphoreType.DMA((9,)),
        ],
        compiler_params=params(),
    )(coef, keep, own, xm, xp, tm, tp, cmm, cmp, cpm, cpp, qb)
    mq_send, mqt, own_grad, gxm, gxp, gtm, gtp, gmm, gmp, gpm, gpp = outs
    rx0 = exchange(gxm, -1, 0)
    rx2 = exchange(gxp, 1, 0)
    hi0 = exchange(gtm, 0, -1)
    lo0 = exchange(gtp, 0, 1)
    hi1 = exchange(gmm, -1, -1)
    lo1 = exchange(gmp, -1, 1)
    hi2 = exchange(gpm, 1, -1)
    lo2 = exchange(gpp, 1, 1)
    mq = lax.all_to_all(mq_send, ZLINE, 0, 0, tiled=True)
    kv_back, parts = pl.pallas_call(
        head_kernel,
        out_shape=(whole((16, BLK, 2 * DH), BF), whole((16, 24, D), BF)),
        scratch_shapes=[pltpu.VMEM((2 * DH, 16 * BLK), BF)],
        compiler_params=params(),
    )(own_grad, rx0, rx2, lo0, lo1, lo2, hi0, hi1, hi2, own, qb, mqt, mq, tok_all, cot_all, gain)
    arrived = lax.all_to_all(parts, PLANE, 0, 0, tiled=True)
    kv = lax.all_to_all(kv_back.reshape(H, ROWS, 2 * DH), ZLINE, 0, 0, tiled=True)
    layer_out, grad_tokens = pl.pallas_call(
        finish_kernel,
        out_shape=(whole((ROWS, D), BF), whole((ROWS, D), F32)),
        compiler_params=params(),
    )(tok, gain, mq, kv, w_query, w_key, w_value, w_proj)
    share, temper_sum = pl.pallas_call(
        sum_kernel,
        out_shape=(whole((64, 16, D), BF), whole((H, 128), F32)),
        compiler_params=params(),
    )(arrived)
    near = lax.all_to_all(share, CORES, 0, 0, tiled=True)
    far = lax.ppermute(near, "cr", [(0, 1), (1, 0)])
    square = whole((D, D), F32)
    gq, gk, gv, gp, grad_gain = pl.pallas_call(
        output_kernel,
        out_shape=(square, square, square, square, whole((1, D), F32)),
        in_specs=[smem] + [vmem] * 6,
        scratch_shapes=[pltpu.VMEM((4, D, D), BF)],
        compiler_params=params(),
    )(core.reshape(1), near, far, gain, w_query, w_key, w_value)
    grad_temper = temper_sum[:, 0] / temper
    return (
        layer_out.reshape(tokens.shape),
        grad_tokens.reshape(tokens.shape),
        grad_gain.reshape(D),
        gq,
        gk,
        gv,
        gp,
        grad_temper,
    )


def solution(mesh):
    fine = Mesh(mesh.devices.reshape(4, 2, 2, 4, 2), ALL)
    lattice = ("gx", ("zl", "cr"), ("tx", "zh"))
    blocks = P(*lattice, None, None)
    lists = P(*lattice, None)
    return jax.shard_map(
        local,
        mesh=fine,
        in_specs=(blocks, P(), P(), P(), P(), P(), P(), lists, lists, blocks),
        out_specs=(blocks, blocks, P(), P(), P(), P(), P(), P()),
        check_vma=False,
    )
```

time: 230 us -> 226 us (0.983)
  between operations: 2.22 us -> 15.6 us
  waiting for transfers between devices: 50.2 us -> 37 us
  local copies, waits for them, and re-layouts: 13.2 us -> 4.91 us
  Pallas kernels: 54.4 us -> 58.5 us
    all_to_all x2, waiting for transfers between devices: 29.4 us -> 8.7 us  [the longest x1 8.69 us: local(): lax.all_to_all(kv_back.reshape(H, ROWS, 2 * DH), ZLINE, 0, 0, tiled=True)]
    all_to_all x2, blocking collectives: 52.8 us -> 41 us  [the longest x1 26 us: local(): near = lax.all_to_all(share, CORES, 0, 0, tiled=True)]
    all_to_all x1, blocking collectives: 16.2 us -> 27.7 us  [local(): lax.all_to_all(kv_send, ZLINE, 0, 0, tiled=True).reshape(4, 4, BLK, 2 * DH)]
    pallas_call x2 -> x4, Pallas kernels: 39.7 us -> 49.3 us  [the longest x1 35.9 us: local(): pl.pallas_call(attend_kernel, out_shape=(whole((H, ROWS + 16, 2 * DH), BF...]
    all_to_all x1, waiting for transfers between devices: 0.01 us -> 8.19 us  [local(): qb = lax.all_to_all(qb_send, ZLINE, 0, 0, tiled=True)]
    ppermute x16, waiting for transfers between devices: 20.8 us -> 12.7 us  [exchange(): return lax.ppermute(block, PLANE, pairs)]
    all_gather x0 -> x2, waiting for transfers between devices: none -> 5.95 us  [the longest x1 5.93 us: local(): cot_all = lax.all_gather(cot, ZLINE, axis=0, tiled=True)]
    pallas_call x1, Pallas kernels: 8.99 us -> 3.57 us  [local(): pl.pallas_call(finish_kernel, out_shape=(whole((ROWS, D), BF), whole((ROW...]
  transfers between devices with their start and end apart: 19 -> 22, of which waited for: 8 -> 10; matrix products, arithmetic and copies ran while one was open for 1% -> 1% of each run, Pallas kernels for 1% -> 20%
where the time goes in v2:
time: 226 us
  blocking collectives  68.7 us (30%)
  Pallas kernels  58.5 us (26%)
  starting transfers between devices  39.2 us (17%)
  waiting for transfers between devices  37 us (16%)
  between operations  15.6 us (7%)
  local copies, waits for them, and re-layouts  4.91 us (2%)
    pallas_call x1, Pallas kernels, local(): pl.pallas_call(attend_kernel, out_shape=(whole((H, ROWS + 16, 2 * DH), BF...  35.9 us
    all_to_all x1, blocking collectives, local(): lax.all_to_all(kv_send, ZLINE, 0, 0, tiled=True).reshape(4, 4, BLK, 2 * DH)  27.7 us
    all_to_all x1, blocking collectives, local(): near = lax.all_to_all(share, CORES, 0, 0, tiled=True)  26 us
    ppermute x16, starting transfers between devices, exchange(): return lax.ppermute(block, PLANE, pairs)  23.6 us
    all_to_all x1, blocking collectives, local(): arrived = lax.all_to_all(parts, PLANE, 0, 0, tiled=True)  15.1 us
    ppermute x16, waiting for transfers between devices, exchange(): return lax.ppermute(block, PLANE, pairs)  12.7 us
    all_to_all x1, waiting for transfers between devices, local(): lax.all_to_all(kv_back.reshape(H, ROWS, 2 * DH), ZLINE, 0, 0, tiled=True)  8.69 us
    all_to_all x1, waiting for transfers between devices, local(): qb = lax.all_to_all(qb_send, ZLINE, 0, 0, tiled=True)  8.19 us
  transfers between devices with their start and end apart: 22, of which 10 were waited for; matrix products, arithmetic and copies ran while one was open for 1% of the time, Pallas kernels for 20%

profile of v2, /device:TPU:1, one launch (start us, length us, event | category | flops | bytes accessed | tf_op | source)
XLA Modules:
  0.0 225.5 jit_solution(17751193095458376384)
XLA Ops:
  7.2 0.7 all-gather.3.cloned.1.call-update
  7.9 0.7 all-gather.5.cloned.1.call-update
  8.7 0.6 pad_add_fusion.place
  9.3 5.6 %shard_map.161 = (bf16[8,256,128]{2,1,0:T(8,128)(2,1)}, bf16[8,272,128]{2,1,0:T(8,128)(2,1)}) custom-call(s32[3]{0:T(128)} %pad_add_fusion.place, bf16[256,512]{1,0:T(8,128)(2,1)} %bitcast.24, f32[1,512]{1,0:T(1,128)} %bitcast.28, bf16[256,512]{1,0:T(8,128)(2,1)} %bitcast.27, s32[2,27]{1,0:T(2,128)} %bitcast.32, s32[2,27]{1,0:T(2,128)} %bitcast.33, ...), custom_call_target="tpu_custom_call" | custom-call | tf_op jit(solution)/shard_map/pallas_call | solution.py:319
  14.9 27.7 %all_to_all.30 = bf16[8,256,128]{2,1,0:T(8,128)(2,1)S(1)} all-to-all(bf16[8,256,128]{2,1,0:T(8,128)(2,1)} %get-tuple-element.33), channel_id=1, replica_groups=mesh['gx'=4,'zl'=2,'cr'=2,'tx'=4,'zh'=2] {'zl','cr','zh'}, dimensions={0} | all-to-all | bytes 1048576 | tf_op jit(solution)/shard_map/all_to_all | solution.py:330
  42.6 3.7 %all-to-all-start = ((bf16[8,272,128]{2,1,0:T(8,128)(2,1)}), bf16[8,272,128]{2,1,0:T(8,128)(2,1)S(1)}, u32[]{:S(2)}, u32[]{:S(2)}) async-start(bf16[8,272,128]{2,1,0:T(8,128)(2,1)} %get-tuple-element.32), calls=%async_computation | async-start | bytes 1114112 | tf_op jit(solution)/shard_map/all_to_all | solution.py:340
  46.3 0.9 collective-permute-start
  47.2 1.8 collective-permute-start.1
  49.0 0.9 collective-permute-start.2
  49.9 1.8 collective-permute-start.3
  51.8 0.6 dynamic_slice.3
  53.6 0.6 pad_maximum_fusion.coef
  54.2 0.5 collective-permute-done.2.tm
  54.7 2.5 %collective-permute-start.5 = (bf16[4,128,128]{2,1,0:T(8,128)(2,1)S(1)}, bf16[4,128,128]{2,1,0:T(8,128)(2,1)S(1)}, u32[]{:S(2)}, u32[]{:S(2)}) collective-permute-start(bf16[4,128,128]{2,1,0:T(8,128)(2,1)S(1)} %get-tuple-element.56), channel_id=1, source_target_pairs={{0,38},{2,32},{4,34},{6,36},{32,70},{34,64},{36,66},{38,68},{64,10... | collective-permute-start | bytes 393224 | tf_op jit(solution)/shard_map/ppermute | solution.py:296
  57.2 1.1 collective-permute-start.6
  58.3 0.7 collective-permute-done.4.cmm
  59.0 3.6 %collective-permute-start.7 = (bf16[4,128,128]{2,1,0:T(8,128)(2,1)S(1)}, bf16[4,128,128]{2,1,0:T(8,128)(2,1)S(1)}, u32[]{:S(2)}, u32[]{:S(2)}) collective-permute-start(bf16[4,128,128]{2,1,0:T(8,128)(2,1)S(1)} %get-tuple-element.56), channel_id=1, source_target_pairs={{0,102},{2,96},{4,98},{6,100},{32,6},{34,0},{36,2},{38,4},{64,38},... | collective-permute-start | bytes 393224 | tf_op jit(solution)/shard_map/ppermute | solution.py:296
  62.6 8.2 %all-to-all-done.qb = bf16[8,272,128]{2,1,0:T(8,128)(2,1)S(1)} async-done(((bf16[8,272,128]{2,1,0:T(8,128)(2,1)}), bf16[8,272,128]{2,1,0:T(8,128)(2,1)S(1)}, u32[]{:S(2)}, u32[]{:S(2)}) %all-to-all-start) | async-done | bytes 557088 | tf_op jit(solution)/shard_map/all_to_all | solution.py:340
  70.8 0.8 reshape.74.keep
  71.7 0.5 copy-done.19
  72.3 0.2 copy-done.8
  72.5 0.8 copy-done.9
  73.3 35.9 %shard_map.162 = (bf16[8,272,128]{2,1,0:T(8,128)(2,1)}, bf16[16,128,128]{2,1,0:T(8,128)(2,1)}, f32[4,4,128,128]{3,2,1,0:T(8,128)}, bf16[4,4,128,128]{3,2,1,0:T(8...) custom-call(f32[2]{0:T(128)} %pad_maximum_fusion.coef, ...), custom_call_target="tpu_custom_call" | custom-call | tf_op jit(solution)/shard_map/pallas_call | solution.py:348
  109.2 0.7 collective-permute-start.8
  109.9 0.8 collective-permute-start.9
  110.7 4.2 %all-to-all-start.2 = ((bf16[8,272,128]{2,1,0:T(8,128)(2,1)}), bf16[8,272,128]{2,1,0:T(8,128)(2,1)S(1)}, u32[]{:S(2)}, u32[]{:S(2)}) async-start(bf16[8,272,128]{2,1,0:T(8,128)(2,1)} %get-tuple-element.34), calls=%async_computation.2 | async-start | bytes 1114112 | tf_op jit(solution)/shard_map/all_to_all | solution.py:373
  114.9 0.2 collective-permute-start.10
  115.1 4.6 %collective-permute-start.11 = (bf16[4,128,128]{2,1,0:T(8,128)(2,1)}, bf16[4,128,128]{2,1,0:T(8,128)(2,1)S(1)}, u32[]{:S(2)}, u32[]{:S(2)}) collective-permute-start(bf16[4,128,128]{2,1,0:T(8,128)(2,1)} %get-tuple-element.39), channel_id=1, source_target_pairs={{0,98},{2,100},{4,102},{6,96},{32,2},{34,4},{36,6},{38,0},{64,34},... | collective-permute-start | bytes 393224 | tf_op jit(solution)/shard_map/ppermute | solution.py:296
  119.7 1.7 collective-permute-done.10.lo0
  121.4 1.0 collective-permute-start.13
  122.3 1.3 collective-permute-done.11.lo1
  123.6 3.7 %collective-permute-start.14 = (bf16[4,128,128]{2,1,0:T(8,128)(2,1)}, bf16[4,128,128]{2,1,0:T(8,128)(2,1)S(1)}, u32[]{:S(2)}, u32[]{:S(2)}) collective-permute-start(bf16[4,128,128]{2,1,0:T(8,128)(2,1)} %get-tuple-element.42), channel_id=1, source_target_pairs={{0,102},{2,96},{4,98},{6,100},{32,6},{34,0},{36,2},{38,4},{64,38},... | collective-permute-start | bytes 393224 | tf_op jit(solution)/shard_map/ppermute | solution.py:296
  127.4 2.0 collective-permute-done.12.lo2
  129.3 0.3 collective-permute-done.14.hi1
  129.6 6.3 %collective-permute-done.15.hi2 = bf16[4,128,128]{2,1,0:T(8,128)(2,1)S(1)} collective-permute-done((bf16[4,128,128]{2,1,0:T(8,128)(2,1)}, bf16[4,128,128]{2,1,0:T(8,128)(2,1)S(1)}, u32[]{:S(2)}, u32[]{:S(2)}) %collective-permute-start.15) | collective-permute-done | bytes 131104 | tf_op jit(solution)/shard_map/ppermute | solution.py:296
  136.0 5.9 %all-gather.5.cloned.1.call-done.cot = bf16[2048,512]{1,0:T(8,128)(2,1)} async-done(((bf16[256,512]{1,0:T(8,128)(2,1)}), bf16[2048,512]{1,0:T(8,128)(2,1)}) %all-gather.5.cloned.1.call-update) | async-done | bytes 2097168 | tf_op jit(solution)/shard_map/all_gather | solution.py:306
  142.0 6.7 %shard_map.163 = (bf16[16,128,128]{2,1,0:T(8,128)(2,1)}, bf16[16,24,512]{2,1,0:T(8,128)(2,1)}) custom-call(f32[4,4,128,128]{3,2,1,0:T(8,128)} %get-tuple-element.35.own, bf16[4,4,128,128]{3,2,1,0:T(8,128)(2,1)} %copy-done.6, bf16[4,4,128,128]{3,2,1,0:T(8,128)(2,1)} %copy-done.7, bf16[4,128,128]{2,1,0:T(8,128)(2,1)} %copy-done.10, ...), custom_call_target="tpu_custom_call" | custom-call | tf_op jit(solution)/shard_map/pallas_call | solution.py:374
  148.7 15.1 %all_to_all.31.arrived = bf16[16,24,512]{2,1,0:T(8,128)(2,1)} all-to-all(bf16[16,24,512]{2,1,0:T(8,128)(2,1)} %get-tuple-element.48), channel_id=1, replica_groups=mesh['gx'=4,'zl'=2,'cr'=2,'tx'=4,'zh'=2] {'gx','tx'}, dimensions={0} | all-to-all | bytes 786432 | tf_op jit(solution)/shard_map/all_to_all | solution.py:380
  163.8 2.1 shard_map.165
  165.9 26.0 %all_to_all.32.near = bf16[64,16,512]{2,1,0:T(8,128)(2,1)S(1)} all-to-all(bf16[64,16,512]{2,1,0:T(8,128)(2,1)} %get-tuple-element.49), channel_id=1, replica_groups=mesh['gx'=4,'zl'=2,'cr'=2,'tx'=4,'zh'=2] {'gx','zl','tx','zh'}, dimensions={0} | all-to-all | bytes 2097152 | tf_op jit(solution)/shard_map/all_to_all | solution.py:392
  191.9 4.1 %collective-permute-start.16 = (bf16[64,16,512]{2,1,0:T(8,128)(2,1)S(1)}, bf16[64,16,512]{2,1,0:T(8,128)(2,1)S(1)}, u32[]{:S(2)}, u32[]{:S(2)}) collective-permute-start(bf16[64,16,512]{2,1,0:T(8,128)(2,1)S(1)} %all_to_all.32.near), channel_id=1, source_target_pairs={{0,8},{8,0},{1,9},{9,1},{2,10},{10,2},{3,11},{11,3},{4,12},{12,4},... | collective-permute-start | bytes 3145736 | tf_op jit(solution)/shard_map/ppermute | solution.py:393
  195.9 3.4 %all-to-all-start.3 = ((bf16[8,256,128]{2,1,0:T(8,128)(2,1)}), bf16[8,256,128]{2,1,0:T(8,128)(2,1)S(1)}, u32[]{:S(2)}, u32[]{:S(2)}) async-start(bf16[8,256,128]{2,1,0:T(8,128)(2,1)} %bitcast.11), calls=%async_computation.3 | async-start | bytes 1048576 | tf_op jit(solution)/shard_map/all_to_all | solution.py:381
  199.5 0.5 div.3
  200.0 8.7 %all-to-all-done.3.kv = bf16[8,256,128]{2,1,0:T(8,128)(2,1)S(1)} async-done(((bf16[8,256,128]{2,1,0:T(8,128)(2,1)}), bf16[8,256,128]{2,1,0:T(8,128)(2,1)S(1)}, u32[]{:S(2)}, u32[]{:S(2)}) %all-to-all-start.3) | async-done | bytes 524320 | tf_op jit(solution)/shard_map/all_to_all | solution.py:381
  208.7 0.8 copy-done.4
  209.5 3.6 %shard_map.164 = (bf16[256,512]{1,0:T(8,128)(2,1)}, f32[256,512]{1,0:T(8,128)}) custom-call(bf16[256,512]{1,0:T(8,128)(2,1)} %bitcast.25, f32[1,512]{1,0:T(1,128)} %bitcast.30, bf16[8,272,128]{2,1,0:T(8,128)(2,1)} %copy-done.2, bf16[8,256,128]{2,1,0:T(8,128)(2,1)} %copy-done.4, bf16[512,512]{1,0:T(8,128)(2,1)} %wq.5, bf16[512,512]{1,0:T(8,128)(2,1)} %wk.5, ...), custom_call_target="tpu_custom_call" | custom-call | tf_op jit(solution)/shard_map/pallas_call | solution.py:382
  213.1 1.0 copy-done.5
  214.1 4.6 %shard_map.166 = (f32[512,512]{1,0:T(8,128)}, f32[512,512]{1,0:T(8,128)}, f32[512,512]{1,0:T(8,128)}, f32[512,512]{1,0:T(8,128)}, f32[1,512]{1,0:T(1,128)}) custom-call(s32[1]{0:T(128)} %bitcast.14.core, bf16[64,16,512]{2,1,0:T(8,128)(2,1)} %copy-done.3, bf16[64,16,512]{2,1,0:T(8,128)(2,1)} %copy-done.5, f32[1,512]{1,0:T(1,128)} %bitcast.31, ...), custom_call_target="tpu_custom_call" | custom-call | tf_op jit(solution)/shard_map/pallas_call | solution.py:395
  (63 shorter events, 0.5 us)
Async XLA Ops:
  7.2 128.8 %all-gather.3.cloned.1.call-start = ((), (), s32[]{:S(2)}) async-start(), calls=%async_computation.6 | async-start | bytes 2359296 | tf_op jit(solution)/shard_map/all_gather | solution.py:305
  7.9 134.1 %all-gather.5.cloned.1.call-start = ((), (), s32[]{:S(2)}) async-start(), calls=%async_computation.7 | async-start | bytes 2359296 | tf_op jit(solution)/shard_map/all_gather | solution.py:306
  9.3 42.5 %copy-start.23 = (f32[8]{0:T(128)S(1)}, f32[8]{0:T(128)}, u32[]{:S(2)}) copy-start(f32[8]{0:T(128)} %param.16) | copy-start | bytes 100
  42.6 29.1 %copy-start = (bf16[8,256,128]{2,1,0:T(8,128)(2,1)}, bf16[8,256,128]{2,1,0:T(8,128)(2,1)S(1)}, u32[]{:S(2)}) copy-start(bf16[8,256,128]{2,1,0:T(8,128)(2,1)S(1)} %all_to_all.30) | copy-start | bytes 1572868
  42.6 28.2 %all-to-all-start = ((bf16[8,272,128]{2,1,0:T(8,128)(2,1)}), bf16[8,272,128]{2,1,0:T(8,128)(2,1)S(1)}, u32[]{:S(2)}, u32[]{:S(2)}) async-start(bf16[8,272,128]{2,1,0:T(8,128)(2,1)} %get-tuple-element.32), calls=%async_computation | async-start | bytes 1114112 | tf_op jit(solution)/shard_map/all_to_all | solution.py:340
  46.3 25.3 %collective-permute-start = (bf16[4,4,128,128]{3,2,1,0:T(8,128)(2,1)S(1)}, bf16[4,4,128,128]{3,2,1,0:T(8,128)(2,1)S(1)}, u32[]{:S(2)}, u32[]{:S(2)}) collective-permute-start(bf16[4,4,128,128]{3,2,1,0:T(8,128)(2,1)S(1)} %bitcast.18), channel_id=1, source_target_pairs={{0,32},{2,34},{4,36},{6,38},{32,64},{34,66},{36,68},{38,70},{64,96... | collective-permute-start | bytes 1572872 | tf_op jit(solution)/shard_map/ppermute | solution.py:296
  47.2 24.4 %collective-permute-start.1 = (bf16[4,4,128,128]{3,2,1,0:T(8,128)(2,1)S(1)}, bf16[4,4,128,128]{3,2,1,0:T(8,128)(2,1)S(1)}, u32[]{:S(2)}, u32[]{:S(2)}) collective-permute-start(bf16[4,4,128,128]{3,2,1,0:T(8,128)(2,1)S(1)} %bitcast.19), channel_id=1, source_target_pairs={{0,96},{2,98},{4,100},{6,102},{32,0},{34,2},{36,4},{38,6},{64,32},... | collective-permute-start | bytes 1572872 | tf_op jit(solution)/shard_map/ppermute | solution.py:296
  49.0 5.7 %collective-permute-start.2 = (bf16[4,128,128]{2,1,0:T(8,128)(2,1)S(1)}, bf16[4,128,128]{2,1,0:T(8,128)(2,1)S(1)}, u32[]{:S(2)}, u32[]{:S(2)}) collective-permute-start(bf16[4,128,128]{2,1,0:T(8,128)(2,1)S(1)} %get-tuple-element.57), channel_id=1, source_target_pairs={{0,2},{2,4},{4,6},{6,0},{32,34},{34,36},{36,38},{38,32},{64,66},{6... | collective-permute-start | bytes 393224 | tf_op jit(solution)/shard_map/ppermute | solution.py:296
  49.9 7.3 %collective-permute-start.3 = (bf16[4,128,128]{2,1,0:T(8,128)(2,1)S(1)}, bf16[4,128,128]{2,1,0:T(8,128)(2,1)S(1)}, u32[]{:S(2)}, u32[]{:S(2)}) collective-permute-start(bf16[4,128,128]{2,1,0:T(8,128)(2,1)S(1)} %get-tuple-element.56), channel_id=1, source_target_pairs={{0,6},{2,0},{4,2},{6,4},{32,38},{34,32},{36,34},{38,36},{64,70},{6... | collective-permute-start | bytes 393224 | tf_op jit(solution)/shard_map/ppermute | solution.py:296
  51.8 7.2 %collective-permute-start.4 = (bf16[4,128,128]{2,1,0:T(8,128)(2,1)S(1)}, bf16[4,128,128]{2,1,0:T(8,128)(2,1)S(1)}, u32[]{:S(2)}, u32[]{:S(2)}) collective-permute-start(bf16[4,128,128]{2,1,0:T(8,128)(2,1)S(1)} %get-tuple-element.57), channel_id=1, source_target_pairs={{0,34},{2,36},{4,38},{6,32},{32,66},{34,68},{36,70},{38,64},{64,98... | collective-permute-start | bytes 393224 | tf_op jit(solution)/shard_map/ppermute | solution.py:296
  54.7 16.9 %copy-start.16 = (bf16[4,128,128]{2,1,0:T(8,128)(2,1)}, bf16[4,128,128]{2,1,0:T(8,128)(2,1)S(1)}, u32[]{:S(2)}) copy-start(bf16[4,128,128]{2,1,0:T(8,128)(2,1)S(1)} %collective-permute-done.2.tm) | copy-start | bytes 393220
  54.7 16.9 %collective-permute-start.5 = (bf16[4,128,128]{2,1,0:T(8,128)(2,1)S(1)}, bf16[4,128,128]{2,1,0:T(8,128)(2,1)S(1)}, u32[]{:S(2)}, u32[]{:S(2)}) collective-permute-start(bf16[4,128,128]{2,1,0:T(8,128)(2,1)S(1)} %get-tuple-element.56), channel_id=1, source_target_pairs={{0,38},{2,32},{4,34},{6,36},{32,70},{34,64},{36,66},{38,68},{64,10... | collective-permute-start | bytes 393224 | tf_op jit(solution)/shard_map/ppermute | solution.py:296
  57.2 14.4 %copy-start.17 = (bf16[4,128,128]{2,1,0:T(8,128)(2,1)}, bf16[4,128,128]{2,1,0:T(8,128)(2,1)S(1)}, u32[]{:S(2)}) copy-start(bf16[4,128,128]{2,1,0:T(8,128)(2,1)S(1)} %collective-permute-done.3.tp) | copy-start | bytes 393220
  57.2 14.3 %collective-permute-start.6 = (bf16[4,128,128]{2,1,0:T(8,128)(2,1)S(1)}, bf16[4,128,128]{2,1,0:T(8,128)(2,1)S(1)}, u32[]{:S(2)}, u32[]{:S(2)}) collective-permute-start(bf16[4,128,128]{2,1,0:T(8,128)(2,1)S(1)} %get-tuple-element.57), channel_id=1, source_target_pairs={{0,98},{2,100},{4,102},{6,96},{32,2},{34,4},{36,6},{38,0},{64,34},... | collective-permute-start | bytes 393224 | tf_op jit(solution)/shard_map/ppermute | solution.py:296
  59.0 12.7 %copy-start.18 = (bf16[4,128,128]{2,1,0:T(8,128)(2,1)}, bf16[4,128,128]{2,1,0:T(8,128)(2,1)S(1)}, u32[]{:S(2)}) copy-start(bf16[4,128,128]{2,1,0:T(8,128)(2,1)S(1)} %collective-permute-done.4.cmm) | copy-start | bytes 393220
  59.0 12.6 %collective-permute-start.7 = (bf16[4,128,128]{2,1,0:T(8,128)(2,1)S(1)}, bf16[4,128,128]{2,1,0:T(8,128)(2,1)S(1)}, u32[]{:S(2)}, u32[]{:S(2)}) collective-permute-start(bf16[4,128,128]{2,1,0:T(8,128)(2,1)S(1)} %get-tuple-element.56), channel_id=1, source_target_pairs={{0,102},{2,96},{4,98},{6,100},{32,6},{34,0},{36,2},{38,4},{64,38},... | collective-permute-start | bytes 393224 | tf_op jit(solution)/shard_map/ppermute | solution.py:296
  70.8 0.9 copy-start.1
  71.6 0.7 copy-start.19
  71.6 0.7 copy-start.20
  71.6 0.7 copy-start.21
  71.6 0.9 copy-start.8
  72.5 0.8 copy-start.9
  109.2 26.8 %collective-permute-start.8 = (bf16[4,4,128,128]{3,2,1,0:T(8,128)(2,1)}, bf16[4,4,128,128]{3,2,1,0:T(8,128)(2,1)S(1)}, u32[]{:S(2)}, u32[]{:S(2)}) collective-permute-start(bf16[4,4,128,128]{3,2,1,0:T(8,128)(2,1)} %get-tuple-element.36), channel_id=1, source_target_pairs={{0,96},{2,98},{4,100},{6,102},{32,0},{34,2},{36,4},{38,6},{64,32},... | collective-permute-start | bytes 1572872 | tf_op jit(solution)/shard_map/ppermute | solution.py:296
  109.9 26.1 %collective-permute-start.9 = (bf16[4,4,128,128]{3,2,1,0:T(8,128)(2,1)}, bf16[4,4,128,128]{3,2,1,0:T(8,128)(2,1)S(1)}, u32[]{:S(2)}, u32[]{:S(2)}) collective-permute-start(bf16[4,4,128,128]{3,2,1,0:T(8,128)(2,1)} %get-tuple-element.37), channel_id=1, source_target_pairs={{0,32},{2,34},{4,36},{6,38},{32,64},{34,66},{36,68},{38,70},{64,96... | collective-permute-start | bytes 1572872 | tf_op jit(solution)/shard_map/ppermute | solution.py:296
  110.7 25.3 %all-to-all-start.2 = ((bf16[8,272,128]{2,1,0:T(8,128)(2,1)}), bf16[8,272,128]{2,1,0:T(8,128)(2,1)S(1)}, u32[]{:S(2)}, u32[]{:S(2)}) async-start(bf16[8,272,128]{2,1,0:T(8,128)(2,1)} %get-tuple-element.34), calls=%async_computation.2 | async-start | bytes 1114112 | tf_op jit(solution)/shard_map/all_to_all | solution.py:373
  114.9 6.5 %collective-permute-start.10 = (bf16[4,128,128]{2,1,0:T(8,128)(2,1)}, bf16[4,128,128]{2,1,0:T(8,128)(2,1)S(1)}, u32[]{:S(2)}, u32[]{:S(2)}) collective-permute-start(bf16[4,128,128]{2,1,0:T(8,128)(2,1)} %get-tuple-element.38), channel_id=1, source_target_pairs={{0,2},{2,4},{4,6},{6,0},{32,34},{34,36},{36,38},{38,32},{64,66},{6... | collective-permute-start | bytes 393224 | tf_op jit(solution)/shard_map/ppermute | solution.py:296
  115.1 8.5 %collective-permute-start.11 = (bf16[4,128,128]{2,1,0:T(8,128)(2,1)}, bf16[4,128,128]{2,1,0:T(8,128)(2,1)S(1)}, u32[]{:S(2)}, u32[]{:S(2)}) collective-permute-start(bf16[4,128,128]{2,1,0:T(8,128)(2,1)} %get-tuple-element.39), channel_id=1, source_target_pairs={{0,98},{2,100},{4,102},{6,96},{32,2},{34,4},{36,6},{38,0},{64,34},... | collective-permute-start | bytes 393224 | tf_op jit(solution)/shard_map/ppermute | solution.py:296
  119.7 9.6 %collective-permute-start.12 = (bf16[4,128,128]{2,1,0:T(8,128)(2,1)}, bf16[4,128,128]{2,1,0:T(8,128)(2,1)S(1)}, u32[]{:S(2)}, u32[]{:S(2)}) collective-permute-start(bf16[4,128,128]{2,1,0:T(8,128)(2,1)} %get-tuple-element.40), channel_id=1, source_target_pairs={{0,34},{2,36},{4,38},{6,32},{32,66},{34,68},{36,70},{38,64},{64,98... | collective-permute-start | bytes 393224 | tf_op jit(solution)/shard_map/ppermute | solution.py:296
  121.4 20.6 %copy-start.10 = (bf16[4,128,128]{2,1,0:T(8,128)(2,1)}, bf16[4,128,128]{2,1,0:T(8,128)(2,1)S(1)}, u32[]{:S(2)}) copy-start(bf16[4,128,128]{2,1,0:T(8,128)(2,1)S(1)} %collective-permute-done.10.lo0) | copy-start | bytes 393220
  121.4 7.9 %collective-permute-start.13 = (bf16[4,128,128]{2,1,0:T(8,128)(2,1)}, bf16[4,128,128]{2,1,0:T(8,128)(2,1)S(1)}, u32[]{:S(2)}, u32[]{:S(2)}) collective-permute-start(bf16[4,128,128]{2,1,0:T(8,128)(2,1)} %get-tuple-element.41), channel_id=1, source_target_pairs={{0,6},{2,0},{4,2},{6,4},{32,38},{34,32},{36,34},{38,36},{64,70},{6... | collective-permute-start | bytes 393224 | tf_op jit(solution)/shard_map/ppermute | solution.py:296
  123.6 18.3 %copy-start.11 = (bf16[4,128,128]{2,1,0:T(8,128)(2,1)}, bf16[4,128,128]{2,1,0:T(8,128)(2,1)S(1)}, u32[]{:S(2)}) copy-start(bf16[4,128,128]{2,1,0:T(8,128)(2,1)S(1)} %collective-permute-done.11.lo1) | copy-start | bytes 393220
  123.6 6.0 %collective-permute-start.14 = (bf16[4,128,128]{2,1,0:T(8,128)(2,1)}, bf16[4,128,128]{2,1,0:T(8,128)(2,1)S(1)}, u32[]{:S(2)}, u32[]{:S(2)}) collective-permute-start(bf16[4,128,128]{2,1,0:T(8,128)(2,1)} %get-tuple-element.42), channel_id=1, source_target_pairs={{0,102},{2,96},{4,98},{6,100},{32,6},{34,0},{36,2},{38,4},{64,38},... | collective-permute-start | bytes 393224 | tf_op jit(solution)/shard_map/ppermute | solution.py:296
  129.3 12.6 %copy-start.12 = (bf16[4,128,128]{2,1,0:T(8,128)(2,1)}, bf16[4,128,128]{2,1,0:T(8,128)(2,1)S(1)}, u32[]{:S(2)}) copy-start(bf16[4,128,128]{2,1,0:T(8,128)(2,1)S(1)} %collective-permute-done.12.lo2) | copy-start | bytes 393220
  129.3 6.6 %collective-permute-start.15 = (bf16[4,128,128]{2,1,0:T(8,128)(2,1)}, bf16[4,128,128]{2,1,0:T(8,128)(2,1)S(1)}, u32[]{:S(2)}, u32[]{:S(2)}) collective-permute-start(bf16[4,128,128]{2,1,0:T(8,128)(2,1)} %get-tuple-element.43), channel_id=1, source_target_pairs={{0,38},{2,32},{4,34},{6,36},{32,70},{34,64},{36,66},{38,68},{64,10... | collective-permute-start | bytes 393224 | tf_op jit(solution)/shard_map/ppermute | solution.py:296
  129.3 12.6 %copy-start.13 = (bf16[4,128,128]{2,1,0:T(8,128)(2,1)}, bf16[4,128,128]{2,1,0:T(8,128)(2,1)S(1)}, u32[]{:S(2)}) copy-start(bf16[4,128,128]{2,1,0:T(8,128)(2,1)S(1)} %collective-permute-done.13.hi0) | copy-start | bytes 393220
  129.6 12.4 %copy-start.14 = (bf16[4,128,128]{2,1,0:T(8,128)(2,1)}, bf16[4,128,128]{2,1,0:T(8,128)(2,1)S(1)}, u32[]{:S(2)}) copy-start(bf16[4,128,128]{2,1,0:T(8,128)(2,1)S(1)} %collective-permute-done.14.hi1) | copy-start | bytes 393220
  135.9 6.0 %copy-start.15 = (bf16[4,128,128]{2,1,0:T(8,128)(2,1)}, bf16[4,128,128]{2,1,0:T(8,128)(2,1)S(1)}, u32[]{:S(2)}) copy-start(bf16[4,128,128]{2,1,0:T(8,128)(2,1)S(1)} %collective-permute-done.15.hi2) | copy-start | bytes 393220
  135.9 6.0 %copy-start.2 = (bf16[8,272,128]{2,1,0:T(8,128)(2,1)}, bf16[8,272,128]{2,1,0:T(8,128)(2,1)S(1)}, u32[]{:S(2)}) copy-start(bf16[8,272,128]{2,1,0:T(8,128)(2,1)S(1)} %all-to-all-done.2.mq) | copy-start | bytes 1671172
  136.0 6.0 %copy-start.6 = (bf16[4,4,128,128]{3,2,1,0:T(8,128)(2,1)}, bf16[4,4,128,128]{3,2,1,0:T(8,128)(2,1)S(1)}, u32[]{:S(2)}) copy-start(bf16[4,4,128,128]{3,2,1,0:T(8,128)(2,1)S(1)} %collective-permute-done.8.rx0) | copy-start | bytes 1572868
  136.0 6.0 %copy-start.7 = (bf16[4,4,128,128]{3,2,1,0:T(8,128)(2,1)}, bf16[4,4,128,128]{3,2,1,0:T(8,128)(2,1)S(1)}, u32[]{:S(2)}) copy-start(bf16[4,4,128,128]{3,2,1,0:T(8,128)(2,1)S(1)} %collective-permute-done.9.rx2) | copy-start | bytes 1572868
  165.9 33.5 %copy-start.22 = (f32[8,128]{1,0:T(8,128)S(1)}, f32[8,128]{1,0:T(8,128)}, u32[]{:S(2)}) copy-start(f32[8,128]{1,0:T(8,128)} %get-tuple-element.55) | copy-start | bytes 12292
  191.8 21.2 %copy-start.3 = (bf16[64,16,512]{2,1,0:T(8,128)(2,1)}, bf16[64,16,512]{2,1,0:T(8,128)(2,1)S(1)}, u32[]{:S(2)}) copy-start(bf16[64,16,512]{2,1,0:T(8,128)(2,1)S(1)} %all_to_all.32.near) | copy-start | bytes 3145732
  191.9 21.2 %collective-permute-start.16 = (bf16[64,16,512]{2,1,0:T(8,128)(2,1)S(1)}, bf16[64,16,512]{2,1,0:T(8,128)(2,1)S(1)}, u32[]{:S(2)}, u32[]{:S(2)}) collective-permute-start(bf16[64,16,512]{2,1,0:T(8,128)(2,1)S(1)} %all_to_all.32.near), channel_id=1, source_target_pairs={{0,8},{8,0},{1,9},{9,1},{2,10},{10,2},{3,11},{11,3},{4,12},{12,4},... | collective-permute-start | bytes 3145736 | tf_op jit(solution)/shard_map/ppermute | solution.py:393
  195.9 12.8 %all-to-all-start.3 = ((bf16[8,256,128]{2,1,0:T(8,128)(2,1)}), bf16[8,256,128]{2,1,0:T(8,128)(2,1)S(1)}, u32[]{:S(2)}, u32[]{:S(2)}) async-start(bf16[8,256,128]{2,1,0:T(8,128)(2,1)} %bitcast.11), calls=%async_computation.3 | async-start | bytes 1048576 | tf_op jit(solution)/shard_map/all_to_all | solution.py:381
  208.7 0.8 copy-start.4
  213.1 1.0 copy-start.5
Sparse Core Ops, SparseCore 0:
  9.6 70.7 all-gather.2
  82.1 59.7 all-gather.4

commit v3 on v2

v3 whole, which is shorter than its diff:
```python
import math

import jax
import jax.numpy as jnp
from jax import lax
from jax.experimental import pallas as pl
from jax.experimental.pallas import tpu as pltpu
from jax.sharding import Mesh, PartitionSpec as P

NORM_EPS = 1e-05
HEAD_EPS = 1e-06
D = 512
H = 8
DH = 64
BLK = 128
NB = 27
ROWS = 256
SCALE = DH**-0.5
BF = jnp.bfloat16
F32 = jnp.float32
GROUP = ("gx", "zl", "cr")
RING = ("zl", "tx", "zh")
CHIPS = ("gx", "zl", "tx", "zh")
ALL = ("gx", "zl", "cr", "tx", "zh")
EXTRA = 8
VMEM_LIMIT = 56 * 1024 * 1024


def params():
    return pltpu.CompilerParams(vmem_limit_bytes=VMEM_LIMIT)


def cost(micros):
    return pl.CostEstimate(
        flops=int(micros * 1e9), bytes_accessed=int(micros * 1e6), transcendentals=0
    )


def dot_nn(left, right):
    return jnp.dot(left, right, preferred_element_type=F32)


def dot_nt(left, right):
    return lax.dot_general(left, right, (((1,), (1,)), ((), ())), preferred_element_type=F32)


def dot_tn(left, right):
    return lax.dot_general(left, right, (((0,), (0,)), ((), ())), preferred_element_type=F32)


def head(values, index):
    return values[:, index * DH : (index + 1) * DH]


def normed_hidden(tokens, gain):
    values = tokens.astype(F32)
    factor = lax.rsqrt(jnp.mean(values * values, axis=-1, keepdims=True) + NORM_EPS)
    unit = values * factor
    return unit, factor, (unit * gain).astype(BF)


def high_low(values):
    upper = values.astype(BF).astype(F32)
    return upper, values - upper


def seat(h, slot):
    return (h // 2) * 4 + slot * 2 + h % 2


def project_kernel(
    place, tok, gain, cot, neighbours, valid, wq, wk, wv, wp, kv_out, qb_out, rows_out
):
    _, _, hidden = normed_hidden(tok[...], gain[...])
    for k in range(8):
        lines = slice((k % 2) * BLK, (k % 2 + 1) * BLK)
        rows_out[k, :, :D] = hidden[lines]
        rows_out[k, :, D:] = cot[lines]
    lane = lax.broadcasted_iota(jnp.int32, (ROWS, 128), 1)
    factors = jnp.zeros((ROWS, 128), F32)
    key_f = dot_nn(hidden, wk[...])
    value = dot_nn(hidden, wv[...]).astype(BF)
    for h in range(H):
        part = head(key_f, h)
        factor = lax.rsqrt(jnp.mean(part * part, axis=-1, keepdims=True) + HEAD_EPS)
        factors = jnp.where(lane == H + h, factor, factors)
        joined = jnp.concatenate([(part * factor).astype(BF), head(value, h)], axis=1)
        kv_out[seat(h, 0)] = joined[:BLK]
        kv_out[seat(h, 1)] = joined[BLK:]
    query_f = dot_nn(hidden, wq[...])
    back = dot_nt(cot[...], wp[...]).astype(BF)
    for h in range(H):
        part = head(query_f, h)
        factor = lax.rsqrt(jnp.mean(part * part, axis=-1, keepdims=True) + HEAD_EPS)
        factors = jnp.where(lane == h, factor, factors)
        joined = jnp.concatenate([(part * factor).astype(BF), head(back, h)], axis=1)
        qb_out[seat(h, 0), :BLK] = joined[:BLK]
        qb_out[seat(h, 1), :BLK] = joined[BLK:]
    ids = neighbours[...]
    keep = valid[...]
    own_t = place[2] + lax.broadcasted_iota(jnp.int32, (2, NB), 0)
    step_t = jnp.bitwise_and(ids - own_t + 1, 15)
    step_y = jnp.bitwise_and(jnp.right_shift(ids, 4) - place[1] + 1, 3)
    step_x = jnp.bitwise_and(jnp.right_shift(ids, 6) - place[0] + 1, 3)
    slots = step_x * 9 + step_y * 3 + step_t
    short = lax.broadcasted_iota(jnp.int32, (2, 128), 1)
    kept = jnp.zeros((2, 128), F32)
    for slot in range(NB):
        hit = short == slots[:, slot : slot + 1]
        kept = kept + jnp.where(hit, keep[:, slot : slot + 1].astype(F32), 0.0)
    turned = factors.T
    for h in range(H):
        for slot in range(2):
            lanes = slice(slot * BLK, (slot + 1) * BLK)
            rows = [kept[slot : slot + 1]]
            rows += list(high_low(turned[h : h + 1, lanes]))
            rows += list(high_low(turned[H + h : H + h + 1, lanes]))
            rows.append(jnp.zeros((3, 128), F32))
            qb_out[seat(h, slot), BLK:] = jnp.concatenate(rows, axis=0).astype(BF)


def attend_kernel(
    coef, keep, own, before, after, qb, mq_out, mqt_out, own_out, before_out, after_out,
    kvall, kvt, acc, wbuf, sems,
):
    copies = []
    for number, src in enumerate((before, own, after)):
        copies.append(pltpu.make_async_copy(src, kvall.at[:, number], sems.at[number]))
    for copy in copies:
        copy.start()
    acc[...] = jnp.zeros_like(acc)
    for copy in copies:
        copy.wait()
    for place in range(16):
        for t in range(3):
            kvt[place, :, t * BLK : (t + 1) * BLK] = kvall[place, t].T

    exp_coef = coef[0]
    grad_coef = coef[1]
    lane = lax.broadcasted_iota(jnp.int32, (BLK, 2 * DH), 1)
    low = (lane < DH).astype(F32).astype(BF)
    high = (lane >= DH).astype(F32).astype(BF)

    def fold(values):
        return jnp.sum(values.reshape(-1, 8, BLK), axis=0)

    def one_block(number, carry):
        x = number // 4
        y = number % 4
        both = qb[number, :BLK, :]
        spread = jnp.concatenate([both * low, both * high], axis=0)
        total = jnp.zeros((8, BLK), F32)
        inner = jnp.zeros((8, BLK), F32)
        for g in range(9):
            dx, dy = g // 3, g % 3
            place = (x + dx + 3) % 4 * 4 + (y + dy + 3) % 4
            keys = kvall[place].reshape(3 * BLK, 2 * DH)
            pair = dot_nt(keys, spread)
            for k in range(3):
                score = pair[k * BLK : (k + 1) * BLK, :BLK]
                slope = pair[k * BLK : (k + 1) * BLK, BLK:]
                weight = jnp.exp2(score * exp_coef) * keep[number * NB + g * 3 + k]
                total = total + fold(weight)
                inner = inner + fold(weight * slope)
                base = (g * 3 + k) * BLK
                wbuf[base : base + BLK, :BLK] = weight
                wbuf[base : base + BLK, BLK:] = slope
        total_row = jnp.sum(total, axis=0, keepdims=True)
        inverse = 1.0 / total_row
        inner_row = jnp.sum(inner, axis=0, keepdims=True) * inverse
        out = jnp.zeros((2 * DH, 2 * BLK), F32)
        for g in range(9):
            dx, dy = g // 3, g % 3
            place = (x + dx + 3) % 4 * 4 + (y + dy + 3) % 4
            base = g * 3 * BLK
            prob = wbuf[base : base + 3 * BLK, :BLK] * inverse
            slope = wbuf[base : base + 3 * BLK, BLK:]
            scaled = (prob * (slope - inner_row)) * grad_coef
            mixed = jnp.concatenate([scaled.astype(BF), prob.astype(BF)], axis=1)
            update = dot_nn(mixed, spread)
            acc[place] += update.reshape(3, BLK, 2 * DH)
            out = out + dot_nn(kvt[place], mixed)
        extra = qb[number, BLK:, :].astype(F32)
        factor = extra[1:2] + extra[2:3]
        query_t = both.astype(F32).T[:DH]
        grad_t = out[:DH, :BLK]
        inside = jnp.sum(query_t * grad_t, axis=0, keepdims=True)
        query_d = (grad_t - query_t * (inside * (1.0 / DH))) * factor
        joined = jnp.concatenate([out[DH:, BLK:], query_d], axis=0)
        mq_out[number, :BLK, :] = joined.T.astype(BF)
        mqt_out[number] = joined.astype(BF)
        return carry + inside

    inside = lax.fori_loop(0, 16, one_block, jnp.zeros((1, BLK), F32))
    upper, lower = high_low(jnp.broadcast_to(jnp.sum(inside, axis=1, keepdims=True), (1, BLK)))
    tail = jnp.concatenate([upper, lower, jnp.zeros((6, BLK), F32)], axis=0).astype(BF)
    for chunk in range(16):
        mq_out[chunk, BLK:, :] = tail
    own_out[...] = acc[:, 1]
    before_out[...] = acc[:, 0].astype(BF)
    after_out[...] = acc[:, 2].astype(BF)


def head_kernel(
    site, own, low, high, kv, qb, mqt, mq, near, far, kv_out, parts_out, turned,
):
    core = site[0]
    for b in range(16):
        total = own[b] + low[b].astype(F32) + high[b].astype(F32)
        total_t = total.T
        key_t = kv[b].astype(F32).T[:DH]
        extra = qb[b, BLK:, :].astype(F32)
        factor = extra[3:4] + extra[4:5]
        grad_t = total_t[:DH]
        inside = jnp.sum(key_t * grad_t, axis=0, keepdims=True) * (1.0 / DH)
        joined = jnp.concatenate([(grad_t - key_t * inside) * factor, total_t[DH:]], axis=0)
        turned[b] = joined.astype(BF)
        target_x = jnp.bitwise_xor(site[1], b // 4)
        target_y = jnp.bitwise_xor(site[2], b % 4)
        kv_out[target_x, target_y] = joined.T.astype(BF)
    query_part = jnp.zeros((DH, D), F32)
    proj_part = jnp.zeros((DH, D), F32)
    both_part = jnp.zeros((2 * DH, D), F32)
    for which, source in ((core, near), (1 - core, far)):
        for half in range(2):
            rows = source[half * 4 : half * 4 + 4].reshape(4 * BLK, 2 * D)
            hidden, cot = rows[:, :D], rows[:, D:]
            spots = [(half * 4 + k) * 2 + which for k in range(4)]
            mixed_t = jnp.concatenate([mqt[spot] for spot in spots], axis=1)
            both_t = jnp.concatenate([turned[spot] for spot in spots], axis=1)
            proj_part = proj_part + dot_nn(mixed_t[:DH], cot)
            query_part = query_part + dot_nn(mixed_t[DH:], hidden)
            both_part = both_part + dot_nn(both_t, hidden)
    lines = []
    for row in (BLK, BLK + 1):
        pairs = [
            mq[seat(h, 0), row : row + 1].astype(F32) + mq[seat(h, 1), row : row + 1].astype(F32)
            for h in range(H)
        ]
        lines.append(0.5 * jnp.concatenate(pairs, axis=0))
    whole_sum = lines[0] + lines[1]
    upper, lower = high_low(whole_sum)
    extra = jnp.concatenate([upper, lower, upper, lower], axis=1).astype(BF)
    joined = jnp.concatenate([query_part, both_part, proj_part], axis=0).astype(BF)
    for g in range(16):
        parts_out[g, :16] = joined[g * 16 : (g + 1) * 16]
        parts_out[g, 16:] = extra


def sum_kernel(arrived, share_out, temper_out):
    total = jnp.zeros((24, D), F32)
    for g in range(16):
        total = total + arrived[g].astype(F32)
    temper_out[...] = total[16:, :128] + total[16:, 128:256]
    share = total[:16].astype(BF)
    for k in range(64):
        share_out[k] = share


def output_kernel(core, near, far, gain, wq, wk, wv, gq, gk, gv, gp, gg, turned):
    for which, source in ((core[0], near), (1 - core[0], far)):
        for chip in range(64):
            gx, zl, tx, zh = chip // 16, chip // 8 % 2, chip // 2 % 4, chip % 2
            quarter = tx % 2 * 2 + zh
            start = pl.multiple_of(gx * 128 + which * 64 + quarter * 16, 16)
            turned[zl * 2 + tx // 2, pl.ds(start, 16), :] = source[chip]
    gp[...] = turned[3].astype(F32)
    total = jnp.zeros((D, 1), F32)
    for m, (out, weight) in enumerate(((gq, wq), (gk, wk), (gv, wv))):
        value = turned[m].T.astype(F32)
        out[...] = value
        total = total + jnp.sum(value * weight[...].astype(F32), axis=1, keepdims=True)
    line = jnp.broadcast_to(total, (D, 128)).T
    gg[...] = line[:1] / gain[...]


def finish_kernel(
    site, tok, gain, mq, kv0, kv1, kv2, kv3, wq, wk, wv, wp, layer_out, grad_tok, kv,
):
    for step_y, piece in enumerate((kv0, kv1, kv2, kv3)):
        for step_x in range(4):
            source_x = jnp.bitwise_xor(site[1], step_x)
            source_y = jnp.bitwise_xor(site[2], step_y)
            kv[source_x * 4 + source_y] = piece[step_x]

    def gathered(ref, lanes):
        halves = [
            jnp.concatenate([ref[seat(h, slot), :BLK, lanes] for h in range(H)], axis=1)
            for slot in range(2)
        ]
        return jnp.concatenate(halves, axis=0)

    left, right = slice(0, DH), slice(DH, 2 * DH)
    unit, factor_in, _ = normed_hidden(tok[...], gain[...])
    layer_out[...] = dot_nn(gathered(mq, left), wp[...]).astype(BF)
    query_d, key_d, value_d = gathered(mq, right), gathered(kv, left), gathered(kv, right)
    back_hidden = dot_nt(query_d, wq[...]) + dot_nt(key_d, wk[...]) + dot_nt(value_d, wv[...])
    slope_in = back_hidden * gain[...]
    grad_tok[...] = factor_in * (
        slope_in - unit * jnp.mean(slope_in * unit, axis=-1, keepdims=True)
    )


def whole(shape, dtype):
    return jax.ShapeDtypeStruct(shape, dtype)


def shift(block, step):
    spots = [(t % 2) * 8 + t // 2 for t in range(16)]
    return lax.ppermute(block, RING, [(spots[t], spots[(t + step) % 16]) for t in range(16)])


def swap_cores(block):
    return lax.ppermute(block, "cr", [(0, 1), (1, 0)])


def swap_near(block, axes, step):
    return lax.ppermute(block, axes, [(i, i ^ step) for i in range(4)])


def local(
    tokens, norm_gain, w_query, w_key, w_value, w_proj, temper, neighbours, valid_mask, cotangent
):
    tok = tokens.reshape(ROWS, D)
    cot = cotangent.reshape(ROWS, D)
    gain = norm_gain.reshape(1, D)
    core = lax.axis_index("cr")
    place = jnp.stack(
        [
            lax.axis_index("gx"),
            lax.axis_index("zl") * 2 + core,
            (lax.axis_index("tx") * 2 + lax.axis_index("zh")) * 2,
        ]
    )
    any_spec = pl.BlockSpec(memory_space=pl.ANY)
    smem = pl.BlockSpec(memory_space=pltpu.SMEM)
    vmem = pl.BlockSpec(memory_space=pltpu.VMEM)

    pair = (16, BLK, 2 * DH)
    wide = (16, BLK + EXTRA, 2 * DH)
    kv_send, qb_send, rows_send = pl.pallas_call(
        project_kernel,
        cost_estimate=cost(6),
        out_shape=(whole(pair, BF), whole(wide, BF), whole((8, BLK, 2 * D), BF)),
        in_specs=[smem] + [vmem] * 9,
        out_specs=(vmem, vmem, vmem),
        compiler_params=params(),
    )(
        place, tok, gain, cot, neighbours.reshape(2, NB), valid_mask.reshape(2, NB),
        w_query, w_key, w_value, w_proj,
    )

    own = lax.all_to_all(kv_send, GROUP, 0, 0, tiled=True)
    before = shift(own, 1)
    after = shift(own, -1)
    qb_send, own = lax.optimization_barrier((qb_send, own))
    qb = lax.all_to_all(qb_send, GROUP, 0, 0, tiled=True)
    rows_send, qb, before, after = lax.optimization_barrier((rows_send, qb, before, after))
    rows_near = lax.all_to_all(rows_send, ("gx", "zl"), 0, 0, tiled=True)
    keep = qb[:, BLK, :NB].astype(F32).reshape(16 * NB)
    head_id = lax.axis_index("gx") * 2 + core
    temp = temper[head_id] * SCALE
    coef = jnp.stack([temp * math.log2(math.e), temp])

    mq_send, mqt, own_grad, before_grad, after_grad = pl.pallas_call(
        attend_kernel,
        cost_estimate=cost(36),
        out_shape=(
            whole(wide, BF), whole((16, 2 * DH, BLK), BF), whole(pair, F32),
            whole(pair, BF), whole(pair, BF),
        ),
        in_specs=[smem, smem] + [any_spec] * 3 + [vmem],
        out_specs=tuple([vmem] * 5),
        scratch_shapes=[
            pltpu.VMEM((16, 3, BLK, 2 * DH), BF),
            pltpu.VMEM((16, 2 * DH, 3 * BLK), BF),
            pltpu.VMEM((16, 3, BLK, 2 * DH), F32),
            pltpu.VMEM((NB * BLK, 2 * BLK), F32),
            pltpu.SemaphoreType.DMA((3,)),
        ],
        compiler_params=params(),
    )(coef, keep, own, before, after, qb)
    from_after = shift(before_grad, -1)
    from_before = shift(after_grad, 1)
    rows_near, mq_send = lax.optimization_barrier((rows_near, mq_send))
    rows_far = swap_cores(rows_near)
    mq = lax.all_to_all(mq_send, GROUP, 0, 0, tiled=True)
    site = jnp.stack([core, lax.axis_index("gx"), lax.axis_index("zl") * 2 + core])
    kv_back, parts = pl.pallas_call(
        head_kernel,
        cost_estimate=cost(7),
        out_shape=(whole((4, 4, BLK, 2 * DH), BF), whole((16, 24, D), BF)),
        in_specs=[smem] + [vmem] * 9,
        scratch_shapes=[pltpu.VMEM((16, 2 * DH, BLK), BF)],
        compiler_params=params(),
    )(site, own_grad, from_after, from_before, own, qb, mqt, mq, rows_near, rows_far)
    arrived = lax.all_to_all(parts, RING, 0, 0, tiled=True)
    turn = [kv_back[0]] + [swap_near(kv_back[step], "gx", step) for step in range(1, 4)]
    arrived, *turn = lax.optimization_barrier((arrived, *turn))
    share, temper_sum = pl.pallas_call(
        sum_kernel,
        cost_estimate=cost(2),
        out_shape=(whole((64, 16, D), BF), whole((H, 128), F32)),
        compiler_params=params(),
    )(arrived)
    near = lax.all_to_all(share, CHIPS, 0, 0, tiled=True)
    kv = [jnp.stack([piece[step] for piece in turn]) for step in range(4)]
    kv = [kv[0]] + [swap_near(kv[step], ("zl", "cr"), step) for step in range(1, 4)]
    near, *kv = lax.optimization_barrier((near, *kv))
    layer_out, grad_tokens = pl.pallas_call(
        finish_kernel,
        cost_estimate=cost(4),
        out_shape=(whole((ROWS, D), BF), whole((ROWS, D), F32)),
        in_specs=[smem] + [vmem] * 11,
        scratch_shapes=[pltpu.VMEM(pair, BF)],
        compiler_params=params(),
    )(site, tok, gain, mq, *kv, w_query, w_key, w_value, w_proj)
    far = swap_cores(near)
    square = whole((D, D), F32)
    gq, gk, gv, gp, grad_gain = pl.pallas_call(
        output_kernel,
        cost_estimate=cost(5),
        out_shape=(square, square, square, square, whole((1, D), F32)),
        in_specs=[smem] + [vmem] * 6,
        scratch_shapes=[pltpu.VMEM((4, D, D), BF)],
        compiler_params=params(),
    )(core.reshape(1), near, far, gain, w_query, w_key, w_value)
    grad_temper = temper_sum[:, 0] / temper
    return (
        layer_out.reshape(tokens.shape),
        grad_tokens.reshape(tokens.shape),
        grad_gain.reshape(D),
        gq,
        gk,
        gv,
        gp,
        grad_temper,
    )


def solution(mesh):
    fine = Mesh(mesh.devices.reshape(4, 2, 2, 4, 2), ALL)
    lattice = ("gx", ("zl", "cr"), ("tx", "zh"))
    blocks = P(*lattice, None, None)
    lists = P(*lattice, None)
    return jax.shard_map(
        local,
        mesh=fine,
        in_specs=(blocks, P(), P(), P(), P(), P(), P(), lists, lists, blocks),
        out_specs=(blocks, blocks, P(), P(), P(), P(), P(), P()),
        check_vma=False,
    )
```

time: 226 us -> 174 us (0.77)
  blocking collectives: 68.7 us -> 17.1 us
  between operations: 15.6 us -> 2.08 us
  starting transfers between devices: 39.2 us -> 45.5 us
  waiting for transfers between devices: 37 us -> 41.8 us
    all_to_all x3 -> x1, blocking collectives: 68.7 us -> 17.1 us  [local(): own = lax.all_to_all(kv_send, GROUP, 0, 0, tiled=True)]
    ppermute x17 -> x12, waiting for transfers between devices: 12.8 us -> 30.1 us  [the longest x6 19.1 us: swap_near(): return lax.ppermute(block, axes, [(i, i ^ step) for i in range(4)])]
    all_to_all x3 -> x5, starting transfers between devices: 11.4 us -> 27.2 us  [the longest x1 9.65 us: local(): near = lax.all_to_all(share, CHIPS, 0, 0, tiled=True)]
    ppermute x17 -> x12, starting transfers between devices: 27.7 us -> 18.4 us  [the longest x6 8.37 us: swap_near(): return lax.ppermute(block, axes, [(i, i ^ step) for i in range(4)])]
    all_gather x2 -> x0, waiting for transfers between devices: 5.95 us -> none  [the longest x1 5.93 us: local(): cot_all = lax.all_gather(cot, ZLINE, axis=0, tiled=True)]
    all_to_all x3 -> x5, waiting for transfers between devices: 16.9 us -> 11.6 us  [the longest x1 10.8 us: local(): qb = lax.all_to_all(qb_send, GROUP, 0, 0, tiled=True)]
  transfers between devices with their start and end apart: 22 -> 17, of which waited for: 10 -> 9; matrix products, arithmetic and copies ran while one was open for 1% -> 2% of each run, Pallas kernels for 20% -> 22%
where the time goes in v3:
time: 174 us; the launch traced here: 173 us
  Pallas kernels  57.5 us (33%)
  starting transfers between devices  45.5 us (26%)
  waiting for transfers between devices  41.8 us (24%)
  blocking collectives  17.1 us (10%)
  local copies, waits for them, and re-layouts  5.99 us (3%)
  other arithmetic  3.05 us (2%)
  between operations  2.08 us (1%)
    pallas_call x1, Pallas kernels, local(): pl.pallas_call(attend_kernel, cost_estimate=cost(36), out_shape=(whole(wi...  34.8 us
    ppermute x6, waiting for transfers between devices, swap_near(): return lax.ppermute(block, axes, [(i, i ^ step) for i in range(4)])  19.1 us
    all_to_all x1, blocking collectives, local(): own = lax.all_to_all(kv_send, GROUP, 0, 0, tiled=True)  17.1 us
    ppermute x4, waiting for transfers between devices, shift(): lax.ppermute(block, RING, [(spots[t], spots[(t + step) % 16]) for t in ra...  11 us
    all_to_all x1, waiting for transfers between devices, local(): qb = lax.all_to_all(qb_send, GROUP, 0, 0, tiled=True)  10.8 us
    all_to_all x1, starting transfers between devices, local(): near = lax.all_to_all(share, CHIPS, 0, 0, tiled=True)  9.65 us
    ppermute x6, starting transfers between devices, swap_near(): return lax.ppermute(block, axes, [(i, i ^ step) for i in range(4)])  8.37 us
    ppermute x4, starting transfers between devices, shift(): lax.ppermute(block, RING, [(spots[t], spots[(t + step) % 16]) for t in ra...  8.12 us
  transfers between devices with their start and end apart: 17, of which 9 were waited for; matrix products, arithmetic and copies ran while one was open for 2% of the time, Pallas kernels for 22%

profile of v3, /device:TPU:1, one launch (start us, length us, event | category | flops | bytes accessed | tf_op | source)
XLA Modules:
  0.0 173.0 jit_solution(1754600999938806563)
XLA Ops:
  0.6 0.6 pad_add_fusion.1.place
  1.2 6.5 %shard_map.161 = (bf16[16,128,128]{2,1,0:T(8,128)(2,1)}, bf16[16,136,128]{2,1,0:T(8,128)(2,1)}, bf16[8,128,1024]{2,1,0:T(8,128)(2,1)}) custom-call(s32[3]{0:T(128)} %pad_add_fusion.1.place, bf16[256,512]{1,0:T(8,128)(2,1)} %bitcast.21, f32[1,512]{1,0:T(1,128)} %bitcast.23, bf16[256,512]{1,0:T(8,128)(2,1)} %bitcast.20, s32[2,27]{1,0:T(2,128)} %bitcast.26, ...), custom_call_target="tpu_custom_call" | custom-call | flops 6000000000 | bytes 6000000 | tf_op jit(solution)/shard_map/pallas_call | solution.py:341
  7.7 17.1 %all_to_all.30.own.kv = bf16[16,128,128]{2,1,0:T(8,128)(2,1)S(1)} all-to-all(bf16[16,128,128]{2,1,0:T(8,128)(2,1)} %get-tuple-element.47), channel_id=1, replica_groups=mesh['gx'=4,'zl'=2,'cr'=2,'tx'=4,'zh'=2] {'gx','zl','cr'}, dimensions={0} | all-to-all | bytes 1048576 | tf_op jit(solution)/shard_map/all_to_all | solution.py:353
  24.8 5.5 %collective-permute-start.1 = (bf16[16,128,128]{2,1,0:T(8,128)(2,1)S(1)}, bf16[16,128,128]{2,1,0:T(8,128)(2,1)S(1)}, u32[]{:S(2)}, u32[]{:S(2)}) collective-permute-start(bf16[16,128,128]{2,1,0:T(8,128)(2,1)S(1)} %all_to_all.30.own.kv), channel_id=1, source_target_pairs={{0,23},{16,0},{1,16},{17,1},{2,17},{18,2},{3,18},{19,3},{4,19},{20... | collective-permute-start | bytes 1572872 | tf_op jit(solution)/shard_map/ppermute | solution.py:310
  30.3 3.9 %all-to-all-start.1 = ((bf16[16,136,128]{2,1,0:T(8,128)(2,1)}), bf16[16,136,128]{2,1,0:T(8,128)(2,1)S(1)}, u32[]{:S(2)}, u32[]{:S(2)}) async-start(bf16[16,136,128]{2,1,0:T(8,128)(2,1)} %get-tuple-element.48), calls=%async_computation.1 | async-start | bytes 1114112 | tf_op jit(solution)/shard_map/all_to_all | solution.py:357
  34.2 0.6 dynamic_slice.3
  36.1 0.6 pad_maximum_fusion.4.coef
  36.7 10.8 %all-to-all-done.1.qb = bf16[16,136,128]{2,1,0:T(8,128)(2,1)S(1)} async-done(((bf16[16,136,128]{2,1,0:T(8,128)(2,1)}), bf16[16,136,128]{2,1,0:T(8,128)(2,1)S(1)}, u32[]{:S(2)}, u32[]{:S(2)}) %all-to-all-start.1) | async-done | bytes 557088 | tf_op jit(solution)/shard_map/all_to_all | solution.py:357
  47.5 0.0 collective-permute-done.1.after
  47.5 0.0 collective-permute-done.before
  47.5 0.8 copy-done.8
  48.4 0.7 reshape.59.keep
  49.1 0.0 copy-done.9
  49.1 4.0 %all-to-all-start.2 = ((bf16[8,128,1024]{2,1,0:T(8,128)(2,1)}), bf16[8,128,1024]{2,1,0:T(8,128)(2,1)S(1)}, u32[]{:S(2)}, u32[]{:S(2)}) async-start(bf16[8,128,1024]{2,1,0:T(8,128)(2,1)} %get-tuple-element.49), calls=%async_computation.2 | async-start | bytes 4194304 | tf_op jit(solution)/shard_map/all_to_all | solution.py:359
  53.2 34.8 %shard_map.162 = (bf16[16,136,128]{2,1,0:T(8,128)(2,1)}, bf16[16,128,128]{2,1,0:T(8,128)(2,1)}, f32[16,128,128]{2,1,0:T(8,128)}, bf16[16,128,128]{2,1,0:T(8,128)(2,1)}, bf16[16,128,128]{2,1,0:T(8,128)(2,1)}) custom-call(f32[2]{0:T(128)} %pad_maximum_fusion.4.coef, f32[432]{0:T(512)} %reshape.59.keep, bf16[16,128,128]{2,1,0:T(8,128)(2,1)} %copy-done.4, ...), custom_call_target="tpu_custom_call" | custom-call | flops 35999997952 | bytes 36000000 | tf_op jit(solution)/shard_map/pallas_call | solution.py:365
  88.0 1.4 collective-permute-start.4
  89.4 2.6 %collective-permute-start.2 = (bf16[16,128,128]{2,1,0:T(8,128)(2,1)}, bf16[16,128,128]{2,1,0:T(8,128)(2,1)S(1)}, u32[]{:S(2)}, u32[]{:S(2)}) collective-permute-start(bf16[16,128,128]{2,1,0:T(8,128)(2,1)} %get-tuple-element.57), channel_id=1, source_target_pairs={{0,23},{16,0},{1,16},{17,1},{2,17},{18,2},{3,18},{19,3},{4,19},{20... | collective-permute-start | bytes 1572872 | tf_op jit(solution)/shard_map/ppermute | solution.py:310
  92.0 5.2 %all-to-all-start.3 = ((bf16[16,136,128]{2,1,0:T(8,128)(2,1)}), bf16[16,136,128]{2,1,0:T(8,128)(2,1)S(1)}, u32[]{:S(2)}, u32[]{:S(2)}) async-start(bf16[16,136,128]{2,1,0:T(8,128)(2,1)} %get-tuple-element.55), calls=%async_computation.3 | async-start | bytes 1114112 | tf_op jit(solution)/shard_map/all_to_all | solution.py:387
  97.2 0.6 pad_add_fusion.site
  97.8 10.3 %collective-permute-done.2.low = bf16[16,128,128]{2,1,0:T(8,128)(2,1)S(1)} collective-permute-done((bf16[16,128,128]{2,1,0:T(8,128)(2,1)}, bf16[16,128,128]{2,1,0:T(8,128)(2,1)S(1)}, u32[]{:S(2)}, u32[]{:S(2)}) %collective-permute-start.2) | collective-permute-done | bytes 524320 | tf_op jit(solution)/shard_map/ppermute | solution.py:310
  108.1 0.7 collective-permute-done.3.high
  108.8 0.8 all-to-all-done.3.mq
  109.6 0.0 collective-permute-done.4.far
  109.6 0.8 copy-done.3
  110.4 5.9 %shard_map.163 = (bf16[4,4,128,128]{3,2,1,0:T(8,128)(2,1)}, bf16[16,24,512]{2,1,0:T(8,128)(2,1)}) custom-call(s32[3]{0:T(128)} %pad_add_fusion.site, f32[16,128,128]{2,1,0:T(8,128)} %get-tuple-element.56.own, bf16[16,128,128]{2,1,0:T(8,128)(2,1)} %copy-done.10, bf16[16,128,128]{2,1,0:T(8,128)(2,1)} %collective-permute-done.3.high, ...), custom_call_target="tpu_custom_call" | custom-call | flops 7000000000 | bytes 7000000 | tf_op jit(solution)/shard_map/pallas_call | solution.py:389
  116.3 4.4 %all-to-all-start.4 = ((bf16[16,24,512]{2,1,0:T(8,128)(2,1)}), bf16[16,24,512]{2,1,0:T(8,128)(2,1)S(1)}, u32[]{:S(2)}, u32[]{:S(2)}) async-start(bf16[16,24,512]{2,1,0:T(8,128)(2,1)} %get-tuple-element.61), calls=%async_computation.4 | async-start | bytes 786432 | tf_op jit(solution)/shard_map/all_to_all | solution.py:397
  120.7 1.1 slice_bitcast_fusion
  121.8 2.0 %collective-permute-start.7 = (bf16[4,128,128]{2,1,0:T(8,128)(2,1)S(1)}, bf16[4,128,128]{2,1,0:T(8,128)(2,1)S(1)}, u32[]{:S(2)}, u32[]{:S(2)}) collective-permute-start(bf16[4,128,128]{2,1,0:T(8,128)(2,1)S(1)} %get-tuple-element.82), channel_id=1, source_target_pairs={{0,96},{32,64},{64,32},{96,0},{1,97},{33,65},{65,33},{97,1},{2,98}... | collective-permute-start | bytes 393224 | tf_op jit(solution)/shard_map/ppermute | solution.py:318
  123.8 0.6 collective-permute-start.6
  124.4 0.8 collective-permute-start.5
  125.2 2.0 %collective-permute-done.7 = bf16[4,128,128]{2,1,0:T(8,128)(2,1)S(1)} collective-permute-done((bf16[4,128,128]{2,1,0:T(8,128)(2,1)S(1)}, bf16[4,128,128]{2,1,0:T(8,128)(2,1)S(1)}, u32[]{:S(2)}, u32[]{:S(2)}) %collective-permute-start.7) | collective-permute-done | bytes 131104 | tf_op jit(solution)/shard_map/ppermute | solution.py:318
  127.1 2.3 %collective-permute-done.6 = bf16[4,128,128]{2,1,0:T(8,128)(2,1)S(1)} collective-permute-done((bf16[4,128,128]{2,1,0:T(8,128)(2,1)S(1)}, bf16[4,128,128]{2,1,0:T(8,128)(2,1)S(1)}, u32[]{:S(2)}, u32[]{:S(2)}) %collective-permute-start.6) | collective-permute-done | bytes 131104 | tf_op jit(solution)/shard_map/ppermute | solution.py:318
  129.5 0.3 collective-permute-done.5
  129.7 0.7 copy-done.5
  130.5 2.1 %shard_map.164 = (bf16[64,16,512]{2,1,0:T(8,128)(2,1)}, f32[8,128]{1,0:T(8,128)}) custom-call(bf16[16,24,512]{2,1,0:T(8,128)(2,1)} %copy-done.5), custom_call_target="tpu_custom_call" | custom-call | flops 2000000000 | bytes 2000000 | tf_op jit(solution)/shard_map/pallas_call | solution.py:400
  132.6 9.6 %all-to-all-start.5 = ((bf16[64,16,512]{2,1,0:T(8,128)(2,1)}), bf16[64,16,512]{2,1,0:T(8,128)(2,1)S(1)}, u32[]{:S(2)}, u32[]{:S(2)}) async-start(bf16[64,16,512]{2,1,0:T(8,128)(2,1)} %get-tuple-element.64), calls=%async_computation.5 | async-start | bytes 2097152 | tf_op jit(solution)/shard_map/all_to_all | solution.py:406
  142.3 3.0 %collective-permute-start.8 = (bf16[4,128,128]{2,1,0:T(8,128)(2,1)S(1)}, bf16[4,128,128]{2,1,0:T(8,128)(2,1)S(1)}, u32[]{:S(2)}, u32[]{:S(2)}) collective-permute-start(bf16[4,128,128]{2,1,0:T(8,128)(2,1)S(1)} %pad_maximum_fusion.1), channel_id=1, source_target_pairs={{0,8},{8,0},{16,24},{24,16},{1,9},{9,1},{17,25},{25,17},{2,10},{10... | collective-permute-start | bytes 393224 | tf_op jit(solution)/shard_map/ppermute | solution.py:318
  145.4 1.6 collective-permute-start.9
  147.0 0.4 collective-permute-start.10
  147.4 0.7 pad_maximum_fusion.kv0
  148.1 11.7 %collective-permute-done.9.kv2 = bf16[4,128,128]{2,1,0:T(8,128)(2,1)S(1)} collective-permute-done((bf16[4,128,128]{2,1,0:T(8,128)(2,1)S(1)}, bf16[4,128,128]{2,1,0:T(8,128)(2,1)S(1)}, u32[]{:S(2)}, u32[]{:S(2)}) %collective-permute-start.9) | collective-permute-done | bytes 131104 | tf_op jit(solution)/shard_map/ppermute | solution.py:318
  159.8 2.9 %collective-permute-done.10.kv3 = bf16[4,128,128]{2,1,0:T(8,128)(2,1)S(1)} collective-permute-done((bf16[4,128,128]{2,1,0:T(8,128)(2,1)S(1)}, bf16[4,128,128]{2,1,0:T(8,128)(2,1)S(1)}, u32[]{:S(2)}, u32[]{:S(2)}) %collective-permute-start.10) | collective-permute-done | bytes 131104 | tf_op jit(solution)/shard_map/ppermute | solution.py:318
  162.7 0.5 collective-permute-start.11
  163.1 0.1 slice_reduce_fusion
  163.3 0.5 div.3
  163.8 3.6 %shard_map.165 = (bf16[256,512]{1,0:T(8,128)(2,1)}, f32[256,512]{1,0:T(8,128)}) custom-call(s32[3]{0:T(128)} %pad_add_fusion.site, bf16[256,512]{1,0:T(8,128)(2,1)} %bitcast.22, f32[1,512]{1,0:T(1,128)} %bitcast.24, bf16[16,136,128]{2,1,0:T(8,128)(2,1)} %copy-done.3, bf16[4,128,128]{2,1,0:T(8,128)(2,1)} %pad_maximum_fusion.kv0, ...), custom_call_target="tpu_custom_call" | custom-call | flops 4000000000 | bytes 4000000 | tf_op jit(solution)/shard_map/pallas_call | solution.py:410
  167.4 1.0 copy-done.7
  168.4 4.6 %shard_map.166 = (f32[512,512]{1,0:T(8,128)}, f32[512,512]{1,0:T(8,128)}, f32[512,512]{1,0:T(8,128)}, f32[512,512]{1,0:T(8,128)}, f32[1,512]{1,0:T(1,128)}) custom-call(s32[1]{0:T(128)} %bitcast.core, bf16[64,16,512]{2,1,0:T(8,128)(2,1)} %copy-done.1, bf16[64,16,512]{2,1,0:T(8,128)(2,1)} %copy-done.7, f32[1,512]{1,0:T(1,128)} %bitcast.25, ...), custom_call_target="tpu_custom_call" | custom-call | flops 5000000000 | bytes 5000000 | tf_op jit(solution)/shard_map/pallas_call | solution.py:420
  (38 shorter events, 0.2 us)
Async XLA Ops:
  7.7 26.5 %copy-start.14 = (f32[8]{0:T(128)S(1)}, f32[8]{0:T(128)}, u32[]{:S(2)}) copy-start(f32[8]{0:T(128)} %param.16) | copy-start | bytes 100
  24.8 24.4 %copy-start.4 = (bf16[16,128,128]{2,1,0:T(8,128)(2,1)}, bf16[16,128,128]{2,1,0:T(8,128)(2,1)S(1)}, u32[]{:S(2)}) copy-start(bf16[16,128,128]{2,1,0:T(8,128)(2,1)S(1)} %all_to_all.30.own.kv) | copy-start | bytes 1572868
  24.8 22.7 %collective-permute-start.1 = (bf16[16,128,128]{2,1,0:T(8,128)(2,1)S(1)}, bf16[16,128,128]{2,1,0:T(8,128)(2,1)S(1)}, u32[]{:S(2)}, u32[]{:S(2)}) collective-permute-start(bf16[16,128,128]{2,1,0:T(8,128)(2,1)S(1)} %all_to_all.30.own.kv), channel_id=1, source_target_pairs={{0,23},{16,0},{1,16},{17,1},{2,17},{18,2},{3,18},{19,3},{4,19},{20... | collective-permute-start | bytes 1572872 | tf_op jit(solution)/shard_map/ppermute | solution.py:310
  30.3 17.2 %collective-permute-start = (bf16[16,128,128]{2,1,0:T(8,128)(2,1)S(1)}, bf16[16,128,128]{2,1,0:T(8,128)(2,1)S(1)}, u32[]{:S(2)}, u32[]{:S(2)}) collective-permute-start(bf16[16,128,128]{2,1,0:T(8,128)(2,1)S(1)} %all_to_all.30.own.kv), channel_id=1, source_target_pairs={{0,16},{16,1},{1,17},{17,2},{2,18},{18,3},{3,19},{19,4},{4,20},{20... | collective-permute-start | bytes 1572872 | tf_op jit(solution)/shard_map/ppermute | solution.py:310
  30.3 17.2 %all-to-all-start.1 = ((bf16[16,136,128]{2,1,0:T(8,128)(2,1)}), bf16[16,136,128]{2,1,0:T(8,128)(2,1)S(1)}, u32[]{:S(2)}, u32[]{:S(2)}) async-start(bf16[16,136,128]{2,1,0:T(8,128)(2,1)} %get-tuple-element.48), calls=%async_computation.1 | async-start | bytes 1114112 | tf_op jit(solution)/shard_map/all_to_all | solution.py:357
  47.5 1.6 copy-start.2
  47.5 0.8 copy-start.8
  48.3 0.8 copy-start.9
  49.1 38.8 %all-to-all-start.2 = ((bf16[8,128,1024]{2,1,0:T(8,128)(2,1)}), bf16[8,128,1024]{2,1,0:T(8,128)(2,1)S(1)}, u32[]{:S(2)}, u32[]{:S(2)}) async-start(bf16[8,128,1024]{2,1,0:T(8,128)(2,1)} %get-tuple-element.49), calls=%async_computation.2 | async-start | bytes 4194304 | tf_op jit(solution)/shard_map/all_to_all | solution.py:359
  88.0 21.6 %copy-start = (bf16[8,128,1024]{2,1,0:T(8,128)(2,1)}, bf16[8,128,1024]{2,1,0:T(8,128)(2,1)S(1)}, u32[]{:S(2)}) copy-start(bf16[8,128,1024]{2,1,0:T(8,128)(2,1)S(1)} %all-to-all-done.2.near) | copy-start | bytes 6291460
  88.0 21.6 %collective-permute-start.4 = (bf16[8,128,1024]{2,1,0:T(8,128)(2,1)S(1)}, bf16[8,128,1024]{2,1,0:T(8,128)(2,1)}, u32[]{:S(2)}, u32[]{:S(2)}) collective-permute-start(bf16[8,128,1024]{2,1,0:T(8,128)(2,1)S(1)} %all-to-all-done.2.near), channel_id=1, source_target_pairs={{0,8},{8,0},{1,9},{9,1},{2,10},{10,2},{3,11},{11,3},{4,12},{12,4},... | collective-permute-start | bytes 6291464 | tf_op jit(solution)/shard_map/ppermute | solution.py:314
  89.4 18.7 %collective-permute-start.2 = (bf16[16,128,128]{2,1,0:T(8,128)(2,1)}, bf16[16,128,128]{2,1,0:T(8,128)(2,1)S(1)}, u32[]{:S(2)}, u32[]{:S(2)}) collective-permute-start(bf16[16,128,128]{2,1,0:T(8,128)(2,1)} %get-tuple-element.57), channel_id=1, source_target_pairs={{0,23},{16,0},{1,16},{17,1},{2,17},{18,2},{3,18},{19,3},{4,19},{20... | collective-permute-start | bytes 1572872 | tf_op jit(solution)/shard_map/ppermute | solution.py:310
  92.0 16.8 %collective-permute-start.3 = (bf16[16,128,128]{2,1,0:T(8,128)(2,1)}, bf16[16,128,128]{2,1,0:T(8,128)(2,1)}, u32[]{:S(2)}, u32[]{:S(2)}) collective-permute-start(bf16[16,128,128]{2,1,0:T(8,128)(2,1)} %get-tuple-element.58), channel_id=1, source_target_pairs={{0,16},{16,1},{1,17},{17,2},{2,18},{18,3},{3,19},{19,4},{4,20},{20... | collective-permute-start | bytes 1572872 | tf_op jit(solution)/shard_map/ppermute | solution.py:310
  92.0 17.6 %all-to-all-start.3 = ((bf16[16,136,128]{2,1,0:T(8,128)(2,1)}), bf16[16,136,128]{2,1,0:T(8,128)(2,1)S(1)}, u32[]{:S(2)}, u32[]{:S(2)}) async-start(bf16[16,136,128]{2,1,0:T(8,128)(2,1)} %get-tuple-element.55), calls=%async_computation.3 | async-start | bytes 1114112 | tf_op jit(solution)/shard_map/all_to_all | solution.py:387
  108.1 1.5 copy-start.10
  109.6 0.8 copy-start.3
  116.3 13.4 %all-to-all-start.4 = ((bf16[16,24,512]{2,1,0:T(8,128)(2,1)}), bf16[16,24,512]{2,1,0:T(8,128)(2,1)S(1)}, u32[]{:S(2)}, u32[]{:S(2)}) async-start(bf16[16,24,512]{2,1,0:T(8,128)(2,1)} %get-tuple-element.61), calls=%async_computation.4 | async-start | bytes 786432 | tf_op jit(solution)/shard_map/all_to_all | solution.py:397
  121.8 5.3 %collective-permute-start.7 = (bf16[4,128,128]{2,1,0:T(8,128)(2,1)S(1)}, bf16[4,128,128]{2,1,0:T(8,128)(2,1)S(1)}, u32[]{:S(2)}, u32[]{:S(2)}) collective-permute-start(bf16[4,128,128]{2,1,0:T(8,128)(2,1)S(1)} %get-tuple-element.82), channel_id=1, source_target_pairs={{0,96},{32,64},{64,32},{96,0},{1,97},{33,65},{65,33},{97,1},{2,98}... | collective-permute-start | bytes 393224 | tf_op jit(solution)/shard_map/ppermute | solution.py:318
  123.8 5.7 %collective-permute-start.6 = (bf16[4,128,128]{2,1,0:T(8,128)(2,1)S(1)}, bf16[4,128,128]{2,1,0:T(8,128)(2,1)S(1)}, u32[]{:S(2)}, u32[]{:S(2)}) collective-permute-start(bf16[4,128,128]{2,1,0:T(8,128)(2,1)S(1)} %get-tuple-element.83), channel_id=1, source_target_pairs={{0,64},{32,96},{64,0},{96,32},{1,65},{33,97},{65,1},{97,33},{2,66}... | collective-permute-start | bytes 393224 | tf_op jit(solution)/shard_map/ppermute | solution.py:318
  124.4 5.3 %collective-permute-start.5 = (bf16[4,128,128]{2,1,0:T(8,128)(2,1)S(1)}, bf16[4,128,128]{2,1,0:T(8,128)(2,1)S(1)}, u32[]{:S(2)}, u32[]{:S(2)}) collective-permute-start(bf16[4,128,128]{2,1,0:T(8,128)(2,1)S(1)} %get-tuple-element.84), channel_id=1, source_target_pairs={{0,32},{32,0},{64,96},{96,64},{1,33},{33,1},{65,97},{97,65},{2,34}... | collective-permute-start | bytes 393224 | tf_op jit(solution)/shard_map/ppermute | solution.py:318
  129.7 0.7 copy-start.5
  132.6 30.5 %copy-start.6 = (f32[8,128]{1,0:T(8,128)S(1)}, f32[8,128]{1,0:T(8,128)}, u32[]{:S(2)}) copy-start(f32[8,128]{1,0:T(8,128)} %get-tuple-element.81) | copy-start | bytes 12292
  132.6 30.1 %all-to-all-start.5 = ((bf16[64,16,512]{2,1,0:T(8,128)(2,1)}), bf16[64,16,512]{2,1,0:T(8,128)(2,1)S(1)}, u32[]{:S(2)}, u32[]{:S(2)}) async-start(bf16[64,16,512]{2,1,0:T(8,128)(2,1)} %get-tuple-element.64), calls=%async_computation.5 | async-start | bytes 2097152 | tf_op jit(solution)/shard_map/all_to_all | solution.py:406
  142.3 5.8 %collective-permute-start.8 = (bf16[4,128,128]{2,1,0:T(8,128)(2,1)S(1)}, bf16[4,128,128]{2,1,0:T(8,128)(2,1)S(1)}, u32[]{:S(2)}, u32[]{:S(2)}) collective-permute-start(bf16[4,128,128]{2,1,0:T(8,128)(2,1)S(1)} %pad_maximum_fusion.1), channel_id=1, source_target_pairs={{0,8},{8,0},{16,24},{24,16},{1,9},{9,1},{17,25},{25,17},{2,10},{10... | collective-permute-start | bytes 393224 | tf_op jit(solution)/shard_map/ppermute | solution.py:318
  145.4 14.3 %collective-permute-start.9 = (bf16[4,128,128]{2,1,0:T(8,128)(2,1)S(1)}, bf16[4,128,128]{2,1,0:T(8,128)(2,1)S(1)}, u32[]{:S(2)}, u32[]{:S(2)}) collective-permute-start(bf16[4,128,128]{2,1,0:T(8,128)(2,1)S(1)} %pad_maximum_fusion.2), channel_id=1, source_target_pairs={{0,16},{8,24},{16,0},{24,8},{1,17},{9,25},{17,1},{25,9},{2,18},{10... | collective-permute-start | bytes 393224 | tf_op jit(solution)/shard_map/ppermute | solution.py:318
  147.0 15.7 %collective-permute-start.10 = (bf16[4,128,128]{2,1,0:T(8,128)(2,1)S(1)}, bf16[4,128,128]{2,1,0:T(8,128)(2,1)S(1)}, u32[]{:S(2)}, u32[]{:S(2)}) collective-permute-start(bf16[4,128,128]{2,1,0:T(8,128)(2,1)S(1)} %pad_maximum_fusion.3), channel_id=1, source_target_pairs={{0,24},{8,16},{16,8},{24,0},{1,25},{9,17},{17,9},{25,1},{2,26},{10... | collective-permute-start | bytes 393224 | tf_op jit(solution)/shard_map/ppermute | solution.py:318
  148.1 15.7 %copy-start.11 = (bf16[4,128,128]{2,1,0:T(8,128)(2,1)}, bf16[4,128,128]{2,1,0:T(8,128)(2,1)S(1)}, u32[]{:S(2)}) copy-start(bf16[4,128,128]{2,1,0:T(8,128)(2,1)S(1)} %collective-permute-done.8.kv1) | copy-start | bytes 393220
  159.8 4.0 %copy-start.12 = (bf16[4,128,128]{2,1,0:T(8,128)(2,1)}, bf16[4,128,128]{2,1,0:T(8,128)(2,1)S(1)}, u32[]{:S(2)}) copy-start(bf16[4,128,128]{2,1,0:T(8,128)(2,1)S(1)} %collective-permute-done.9.kv2) | copy-start | bytes 393220
  162.7 1.1 copy-start.13
  162.7 4.7 %copy-start.1 = (bf16[64,16,512]{2,1,0:T(8,128)(2,1)}, bf16[64,16,512]{2,1,0:T(8,128)(2,1)S(1)}, u32[]{:S(2)}) copy-start(bf16[64,16,512]{2,1,0:T(8,128)(2,1)S(1)} %all-to-all-done.5.near) | copy-start | bytes 3145732
  162.7 4.7 %collective-permute-start.11 = (bf16[64,16,512]{2,1,0:T(8,128)(2,1)S(1)}, bf16[64,16,512]{2,1,0:T(8,128)(2,1)S(1)}, u32[]{:S(2)}, u32[]{:S(2)}) collective-permute-start(bf16[64,16,512]{2,1,0:T(8,128)(2,1)S(1)} %all-to-all-done.5.near), channel_id=1, source_target_pairs={{0,8},{8,0},{1,9},{9,1},{2,10},{10,2},{3,11},{11,3},{4,12},{12,4},... | collective-permute-start | bytes 3145736 | tf_op jit(solution)/shard_map/ppermute | solution.py:314
  167.4 1.0 copy-start.7

commit v4 on v3

--- a/solution.py
+++ b/solution.py
@@ -68,14 +68,8 @@
     return (h // 2) * 4 + slot * 2 + h % 2
 
 
-def project_kernel(
-    place, tok, gain, cot, neighbours, valid, wq, wk, wv, wp, kv_out, qb_out, rows_out
-):
+def key_kernel(tok, gain, wk, wv, kv_out, fac_out):
     _, _, hidden = normed_hidden(tok[...], gain[...])
-    for k in range(8):
-        lines = slice((k % 2) * BLK, (k % 2 + 1) * BLK)
-        rows_out[k, :, :D] = hidden[lines]
-        rows_out[k, :, D:] = cot[lines]
     lane = lax.broadcasted_iota(jnp.int32, (ROWS, 128), 1)
     factors = jnp.zeros((ROWS, 128), F32)
     key_f = dot_nn(hidden, wk[...])
@@ -87,6 +81,17 @@
         joined = jnp.concatenate([(part * factor).astype(BF), head(value, h)], axis=1)
         kv_out[seat(h, 0)] = joined[:BLK]
         kv_out[seat(h, 1)] = joined[BLK:]
+    fac_out[...] = factors
+
+
+def query_kernel(tok, gain, cot, neighbours, valid, factors_in, wq, wp, qb_out, rows_out):
+    _, _, hidden = normed_hidden(tok[...], gain[...])
+    for k in range(8):
+        lines = slice((k % 2) * BLK, (k % 2 + 1) * BLK)
+        rows_out[k, :, :D] = hidden[lines]
+        rows_out[k, :, D:] = cot[lines]
+    lane = lax.broadcasted_iota(jnp.int32, (ROWS, 128), 1)
+    factors = factors_in[...]
     query_f = dot_nn(hidden, wq[...])
     back = dot_nt(cot[...], wp[...]).astype(BF)
     for h in range(H):
@@ -98,10 +103,12 @@
         qb_out[seat(h, 1), :BLK] = joined[BLK:]
     ids = neighbours[...]
     keep = valid[...]
-    own_t = place[2] + lax.broadcasted_iota(jnp.int32, (2, NB), 0)
+    place_y = lax.axis_index("zl") * 2 + lax.axis_index("cr")
+    place_t = (lax.axis_index("tx") * 2 + lax.axis_index("zh")) * 2
+    own_t = place_t + lax.broadcasted_iota(jnp.int32, (2, NB), 0)
     step_t = jnp.bitwise_and(ids - own_t + 1, 15)
-    step_y = jnp.bitwise_and(jnp.right_shift(ids, 4) - place[1] + 1, 3)
-    step_x = jnp.bitwise_and(jnp.right_shift(ids, 6) - place[0] + 1, 3)
+    step_y = jnp.bitwise_and(jnp.right_shift(ids, 4) - place_y + 1, 3)
+    step_x = jnp.bitwise_and(jnp.right_shift(ids, 6) - lax.axis_index("gx") + 1, 3)
     slots = step_x * 9 + step_y * 3 + step_t
     short = lax.broadcasted_iota(jnp.int32, (2, 128), 1)
     kept = jnp.zeros((2, 128), F32)
@@ -120,14 +127,18 @@
 
 
 def attend_kernel(
-    coef, keep, own, before, after, qb, mq_out, mqt_out, own_out, before_out, after_out,
-    kvall, kvt, acc, wbuf, sems,
+    coef, own, before, after, qb, mq_out, mqt_out, own_out, before_out, after_out,
+    kvall, kvt, acc, wbuf, wbuf2, keep_rows, keep, sems,
 ):
     copies = []
     for number, src in enumerate((before, own, after)):
         copies.append(pltpu.make_async_copy(src, kvall.at[:, number], sems.at[number]))
     for copy in copies:
         copy.start()
+    for number in range(16):
+        keep_rows[number : number + 1] = qb[number, BLK:, :].astype(F32)[:1]
+    copies.append(pltpu.make_async_copy(keep_rows, keep, sems.at[3]))
+    copies[3].start()
     acc[...] = jnp.zeros_like(acc)
     for copy in copies:
         copy.wait()
@@ -144,55 +155,90 @@
     def fold(values):
         return jnp.sum(values.reshape(-1, 8, BLK), axis=0)
 
-    def one_block(number, carry):
-        x = number // 4
-        y = number % 4
+    def spread_of(number):
         both = qb[number, :BLK, :]
-        spread = jnp.concatenate([both * low, both * high], axis=0)
-        total = jnp.zeros((8, BLK), F32)
-        inner = jnp.zeros((8, BLK), F32)
-        for g in range(9):
-            dx, dy = g // 3, g % 3
-            place = (x + dx + 3) % 4 * 4 + (y + dy + 3) % 4
-            keys = kvall[place].reshape(3 * BLK, 2 * DH)
-            pair = dot_nt(keys, spread)
-            for k in range(3):
-                score = pair[k * BLK : (k + 1) * BLK, :BLK]
-                slope = pair[k * BLK : (k + 1) * BLK, BLK:]
-                weight = jnp.exp2(score * exp_coef) * keep[number * NB + g * 3 + k]
-                total = total + fold(weight)
-                inner = inner + fold(weight * slope)
-                base = (g * 3 + k) * BLK
-                wbuf[base : base + BLK, :BLK] = weight
-                wbuf[base : base + BLK, BLK:] = slope
-        total_row = jnp.sum(total, axis=0, keepdims=True)
-        inverse = 1.0 / total_row
-        inner_row = jnp.sum(inner, axis=0, keepdims=True) * inverse
-        out = jnp.zeros((2 * DH, 2 * BLK), F32)
-        for g in range(9):
-            dx, dy = g // 3, g % 3
-            place = (x + dx + 3) % 4 * 4 + (y + dy + 3) % 4
-            base = g * 3 * BLK
-            prob = wbuf[base : base + 3 * BLK, :BLK] * inverse
-            slope = wbuf[base : base + 3 * BLK, BLK:]
-            scaled = (prob * (slope - inner_row)) * grad_coef
-            mixed = jnp.concatenate([scaled.astype(BF), prob.astype(BF)], axis=1)
-            update = dot_nn(mixed, spread)
-            acc[place] += update.reshape(3, BLK, 2 * DH)
-            out = out + dot_nn(kvt[place], mixed)
+        return jnp.concatenate([both * low, both * high], axis=0)
+
+    def place_of(number, g):
+        return (number // 4 + g // 3 + 3) % 4 * 4 + (number % 4 + g % 3 + 3) % 4
+
+    def first_group(number, g, spread, sums, buffer):
+        keys = kvall[place_of(number, g)].reshape(3 * BLK, 2 * DH)
+        pair = dot_nt(keys, spread)
+        total, inner = sums
+        for k in range(3):
+            score = pair[k * BLK : (k + 1) * BLK, :BLK] * exp_coef
+            slope = pair[k * BLK : (k + 1) * BLK, BLK:]
+            weight = jnp.exp2(score)
+            slot = g * 3 + k
+            kept = keep[number, slot]
+            total = total + fold(weight) * kept
+            inner = inner + fold(weight * slope) * kept
+            base = (g * 3 + k) * BLK
+            buffer[base : base + BLK, :BLK] = score
+            buffer[base : base + BLK, BLK:] = slope
+        return total, inner
+
+    def second_group(number, g, spread, inverse, inner_row, out, heat, buffer):
+        place = place_of(number, g)
+        pieces = []
+        for k in range(3):
+            slot = g * 3 + k
+            base = slot * BLK
+            score = buffer[base : base + BLK, :BLK]
+            prob = jnp.exp2(score) * (inverse * keep[number, slot])
+            slope = buffer[base : base + BLK, BLK:]
+            grad = prob * (slope - inner_row)
+            heat = heat + fold(grad * score)
+            scaled = grad * grad_coef
+            pieces.append(jnp.concatenate([scaled.astype(BF), prob.astype(BF)], axis=1))
+        mixed = jnp.concatenate(pieces, axis=0)
+        acc[place] += dot_nn(mixed, spread).reshape(3, BLK, 2 * DH)
+        return out + dot_nn(kvt[place], mixed), heat
+
+    def close(number, out):
         extra = qb[number, BLK:, :].astype(F32)
         factor = extra[1:2] + extra[2:3]
-        query_t = both.astype(F32).T[:DH]
+        query_t = qb[number, :BLK, :].astype(F32).T[:DH]
         grad_t = out[:DH, :BLK]
         inside = jnp.sum(query_t * grad_t, axis=0, keepdims=True)
         query_d = (grad_t - query_t * (inside * (1.0 / DH))) * factor
         joined = jnp.concatenate([out[DH:, BLK:], query_d], axis=0)
         mq_out[number, :BLK, :] = joined.T.astype(BF)
         mqt_out[number] = joined.astype(BF)
-        return carry + inside
-
-    inside = lax.fori_loop(0, 16, one_block, jnp.zeros((1, BLK), F32))
-    upper, lower = high_low(jnp.broadcast_to(jnp.sum(inside, axis=1, keepdims=True), (1, BLK)))
+
+    zero = jnp.zeros((8, BLK), F32)
+
+    def step(number, following, sums, heat, buffer, other):
+        inverse = 1.0 / jnp.sum(sums[0], axis=0, keepdims=True)
+        inner_row = jnp.sum(sums[1], axis=0, keepdims=True) * inverse
+        spread = spread_of(number)
+        next_spread = spread_of(following)
+        next_sums = (zero, zero)
+        out = jnp.zeros((2 * DH, 2 * BLK), F32)
+        for g in range(9):
+            next_sums = first_group(following, g, next_spread, next_sums, other)
+            out, heat = second_group(
+                number, g, spread, inverse, inner_row, out, heat, buffer
+            )
+        close(number, out)
+        return next_sums, heat
+
+    sums = (zero, zero)
+    first_spread = spread_of(0)
+    for g in range(9):
+        sums = first_group(0, g, first_spread, sums, wbuf)
+
+    def two_blocks(index, carry):
+        sums, heat = carry
+        number = index * 2
+        sums, heat = step(number, number + 1, sums, heat, wbuf, wbuf2)
+        following = jnp.minimum(number + 2, 15)
+        return step(number + 1, following, sums, heat, wbuf2, wbuf)
+
+    _, heat = lax.fori_loop(0, 8, two_blocks, (sums, zero))
+    heat = jnp.sum(jnp.sum(heat, axis=0, keepdims=True), axis=1, keepdims=True)
+    upper, lower = high_low(jnp.broadcast_to(heat, (1, BLK)))
     tail = jnp.concatenate([upper, lower, jnp.zeros((6, BLK), F32)], axis=0).astype(BF)
     for chunk in range(16):
         mq_out[chunk, BLK:, :] = tail
@@ -201,8 +247,21 @@
     after_out[...] = acc[:, 2].astype(BF)
 
 
+def early_kernel(site, mqt, near, far, out):
+    query_part = jnp.zeros((DH, D), F32)
+    proj_part = jnp.zeros((DH, D), F32)
+    for which, source in ((site[0], near), (1 - site[0], far)):
+        for half in range(2):
+            rows = source[half * 4 : half * 4 + 4].reshape(4 * BLK, 2 * D)
+            spots = [(half * 4 + k) * 2 + which for k in range(4)]
+            mixed_t = jnp.concatenate([mqt[spot] for spot in spots], axis=1)
+            proj_part = proj_part + dot_nn(mixed_t[:DH], rows[:, D:])
+            query_part = query_part + dot_nn(mixed_t[DH:], rows[:, :D])
+    out[...] = jnp.concatenate([query_part, proj_part], axis=0).astype(BF)
+
+
 def head_kernel(
-    site, own, low, high, kv, qb, mqt, mq, near, far, kv_out, parts_out, turned,
+    site, own, low, high, kv, qb, early, mq, near, far, kv_out, parts_out, turned,
 ):
     core = site[0]
     for b in range(16):
@@ -218,18 +277,12 @@
         target_x = jnp.bitwise_xor(site[1], b // 4)
         target_y = jnp.bitwise_xor(site[2], b % 4)
         kv_out[target_x, target_y] = joined.T.astype(BF)
-    query_part = jnp.zeros((DH, D), F32)
-    proj_part = jnp.zeros((DH, D), F32)
     both_part = jnp.zeros((2 * DH, D), F32)
     for which, source in ((core, near), (1 - core, far)):
         for half in range(2):
-            rows = source[half * 4 : half * 4 + 4].reshape(4 * BLK, 2 * D)
-            hidden, cot = rows[:, :D], rows[:, D:]
+            hidden = source[half * 4 : half * 4 + 4].reshape(4 * BLK, D)
             spots = [(half * 4 + k) * 2 + which for k in range(4)]
-            mixed_t = jnp.concatenate([mqt[spot] for spot in spots], axis=1)
             both_t = jnp.concatenate([turned[spot] for spot in spots], axis=1)
-            proj_part = proj_part + dot_nn(mixed_t[:DH], cot)
-            query_part = query_part + dot_nn(mixed_t[DH:], hidden)
             both_part = both_part + dot_nn(both_t, hidden)
     lines = []
     for row in (BLK, BLK + 1):
@@ -241,7 +294,8 @@
     whole_sum = lines[0] + lines[1]
     upper, lower = high_low(whole_sum)
     extra = jnp.concatenate([upper, lower, upper, lower], axis=1).astype(BF)
-    joined = jnp.concatenate([query_part, both_part, proj_part], axis=0).astype(BF)
+    query_part, proj_part = early[:DH], early[DH:]
+    joined = jnp.concatenate([query_part, both_part.astype(BF), proj_part], axis=0)
     for g in range(16):
         parts_out[g, :16] = joined[g * 16 : (g + 1) * 16]
         parts_out[g, 16:] = extra
@@ -325,39 +379,35 @@
     cot = cotangent.reshape(ROWS, D)
     gain = norm_gain.reshape(1, D)
     core = lax.axis_index("cr")
-    place = jnp.stack(
-        [
-            lax.axis_index("gx"),
-            lax.axis_index("zl") * 2 + core,
-            (lax.axis_index("tx") * 2 + lax.axis_index("zh")) * 2,
-        ]
-    )
     any_spec = pl.BlockSpec(memory_space=pl.ANY)
     smem = pl.BlockSpec(memory_space=pltpu.SMEM)
     vmem = pl.BlockSpec(memory_space=pltpu.VMEM)
 
     pair = (16, BLK, 2 * DH)
     wide = (16, BLK + EXTRA, 2 * DH)
-    kv_send, qb_send, rows_send = pl.pallas_call(
-        project_kernel,
-        cost_estimate=cost(6),
-        out_shape=(whole(pair, BF), whole(wide, BF), whole((8, BLK, 2 * D), BF)),
-        in_specs=[smem] + [vmem] * 9,
-        out_specs=(vmem, vmem, vmem),
+    kv_send, factors = pl.pallas_call(
+        key_kernel,
+        cost_estimate=cost(3),
+        out_shape=(whole(pair, BF), whole((ROWS, 128), F32)),
+        compiler_params=params(),
+    )(tok, gain, w_key, w_value)
+    qb_send, rows_send = pl.pallas_call(
+        query_kernel,
+        cost_estimate=cost(4),
+        out_shape=(whole(wide, BF), whole((8, BLK, 2 * D), BF)),
         compiler_params=params(),
     )(
-        place, tok, gain, cot, neighbours.reshape(2, NB), valid_mask.reshape(2, NB),
-        w_query, w_key, w_value, w_proj,
+        tok, gain, cot, neighbours.reshape(2, NB), valid_mask.reshape(2, NB), factors,
+        w_query, w_proj,
     )
 
     own = lax.all_to_all(kv_send, GROUP, 0, 0, tiled=True)
+    qb_send, own = lax.optimization_barrier((qb_send, own))
     before = shift(own, 1)
     after = shift(own, -1)
-    qb_send, own = lax.optimization_barrier((qb_send, own))
     qb = lax.all_to_all(qb_send, GROUP, 0, 0, tiled=True)
     rows_send, qb, before, after = lax.optimization_barrier((rows_send, qb, before, after))
     rows_near = lax.all_to_all(rows_send, ("gx", "zl"), 0, 0, tiled=True)
-    keep = qb[:, BLK, :NB].astype(F32).reshape(16 * NB)
     head_id = lax.axis_index("gx") * 2 + core
     temp = temper[head_id] * SCALE
     coef = jnp.stack([temp * math.log2(math.e), temp])
@@ -369,31 +419,49 @@
             whole(wide, BF), whole((16, 2 * DH, BLK), BF), whole(pair, F32),
             whole(pair, BF), whole(pair, BF),
         ),
-        in_specs=[smem, smem] + [any_spec] * 3 + [vmem],
+        in_specs=[smem] + [any_spec] * 3 + [vmem],
         out_specs=tuple([vmem] * 5),
         scratch_shapes=[
             pltpu.VMEM((16, 3, BLK, 2 * DH), BF),
             pltpu.VMEM((16, 2 * DH, 3 * BLK), BF),
             pltpu.VMEM((16, 3, BLK, 2 * DH), F32),
             pltpu.VMEM((NB * BLK, 2 * BLK), F32),
-            pltpu.SemaphoreType.DMA((3,)),
+            pltpu.VMEM((NB * BLK, 2 * BLK), F32),
+            pltpu.VMEM((16, 128), F32),
+            pltpu.SMEM((16, 128), F32),
+            pltpu.SemaphoreType.DMA((4,)),
         ],
         compiler_params=params(),
-    )(coef, keep, own, before, after, qb)
+    )(coef, own, before, after, qb)
     from_after = shift(before_grad, -1)
     from_before = shift(after_grad, 1)
     rows_near, mq_send = lax.optimization_barrier((rows_near, mq_send))
     rows_far = swap_cores(rows_near)
     mq = lax.all_to_all(mq_send, GROUP, 0, 0, tiled=True)
     site = jnp.stack([core, lax.axis_index("gx"), lax.axis_index("zl") * 2 + core])
+    early = pl.pallas_call(
+        early_kernel,
+        cost_estimate=cost(3),
+        out_shape=whole((2 * DH, D), BF),
+        in_specs=[smem] + [vmem] * 3,
+        compiler_params=params(),
+    )(site, mqt, rows_near, rows_far)
+    hidden_spec = pl.BlockSpec((8, BLK, D), lambda i: (0, 0, 0))
+
+    def one_spec(array):
+        return pl.BlockSpec(array.shape, lambda i: (0,) * array.ndim)
+
     kv_back, parts = pl.pallas_call(
         head_kernel,
         cost_estimate=cost(7),
         out_shape=(whole((4, 4, BLK, 2 * DH), BF), whole((16, 24, D), BF)),
-        in_specs=[smem] + [vmem] * 9,
+        grid=(1,),
+        in_specs=[smem]
+        + [one_spec(a) for a in (own_grad, from_after, from_before, own, qb, early, mq)]
+        + [hidden_spec, hidden_spec],
         scratch_shapes=[pltpu.VMEM((16, 2 * DH, BLK), BF)],
         compiler_params=params(),
-    )(site, own_grad, from_after, from_before, own, qb, mqt, mq, rows_near, rows_far)
+    )(site, own_grad, from_after, from_before, own, qb, early, mq, rows_near, rows_far)
     arrived = lax.all_to_all(parts, RING, 0, 0, tiled=True)
     turn = [kv_back[0]] + [swap_near(kv_back[step], "gx", step) for step in range(1, 4)]
     arrived, *turn = lax.optimization_barrier((arrived, *turn))
@@ -425,7 +493,7 @@
         scratch_shapes=[pltpu.VMEM((4, D, D), BF)],
         compiler_params=params(),
     )(core.reshape(1), near, far, gain, w_query, w_key, w_value)
-    grad_temper = temper_sum[:, 0] / temper
+    grad_temper = temper_sum[:, 0] / (temper * math.log2(math.e))
     return (
         layer_out.reshape(tokens.shape),
         grad_tokens.reshape(tokens.shape),

time: 174 us -> 162 us (0.931)
  blocking collectives: 17.1 us -> 0 us
  waiting for transfers between devices: 41.8 us -> 47.1 us
  starting transfers between devices: 45.5 us -> 48.4 us
    all_to_all x1 -> x0, blocking collectives: 17.1 us -> none  [local(): own = lax.all_to_all(kv_send, GROUP, 0, 0, tiled=True)]
    all_to_all x0 -> x1, starting transfers between devices: none -> 7.34 us  [local(): own = lax.all_to_all(kv_send, GROUP, 0, 0, tiled=True)]
    pallas_call x1, Pallas kernels: 34.8 us -> 27.7 us  [local(): pl.pallas_call(attend_kernel, cost_estimate=cost(36), out_shape=(whole(wi...]
    pallas_call x1 -> x3, Pallas kernels: 6.46 us -> 12.9 us  [the longest x1 5.07 us: local(): pl.pallas_call(query_kernel, cost_estimate=cost(4), out_shape=(whole(wide...]
    all_to_all x0 -> x1, waiting for transfers between devices: none -> 4.56 us  [local(): own = lax.all_to_all(kv_send, GROUP, 0, 0, tiled=True)]
    ppermute x4, waiting for transfers between devices: 11 us -> 8.35 us  [shift(): lax.ppermute(block, RING, [(spots[t], spots[(t + step) % 16]) for t in ra...]
    all_to_all x1, waiting for transfers between devices: 0.01 us -> 2.24 us  [local(): rows_near = lax.all_to_all(rows_send, ('gx', 'zl'), 0, 0, tiled=True)]
  transfers between devices with their start and end apart: 17 -> 18, of which waited for: 9 -> 9; matrix products, arithmetic and copies ran while one was open for 2% -> 3% of each run, Pallas kernels for 22% -> 25%
where the time goes in v4:
time: 162 us; the launch traced here: 161 us
  Pallas kernels  55.9 us (35%)
  starting transfers between devices  48.4 us (30%)
  waiting for transfers between devices  47.1 us (29%)
  local copies, waits for them, and re-layouts  5.55 us (3%)
  other arithmetic  2.46 us (2%)
  between operations  2.06 us (1%)
    pallas_call x1, Pallas kernels, local(): pl.pallas_call(attend_kernel, cost_estimate=cost(36), out_shape=(whole(wi...  27.7 us
    ppermute x6, waiting for transfers between devices, swap_near(): return lax.ppermute(block, axes, [(i, i ^ step) for i in range(4)])  19.6 us
    all_to_all x1, waiting for transfers between devices, local(): qb = lax.all_to_all(qb_send, GROUP, 0, 0, tiled=True)  10.9 us
    ppermute x4, waiting for transfers between devices, shift(): lax.ppermute(block, RING, [(spots[t], spots[(t + step) % 16]) for t in ra...  8.35 us
    ppermute x6, starting transfers between devices, swap_near(): return lax.ppermute(block, axes, [(i, i ^ step) for i in range(4)])  8.28 us
    all_to_all x1, starting transfers between devices, local(): near = lax.all_to_all(share, CHIPS, 0, 0, tiled=True)  8.03 us
    all_to_all x1, starting transfers between devices, local(): own = lax.all_to_all(kv_send, GROUP, 0, 0, tiled=True)  7.34 us
    ppermute x4, starting transfers between devices, shift(): lax.ppermute(block, RING, [(spots[t], spots[(t + step) % 16]) for t in ra...  6.99 us
  transfers between devices with their start and end apart: 18, of which 9 were waited for; matrix products, arithmetic and copies ran while one was open for 3% of the time, Pallas kernels for 25%

profile of v4, /device:TPU:1, one launch (start us, length us, event | category | flops | bytes accessed | tf_op | source)
XLA Modules:
  0.0 161.5 jit_solution(2667814862201031883)
XLA Ops:
  0.6 4.0 %shard_map.161 = (bf16[16,128,128]{2,1,0:T(8,128)(2,1)}, f32[256,128]{1,0:T(8,128)}) custom-call(bf16[256,512]{1,0:T(8,128)(2,1)} %bitcast.20, f32[1,512]{1,0:T(1,128)} %bitcast.23, bf16[512,512]{1,0:T(8,128)(2,1)} %wk.5, bf16[512,512]{1,0:T(8,128)(2,1)} %wv.5), custom_call_target="tpu_custom_call" | custom-call | flops 3000000000 | bytes 3000000 | tf_op jit(solution)/shard_map/pallas_call | solution.py:388
  4.6 7.3 %all-to-all-start = ((bf16[16,128,128]{2,1,0:T(8,128)(2,1)}), bf16[16,128,128]{2,1,0:T(8,128)(2,1)S(1)}, u32[]{:S(2)}, u32[]{:S(2)}) async-start(bf16[16,128,128]{2,1,0:T(8,128)(2,1)} %get-tuple-element.49), calls=%async_computation | async-start | bytes 1048576 | tf_op jit(solution)/shard_map/all_to_all | solution.py:404
  11.9 5.1 %shard_map.162 = (bf16[16,136,128]{2,1,0:T(8,128)(2,1)}, bf16[8,128,1024]{2,1,0:T(8,128)(2,1)}) custom-call(bf16[256,512]{1,0:T(8,128)(2,1)} %bitcast.21, f32[1,512]{1,0:T(1,128)} %bitcast.24, bf16[256,512]{1,0:T(8,128)(2,1)} %bitcast.19, s32[2,27]{1,0:T(2,128)} %bitcast.27, s32[2,27]{1,0:T(2,128)} %bitcast.28, f32[256,128]{1,0:T(8,128)} %get-tuple-element.46.factors_in, ...), custom_call_target="tpu_custom_call" | custom-call | flops 4000000000 | bytes 4000000 | tf_op jit(solution)/shard_map/pallas_call | solution.py:394
  17.0 4.6 %all-to-all-done.own.kv = bf16[16,128,128]{2,1,0:T(8,128)(2,1)S(1)} async-done(((bf16[16,128,128]{2,1,0:T(8,128)(2,1)}), bf16[16,128,128]{2,1,0:T(8,128)(2,1)S(1)}, u32[]{:S(2)}, u32[]{:S(2)}) %all-to-all-start) | async-done | bytes 524320 | tf_op jit(solution)/shard_map/all_to_all | solution.py:404
  21.6 5.5 %collective-permute-start.1 = (bf16[16,128,128]{2,1,0:T(8,128)(2,1)S(1)}, bf16[16,128,128]{2,1,0:T(8,128)(2,1)S(1)}, u32[]{:S(2)}, u32[]{:S(2)}) collective-permute-start(bf16[16,128,128]{2,1,0:T(8,128)(2,1)S(1)} %all-to-all-done.own.kv), channel_id=1, source_target_pairs={{0,23},{16,0},{1,16},{17,1},{2,17},{18,2},{3,18},{19,3},{4,19},{20... | collective-permute-start | bytes 1572872 | tf_op jit(solution)/shard_map/ppermute | solution.py:364
  27.1 3.9 %all-to-all-start.1 = ((bf16[16,136,128]{2,1,0:T(8,128)(2,1)}), bf16[16,136,128]{2,1,0:T(8,128)(2,1)S(1)}, u32[]{:S(2)}, u32[]{:S(2)}) async-start(bf16[16,136,128]{2,1,0:T(8,128)(2,1)} %get-tuple-element.50), calls=%async_computation.1 | async-start | bytes 1114112 | tf_op jit(solution)/shard_map/all_to_all | solution.py:408
  31.0 0.6 dynamic_slice.3
  32.9 0.6 pad_maximum_fusion.4.coef
  33.4 10.9 %all-to-all-done.1.qb = bf16[16,136,128]{2,1,0:T(8,128)(2,1)S(1)} async-done(((bf16[16,136,128]{2,1,0:T(8,128)(2,1)}), bf16[16,136,128]{2,1,0:T(8,128)(2,1)S(1)}, u32[]{:S(2)}, u32[]{:S(2)}) %all-to-all-start.1) | async-done | bytes 557088 | tf_op jit(solution)/shard_map/all_to_all | solution.py:408
  44.3 0.0 copy-start.9
  44.3 0.8 copy-done.8
  45.1 0.2 copy-done.9
  45.3 0.1 copy-done.3
  45.4 4.0 %all-to-all-start.2 = ((bf16[8,128,1024]{2,1,0:T(8,128)(2,1)}), bf16[8,128,1024]{2,1,0:T(8,128)(2,1)S(1)}, u32[]{:S(2)}, u32[]{:S(2)}) async-start(bf16[8,128,1024]{2,1,0:T(8,128)(2,1)} %get-tuple-element.52), calls=%async_computation.2 | async-start | bytes 4194304 | tf_op jit(solution)/shard_map/all_to_all | solution.py:410
  49.5 27.7 %shard_map.163 = (bf16[16,136,128]{2,1,0:T(8,128)(2,1)}, bf16[16,128,128]{2,1,0:T(8,128)(2,1)}, f32[16,128,128]{2,1,0:T(8,128)}, bf16[16,128,128]{2,1,0:T(8,128)(2,1)}, bf16[16,128,128]{2,1,0:T(8,128)(2,1)}) custom-call(f32[2]{0:T(128)} %pad_maximum_fusion.4.coef, bf16[16,128,128]{2,1,0:T(8,128)(2,1)} %copy-done.4, bf16[16,128,128]{2,1,0:T(8,128)(2,1)} %copy-done.9, ...), custom_call_target="tpu_custom_call" | custom-call | flops 35999997952 | bytes 36000000 | tf_op jit(solution)/shard_map/pallas_call | solution.py:415
  77.2 2.2 %all-to-all-done.2.near = bf16[8,128,1024]{2,1,0:T(8,128)(2,1)S(1)} async-done(((bf16[8,128,1024]{2,1,0:T(8,128)(2,1)}), bf16[8,128,1024]{2,1,0:T(8,128)(2,1)S(1)}, u32[]{:S(2)}, u32[]{:S(2)}) %all-to-all-start.2) | async-done | bytes 2097184 | tf_op jit(solution)/shard_map/all_to_all | solution.py:410
  79.4 1.8 %collective-permute-start.4 = (bf16[8,128,1024]{2,1,0:T(8,128)(2,1)S(1)}, bf16[8,128,1024]{2,1,0:T(8,128)(2,1)}, u32[]{:S(2)}, u32[]{:S(2)}) collective-permute-start(bf16[8,128,1024]{2,1,0:T(8,128)(2,1)S(1)} %all-to-all-done.2.near), channel_id=1, source_target_pairs={{0,8},{8,0},{1,9},{9,1},{2,10},{10,2},{3,11},{11,3},{4,12},{12,4},... | collective-permute-start | bytes 6291464 | tf_op jit(solution)/shard_map/ppermute | solution.py:368
  81.2 0.3 collective-permute-start.2
  81.6 1.1 collective-permute-start.3
  82.7 3.9 %all-to-all-start.3 = ((bf16[16,136,128]{2,1,0:T(8,128)(2,1)}), bf16[16,136,128]{2,1,0:T(8,128)(2,1)S(1)}, u32[]{:S(2)}, u32[]{:S(2)}) async-start(bf16[16,136,128]{2,1,0:T(8,128)(2,1)} %get-tuple-element.57), calls=%async_computation.3 | async-start | bytes 1114112 | tf_op jit(solution)/shard_map/all_to_all | solution.py:440
  86.6 0.6 pad_add_fusion.site
  87.3 3.9 %shard_map.164.early = bf16[128,512]{1,0:T(8,128)(2,1)} custom-call(s32[3]{0:T(128)} %pad_add_fusion.site, bf16[16,128,128]{2,1,0:T(8,128)(2,1)} %get-tuple-element.61.mqt, bf16[8,128,1024]{2,1,0:T(8,128)(2,1)} %copy-done, bf16[8,128,1024]{2,1,0:T(8,128)(2,1)} %collective-permute-done.4.far), custom_call_target="tpu_custom_call" | custom-call | flops 3000000000 | bytes 3000000 | tf_op jit(solution)/shard_map/pallas_call | solution.py:442
  91.1 8.3 %collective-permute-done.2.low = bf16[16,128,128]{2,1,0:T(8,128)(2,1)S(1)} collective-permute-done((bf16[16,128,128]{2,1,0:T(8,128)(2,1)}, bf16[16,128,128]{2,1,0:T(8,128)(2,1)S(1)}, u32[]{:S(2)}, u32[]{:S(2)}) %collective-permute-start.2) | collective-permute-done | bytes 524320 | tf_op jit(solution)/shard_map/ppermute | solution.py:364
  99.5 1.6 all-to-all-done.3.mq
  101.1 0.8 copy-done.2
  101.9 4.9 %shard_map.165 = (bf16[4,4,128,128]{3,2,1,0:T(8,128)(2,1)}, bf16[16,24,512]{2,1,0:T(8,128)(2,1)}) custom-call(s32[3]{0:T(128)} %pad_add_fusion.site, f32[16,128,128]{2,1,0:T(8,128)} %get-tuple-element.58.own, bf16[16,128,128]{2,1,0:T(8,128)(2,1)} %copy-done.10, bf16[16,128,128]{2,1,0:T(8,128)(2,1)} %collective-permute-done.3.high, ...), custom_call_target="tpu_custom_call" | custom-call | flops 7000000000 | bytes 7000000 | tf_op jit(solution)/shard_map/pallas_call | solution.py:454
  106.8 3.7 %all-to-all-start.4 = ((bf16[16,24,512]{2,1,0:T(8,128)(2,1)}), bf16[16,24,512]{2,1,0:T(8,128)(2,1)S(1)}, u32[]{:S(2)}, u32[]{:S(2)}) async-start(bf16[16,24,512]{2,1,0:T(8,128)(2,1)} %get-tuple-element.63), calls=%async_computation.4 | async-start | bytes 786432 | tf_op jit(solution)/shard_map/all_to_all | solution.py:465
  110.4 1.1 slice_bitcast_fusion
  111.6 0.4 collective-permute-start.7
  112.0 0.5 collective-permute-start.6
  112.6 2.3 %collective-permute-start.5 = (bf16[4,128,128]{2,1,0:T(8,128)(2,1)S(1)}, bf16[4,128,128]{2,1,0:T(8,128)(2,1)S(1)}, u32[]{:S(2)}, u32[]{:S(2)}) collective-permute-start(bf16[4,128,128]{2,1,0:T(8,128)(2,1)S(1)} %get-tuple-element.86), channel_id=1, source_target_pairs={{0,32},{32,0},{64,96},{96,64},{1,33},{33,1},{65,97},{97,65},{2,34}... | collective-permute-start | bytes 393224 | tf_op jit(solution)/shard_map/ppermute | solution.py:372
  114.9 4.7 %collective-permute-done.7 = bf16[4,128,128]{2,1,0:T(8,128)(2,1)S(1)} collective-permute-done((bf16[4,128,128]{2,1,0:T(8,128)(2,1)S(1)}, bf16[4,128,128]{2,1,0:T(8,128)(2,1)S(1)}, u32[]{:S(2)}, u32[]{:S(2)}) %collective-permute-start.7) | collective-permute-done | bytes 131104 | tf_op jit(solution)/shard_map/ppermute | solution.py:372
  119.6 0.2 collective-permute-done.5
  119.8 0.7 copy-done.5
  120.6 2.1 %shard_map.166 = (bf16[64,16,512]{2,1,0:T(8,128)(2,1)}, f32[8,128]{1,0:T(8,128)}) custom-call(bf16[16,24,512]{2,1,0:T(8,128)(2,1)} %copy-done.5), custom_call_target="tpu_custom_call" | custom-call | flops 2000000000 | bytes 2000000 | tf_op jit(solution)/shard_map/pallas_call | solution.py:468
  122.7 8.0 %all-to-all-start.5 = ((bf16[64,16,512]{2,1,0:T(8,128)(2,1)}), bf16[64,16,512]{2,1,0:T(8,128)(2,1)S(1)}, u32[]{:S(2)}, u32[]{:S(2)}) async-start(bf16[64,16,512]{2,1,0:T(8,128)(2,1)} %get-tuple-element.66), calls=%async_computation.5 | async-start | bytes 2097152 | tf_op jit(solution)/shard_map/all_to_all | solution.py:474
  130.8 3.1 %collective-permute-start.8 = (bf16[4,128,128]{2,1,0:T(8,128)(2,1)S(1)}, bf16[4,128,128]{2,1,0:T(8,128)(2,1)S(1)}, u32[]{:S(2)}, u32[]{:S(2)}) collective-permute-start(bf16[4,128,128]{2,1,0:T(8,128)(2,1)S(1)} %pad_maximum_fusion.1), channel_id=1, source_target_pairs={{0,8},{8,0},{16,24},{24,16},{1,9},{9,1},{17,25},{25,17},{2,10},{10... | collective-permute-start | bytes 393224 | tf_op jit(solution)/shard_map/ppermute | solution.py:372
  134.0 1.4 collective-permute-start.9
  135.4 0.4 collective-permute-start.10
  135.8 0.7 pad_maximum_fusion.kv0
  136.5 11.7 %collective-permute-done.9.kv2 = bf16[4,128,128]{2,1,0:T(8,128)(2,1)S(1)} collective-permute-done((bf16[4,128,128]{2,1,0:T(8,128)(2,1)S(1)}, bf16[4,128,128]{2,1,0:T(8,128)(2,1)S(1)}, u32[]{:S(2)}, u32[]{:S(2)}) %collective-permute-start.9) | collective-permute-done | bytes 131104 | tf_op jit(solution)/shard_map/ppermute | solution.py:372
  148.2 3.0 %collective-permute-done.10.kv3 = bf16[4,128,128]{2,1,0:T(8,128)(2,1)S(1)} collective-permute-done((bf16[4,128,128]{2,1,0:T(8,128)(2,1)S(1)}, bf16[4,128,128]{2,1,0:T(8,128)(2,1)S(1)}, u32[]{:S(2)}, u32[]{:S(2)}) %collective-permute-start.10) | collective-permute-done | bytes 131104 | tf_op jit(solution)/shard_map/ppermute | solution.py:372
  151.1 0.4 collective-permute-start.11
  151.6 0.1 slice_reduce_fusion
  151.7 0.5 multiply_divide_fusion
  152.2 3.6 %shard_map.167 = (bf16[256,512]{1,0:T(8,128)(2,1)}, f32[256,512]{1,0:T(8,128)}) custom-call(s32[3]{0:T(128)} %pad_add_fusion.site, bf16[256,512]{1,0:T(8,128)(2,1)} %bitcast.22, f32[1,512]{1,0:T(1,128)} %bitcast.25, bf16[16,136,128]{2,1,0:T(8,128)(2,1)} %copy-done.2, bf16[4,128,128]{2,1,0:T(8,128)(2,1)} %pad_maximum_fusion.kv0, ...), custom_call_target="tpu_custom_call" | custom-call | flops 4000000000 | bytes 4000000 | tf_op jit(solution)/shard_map/pallas_call | solution.py:478
  155.9 1.0 copy-done.7
  156.9 4.6 %shard_map.168 = (f32[512,512]{1,0:T(8,128)}, f32[512,512]{1,0:T(8,128)}, f32[512,512]{1,0:T(8,128)}, f32[512,512]{1,0:T(8,128)}, f32[1,512]{1,0:T(1,128)}) custom-call(s32[1]{0:T(128)} %bitcast.core, bf16[64,16,512]{2,1,0:T(8,128)(2,1)} %copy-done.1, bf16[64,16,512]{2,1,0:T(8,128)(2,1)} %copy-done.7, f32[1,512]{1,0:T(1,128)} %bitcast.26, ...), custom_call_target="tpu_custom_call" | custom-call | flops 5000000000 | bytes 5000000 | tf_op jit(solution)/shard_map/pallas_call | solution.py:488
  (38 shorter events, 0.2 us)
Async XLA Ops:
  4.6 17.0 %all-to-all-start = ((bf16[16,128,128]{2,1,0:T(8,128)(2,1)}), bf16[16,128,128]{2,1,0:T(8,128)(2,1)S(1)}, u32[]{:S(2)}, u32[]{:S(2)}) async-start(bf16[16,128,128]{2,1,0:T(8,128)(2,1)} %get-tuple-element.49), calls=%async_computation | async-start | bytes 1048576 | tf_op jit(solution)/shard_map/all_to_all | solution.py:404
  11.9 19.0 %copy-start.14 = (f32[8]{0:T(128)S(1)}, f32[8]{0:T(128)}, u32[]{:S(2)}) copy-start(f32[8]{0:T(128)} %param.16) | copy-start | bytes 100
  21.6 23.7 %copy-start.4 = (bf16[16,128,128]{2,1,0:T(8,128)(2,1)}, bf16[16,128,128]{2,1,0:T(8,128)(2,1)S(1)}, u32[]{:S(2)}) copy-start(bf16[16,128,128]{2,1,0:T(8,128)(2,1)S(1)} %all-to-all-done.own.kv) | copy-start | bytes 1572868
  21.6 22.7 %collective-permute-start.1 = (bf16[16,128,128]{2,1,0:T(8,128)(2,1)S(1)}, bf16[16,128,128]{2,1,0:T(8,128)(2,1)S(1)}, u32[]{:S(2)}, u32[]{:S(2)}) collective-permute-start(bf16[16,128,128]{2,1,0:T(8,128)(2,1)S(1)} %all-to-all-done.own.kv), channel_id=1, source_target_pairs={{0,23},{16,0},{1,16},{17,1},{2,17},{18,2},{3,18},{19,3},{4,19},{20... | collective-permute-start | bytes 1572872 | tf_op jit(solution)/shard_map/ppermute | solution.py:364
  27.1 17.2 %collective-permute-start = (bf16[16,128,128]{2,1,0:T(8,128)(2,1)S(1)}, bf16[16,128,128]{2,1,0:T(8,128)(2,1)S(1)}, u32[]{:S(2)}, u32[]{:S(2)}) collective-permute-start(bf16[16,128,128]{2,1,0:T(8,128)(2,1)S(1)} %all-to-all-done.own.kv), channel_id=1, source_target_pairs={{0,16},{16,1},{1,17},{17,2},{2,18},{18,3},{3,19},{19,4},{4,20},{20... | collective-permute-start | bytes 1572872 | tf_op jit(solution)/shard_map/ppermute | solution.py:364
  27.1 17.2 %all-to-all-start.1 = ((bf16[16,136,128]{2,1,0:T(8,128)(2,1)}), bf16[16,136,128]{2,1,0:T(8,128)(2,1)S(1)}, u32[]{:S(2)}, u32[]{:S(2)}) async-start(bf16[16,136,128]{2,1,0:T(8,128)(2,1)} %get-tuple-element.50), calls=%async_computation.1 | async-start | bytes 1114112 | tf_op jit(solution)/shard_map/all_to_all | solution.py:408
  44.3 1.1 copy-start.3
  44.3 0.8 copy-start.8
  44.3 1.0 copy-start.9
  45.4 34.0 %all-to-all-start.2 = ((bf16[8,128,1024]{2,1,0:T(8,128)(2,1)}), bf16[8,128,1024]{2,1,0:T(8,128)(2,1)S(1)}, u32[]{:S(2)}, u32[]{:S(2)}) async-start(bf16[8,128,1024]{2,1,0:T(8,128)(2,1)} %get-tuple-element.52), calls=%async_computation.2 | async-start | bytes 4194304 | tf_op jit(solution)/shard_map/all_to_all | solution.py:410
  79.4 7.8 %copy-start = (bf16[8,128,1024]{2,1,0:T(8,128)(2,1)}, bf16[8,128,1024]{2,1,0:T(8,128)(2,1)S(1)}, u32[]{:S(2)}) copy-start(bf16[8,128,1024]{2,1,0:T(8,128)(2,1)S(1)} %all-to-all-done.2.near) | copy-start | bytes 6291460
  79.4 7.8 %collective-permute-start.4 = (bf16[8,128,1024]{2,1,0:T(8,128)(2,1)S(1)}, bf16[8,128,1024]{2,1,0:T(8,128)(2,1)}, u32[]{:S(2)}, u32[]{:S(2)}) collective-permute-start(bf16[8,128,1024]{2,1,0:T(8,128)(2,1)S(1)} %all-to-all-done.2.near), channel_id=1, source_target_pairs={{0,8},{8,0},{1,9},{9,1},{2,10},{10,2},{3,11},{11,3},{4,12},{12,4},... | collective-permute-start | bytes 6291464 | tf_op jit(solution)/shard_map/ppermute | solution.py:368
  81.2 18.2 %collective-permute-start.2 = (bf16[16,128,128]{2,1,0:T(8,128)(2,1)}, bf16[16,128,128]{2,1,0:T(8,128)(2,1)S(1)}, u32[]{:S(2)}, u32[]{:S(2)}) collective-permute-start(bf16[16,128,128]{2,1,0:T(8,128)(2,1)} %get-tuple-element.59), channel_id=1, source_target_pairs={{0,23},{16,0},{1,16},{17,1},{2,17},{18,2},{3,18},{19,3},{4,19},{20... | collective-permute-start | bytes 1572872 | tf_op jit(solution)/shard_map/ppermute | solution.py:364
  81.6 17.9 %collective-permute-start.3 = (bf16[16,128,128]{2,1,0:T(8,128)(2,1)}, bf16[16,128,128]{2,1,0:T(8,128)(2,1)}, u32[]{:S(2)}, u32[]{:S(2)}) collective-permute-start(bf16[16,128,128]{2,1,0:T(8,128)(2,1)} %get-tuple-element.60), channel_id=1, source_target_pairs={{0,16},{16,1},{1,17},{17,2},{2,18},{18,3},{3,19},{19,4},{4,20},{20... | collective-permute-start | bytes 1572872 | tf_op jit(solution)/shard_map/ppermute | solution.py:364
  82.7 18.4 %all-to-all-start.3 = ((bf16[16,136,128]{2,1,0:T(8,128)(2,1)}), bf16[16,136,128]{2,1,0:T(8,128)(2,1)S(1)}, u32[]{:S(2)}, u32[]{:S(2)}) async-start(bf16[16,136,128]{2,1,0:T(8,128)(2,1)} %get-tuple-element.57), calls=%async_computation.3 | async-start | bytes 1114112 | tf_op jit(solution)/shard_map/all_to_all | solution.py:440
  99.5 1.6 copy-start.10
  101.1 0.8 copy-start.2
  106.8 13.0 %all-to-all-start.4 = ((bf16[16,24,512]{2,1,0:T(8,128)(2,1)}), bf16[16,24,512]{2,1,0:T(8,128)(2,1)S(1)}, u32[]{:S(2)}, u32[]{:S(2)}) async-start(bf16[16,24,512]{2,1,0:T(8,128)(2,1)} %get-tuple-element.63), calls=%async_computation.4 | async-start | bytes 786432 | tf_op jit(solution)/shard_map/all_to_all | solution.py:465
  111.6 8.0 %collective-permute-start.7 = (bf16[4,128,128]{2,1,0:T(8,128)(2,1)S(1)}, bf16[4,128,128]{2,1,0:T(8,128)(2,1)S(1)}, u32[]{:S(2)}, u32[]{:S(2)}) collective-permute-start(bf16[4,128,128]{2,1,0:T(8,128)(2,1)S(1)} %get-tuple-element.84), channel_id=1, source_target_pairs={{0,96},{32,64},{64,32},{96,0},{1,97},{33,65},{65,33},{97,1},{2,98}... | collective-permute-start | bytes 393224 | tf_op jit(solution)/shard_map/ppermute | solution.py:372
  112.0 7.6 %collective-permute-start.6 = (bf16[4,128,128]{2,1,0:T(8,128)(2,1)S(1)}, bf16[4,128,128]{2,1,0:T(8,128)(2,1)S(1)}, u32[]{:S(2)}, u32[]{:S(2)}) collective-permute-start(bf16[4,128,128]{2,1,0:T(8,128)(2,1)S(1)} %get-tuple-element.85), channel_id=1, source_target_pairs={{0,64},{32,96},{64,0},{96,32},{1,65},{33,97},{65,1},{97,33},{2,66}... | collective-permute-start | bytes 393224 | tf_op jit(solution)/shard_map/ppermute | solution.py:372
  112.6 7.2 %collective-permute-start.5 = (bf16[4,128,128]{2,1,0:T(8,128)(2,1)S(1)}, bf16[4,128,128]{2,1,0:T(8,128)(2,1)S(1)}, u32[]{:S(2)}, u32[]{:S(2)}) collective-permute-start(bf16[4,128,128]{2,1,0:T(8,128)(2,1)S(1)} %get-tuple-element.86), channel_id=1, source_target_pairs={{0,32},{32,0},{64,96},{96,64},{1,33},{33,1},{65,97},{97,65},{2,34}... | collective-permute-start | bytes 393224 | tf_op jit(solution)/shard_map/ppermute | solution.py:372
  119.8 0.7 copy-start.5
  122.7 28.9 %copy-start.6 = (f32[8,128]{1,0:T(8,128)S(1)}, f32[8,128]{1,0:T(8,128)}, u32[]{:S(2)}) copy-start(f32[8,128]{1,0:T(8,128)} %get-tuple-element.83) | copy-start | bytes 12292
  122.7 28.5 %all-to-all-start.5 = ((bf16[64,16,512]{2,1,0:T(8,128)(2,1)}), bf16[64,16,512]{2,1,0:T(8,128)(2,1)S(1)}, u32[]{:S(2)}, u32[]{:S(2)}) async-start(bf16[64,16,512]{2,1,0:T(8,128)(2,1)} %get-tuple-element.66), calls=%async_computation.5 | async-start | bytes 2097152 | tf_op jit(solution)/shard_map/all_to_all | solution.py:474
  130.8 5.7 %collective-permute-start.8 = (bf16[4,128,128]{2,1,0:T(8,128)(2,1)S(1)}, bf16[4,128,128]{2,1,0:T(8,128)(2,1)S(1)}, u32[]{:S(2)}, u32[]{:S(2)}) collective-permute-start(bf16[4,128,128]{2,1,0:T(8,128)(2,1)S(1)} %pad_maximum_fusion.1), channel_id=1, source_target_pairs={{0,8},{8,0},{16,24},{24,16},{1,9},{9,1},{17,25},{25,17},{2,10},{10... | collective-permute-start | bytes 393224 | tf_op jit(solution)/shard_map/ppermute | solution.py:372
  134.0 14.2 %collective-permute-start.9 = (bf16[4,128,128]{2,1,0:T(8,128)(2,1)S(1)}, bf16[4,128,128]{2,1,0:T(8,128)(2,1)S(1)}, u32[]{:S(2)}, u32[]{:S(2)}) collective-permute-start(bf16[4,128,128]{2,1,0:T(8,128)(2,1)S(1)} %pad_maximum_fusion.2), channel_id=1, source_target_pairs={{0,16},{8,24},{16,0},{24,8},{1,17},{9,25},{17,1},{25,9},{2,18},{10... | collective-permute-start | bytes 393224 | tf_op jit(solution)/shard_map/ppermute | solution.py:372
  135.4 15.8 %collective-permute-start.10 = (bf16[4,128,128]{2,1,0:T(8,128)(2,1)S(1)}, bf16[4,128,128]{2,1,0:T(8,128)(2,1)S(1)}, u32[]{:S(2)}, u32[]{:S(2)}) collective-permute-start(bf16[4,128,128]{2,1,0:T(8,128)(2,1)S(1)} %pad_maximum_fusion.3), channel_id=1, source_target_pairs={{0,24},{8,16},{16,8},{24,0},{1,25},{9,17},{17,9},{25,1},{2,26},{10... | collective-permute-start | bytes 393224 | tf_op jit(solution)/shard_map/ppermute | solution.py:372
  136.5 15.8 %copy-start.11 = (bf16[4,128,128]{2,1,0:T(8,128)(2,1)}, bf16[4,128,128]{2,1,0:T(8,128)(2,1)S(1)}, u32[]{:S(2)}) copy-start(bf16[4,128,128]{2,1,0:T(8,128)(2,1)S(1)} %collective-permute-done.8.kv1) | copy-start | bytes 393220
  148.2 4.0 %copy-start.12 = (bf16[4,128,128]{2,1,0:T(8,128)(2,1)}, bf16[4,128,128]{2,1,0:T(8,128)(2,1)S(1)}, u32[]{:S(2)}) copy-start(bf16[4,128,128]{2,1,0:T(8,128)(2,1)S(1)} %collective-permute-done.9.kv2) | copy-start | bytes 393220
  151.1 1.1 copy-start.13
  151.1 4.7 %copy-start.1 = (bf16[64,16,512]{2,1,0:T(8,128)(2,1)}, bf16[64,16,512]{2,1,0:T(8,128)(2,1)S(1)}, u32[]{:S(2)}) copy-start(bf16[64,16,512]{2,1,0:T(8,128)(2,1)S(1)} %all-to-all-done.5.near) | copy-start | bytes 3145732
  151.1 4.7 %collective-permute-start.11 = (bf16[64,16,512]{2,1,0:T(8,128)(2,1)S(1)}, bf16[64,16,512]{2,1,0:T(8,128)(2,1)S(1)}, u32[]{:S(2)}, u32[]{:S(2)}) collective-permute-start(bf16[64,16,512]{2,1,0:T(8,128)(2,1)S(1)} %all-to-all-done.5.near), channel_id=1, source_target_pairs={{0,8},{8,0},{1,9},{9,1},{2,10},{10,2},{3,11},{11,3},{4,12},{12,4},... | collective-permute-start | bytes 3145736 | tf_op jit(solution)/shard_map/ppermute | solution.py:368
  155.9 1.0 copy-start.7

commit v5 on v4

--- a/solution.py
+++ b/solution.py
@@ -23,11 +23,11 @@
 CHIPS = ("gx", "zl", "tx", "zh")
 ALL = ("gx", "zl", "cr", "tx", "zh")
 EXTRA = 8
-VMEM_LIMIT = 56 * 1024 * 1024
-
-
-def params():
-    return pltpu.CompilerParams(vmem_limit_bytes=VMEM_LIMIT)
+MIB = 1024 * 1024
+
+
+def params(mebibytes):
+    return pltpu.CompilerParams(vmem_limit_bytes=mebibytes * MIB)
 
 
 def cost(micros):
@@ -127,8 +127,8 @@
 
 
 def attend_kernel(
-    coef, own, before, after, qb, mq_out, mqt_out, own_out, before_out, after_out,
-    kvall, kvt, acc, wbuf, wbuf2, keep_rows, keep, sems,
+    coef, own, before, after, qb, mq_hbm, mqt_hbm, own_hbm, before_hbm, after_hbm,
+    mq_out, mqt_out, before_out, after_out, kvall, kvt, acc, wbuf, wbuf2, keep_rows, keep, sems,
 ):
     copies = []
     for number, src in enumerate((before, own, after)):
@@ -179,7 +179,7 @@
             buffer[base : base + BLK, BLK:] = slope
         return total, inner
 
-    def second_group(number, g, spread, inverse, inner_row, out, heat, buffer):
+    def second_group(number, g, spread, inverse, inner_row, heat, buffer):
         place = place_of(number, g)
         pieces = []
         for k in range(3):
@@ -194,7 +194,7 @@
             pieces.append(jnp.concatenate([scaled.astype(BF), prob.astype(BF)], axis=1))
         mixed = jnp.concatenate(pieces, axis=0)
         acc[place] += dot_nn(mixed, spread).reshape(3, BLK, 2 * DH)
-        return out + dot_nn(kvt[place], mixed), heat
+        return kvt[place], mixed, heat
 
     def close(number, out):
         extra = qb[number, BLK:, :].astype(F32)
@@ -218,9 +218,16 @@
         out = jnp.zeros((2 * DH, 2 * BLK), F32)
         for g in range(9):
             next_sums = first_group(following, g, next_spread, next_sums, other)
-            out, heat = second_group(
-                number, g, spread, inverse, inner_row, out, heat, buffer
+            turned, mixed, heat = second_group(
+                number, g, spread, inverse, inner_row, heat, buffer
             )
+            if g % 2 == 0 and g < 8:
+                waiting = turned, mixed
+                continue
+            if g % 2 == 1:
+                turned = jnp.concatenate([waiting[0], turned], axis=1)
+                mixed = jnp.concatenate([waiting[1], mixed], axis=0)
+            out = out + dot_nn(turned, mixed)
         close(number, out)
         return next_sums, heat
 
@@ -242,9 +249,22 @@
     tail = jnp.concatenate([upper, lower, jnp.zeros((6, BLK), F32)], axis=0).astype(BF)
     for chunk in range(16):
         mq_out[chunk, BLK:, :] = tail
-    own_out[...] = acc[:, 1]
+    leaving = [
+        pltpu.make_async_copy(source, target, sems.at[4 + number])
+        for number, (source, target) in enumerate(
+            (
+                (before_out, before_hbm), (after_out, after_hbm), (mq_out, mq_hbm),
+                (mqt_out, mqt_hbm), (acc.at[:, 1], own_hbm),
+            )
+        )
+    ]
     before_out[...] = acc[:, 0].astype(BF)
+    leaving[0].start()
     after_out[...] = acc[:, 2].astype(BF)
+    for copy in leaving[1:]:
+        copy.start()
+    for copy in leaving:
+        copy.wait()
 
 
 def early_kernel(site, mqt, near, far, out):
@@ -381,6 +401,7 @@
     core = lax.axis_index("cr")
     any_spec = pl.BlockSpec(memory_space=pl.ANY)
     smem = pl.BlockSpec(memory_space=pltpu.SMEM)
+    hbm = pl.BlockSpec(memory_space=pltpu.HBM)
     vmem = pl.BlockSpec(memory_space=pltpu.VMEM)
 
     pair = (16, BLK, 2 * DH)
@@ -389,13 +410,13 @@
         key_kernel,
         cost_estimate=cost(3),
         out_shape=(whole(pair, BF), whole((ROWS, 128), F32)),
-        compiler_params=params(),
+        compiler_params=params(56),
     )(tok, gain, w_key, w_value)
     qb_send, rows_send = pl.pallas_call(
         query_kernel,
         cost_estimate=cost(4),
         out_shape=(whole(wide, BF), whole((8, BLK, 2 * D), BF)),
-        compiler_params=params(),
+        compiler_params=params(56),
     )(
         tok, gain, cot, neighbours.reshape(2, NB), valid_mask.reshape(2, NB), factors,
         w_query, w_proj,
@@ -420,8 +441,12 @@
             whole(pair, BF), whole(pair, BF),
         ),
         in_specs=[smem] + [any_spec] * 3 + [vmem],
-        out_specs=tuple([vmem] * 5),
+        out_specs=tuple([hbm] * 5),
         scratch_shapes=[
+            pltpu.VMEM(wide, BF),
+            pltpu.VMEM((16, 2 * DH, BLK), BF),
+            pltpu.VMEM(pair, BF),
+            pltpu.VMEM(pair, BF),
             pltpu.VMEM((16, 3, BLK, 2 * DH), BF),
             pltpu.VMEM((16, 2 * DH, 3 * BLK), BF),
             pltpu.VMEM((16, 3, BLK, 2 * DH), F32),
@@ -429,9 +454,9 @@
             pltpu.VMEM((NB * BLK, 2 * BLK), F32),
             pltpu.VMEM((16, 128), F32),
             pltpu.SMEM((16, 128), F32),
-            pltpu.SemaphoreType.DMA((4,)),
+            pltpu.SemaphoreType.DMA((9,)),
         ],
-        compiler_params=params(),
+        compiler_params=params(56),
     )(coef, own, before, after, qb)
     from_after = shift(before_grad, -1)
     from_before = shift(after_grad, 1)
@@ -444,7 +469,7 @@
         cost_estimate=cost(3),
         out_shape=whole((2 * DH, D), BF),
         in_specs=[smem] + [vmem] * 3,
-        compiler_params=params(),
+        compiler_params=params(10),
     )(site, mqt, rows_near, rows_far)
     hidden_spec = pl.BlockSpec((8, BLK, D), lambda i: (0, 0, 0))
 
@@ -460,7 +485,7 @@
         + [one_spec(a) for a in (own_grad, from_after, from_before, own, qb, early, mq)]
         + [hidden_spec, hidden_spec],
         scratch_shapes=[pltpu.VMEM((16, 2 * DH, BLK), BF)],
-        compiler_params=params(),
+        compiler_params=params(56),
     )(site, own_grad, from_after, from_before, own, qb, early, mq, rows_near, rows_far)
     arrived = lax.all_to_all(parts, RING, 0, 0, tiled=True)
     turn = [kv_back[0]] + [swap_near(kv_back[step], "gx", step) for step in range(1, 4)]
@@ -469,7 +494,7 @@
         sum_kernel,
         cost_estimate=cost(2),
         out_shape=(whole((64, 16, D), BF), whole((H, 128), F32)),
-        compiler_params=params(),
+        compiler_params=params(6),
     )(arrived)
     near = lax.all_to_all(share, CHIPS, 0, 0, tiled=True)
     kv = [jnp.stack([piece[step] for piece in turn]) for step in range(4)]
@@ -481,7 +506,7 @@
         out_shape=(whole((ROWS, D), BF), whole((ROWS, D), F32)),
         in_specs=[smem] + [vmem] * 11,
         scratch_shapes=[pltpu.VMEM(pair, BF)],
-        compiler_params=params(),
+        compiler_params=params(56),
     )(site, tok, gain, mq, *kv, w_query, w_key, w_value, w_proj)
     far = swap_cores(near)
     square = whole((D, D), F32)
@@ -491,7 +516,7 @@
         out_shape=(square, square, square, square, whole((1, D), F32)),
         in_specs=[smem] + [vmem] * 6,
         scratch_shapes=[pltpu.VMEM((4, D, D), BF)],
-        compiler_params=params(),
+        compiler_params=params(16),
     )(core.reshape(1), near, far, gain, w_query, w_key, w_value)
     grad_temper = temper_sum[:, 0] / (temper * math.log2(math.e))
     return (

time: 162 us -> 158 us (0.975)
  Pallas kernels: 55.9 us -> 50.9 us
  waiting for transfers between devices: 47.1 us -> 49.4 us
    pallas_call x1, Pallas kernels: 4.63 us -> 2.79 us  [local(): pl.pallas_call(output_kernel, cost_estimate=cost(5), out_shape=(square, s...]
    unnamed x30 -> x36, local copies, waits for them, and re-layouts: 3.68 us -> 3.67 us
  transfers between devices with their start and end apart: 18 -> 18, of which waited for: 9 -> 8; matrix products, arithmetic and copies ran while one was open for 3% -> 2% of each run, Pallas kernels for 25% -> 24%
where the time goes in v5:
time: 158 us; the launch traced here: 157 us
  Pallas kernels  50.9 us (32%)
  waiting for transfers between devices  49.4 us (31%)
  starting transfers between devices  47.4 us (30%)
  local copies, waits for them, and re-layouts  5.55 us (4%)
  between operations  2.14 us (1%)
  other arithmetic  1.92 us (1%)
    pallas_call x1, Pallas kernels, local(): pl.pallas_call(attend_kernel, cost_estimate=cost(36), out_shape=(whole(wi...  26.9 us
    ppermute x6, waiting for transfers between devices, swap_near(): return lax.ppermute(block, axes, [(i, i ^ step) for i in range(4)])  20.7 us
    all_to_all x1, waiting for transfers between devices, local(): qb = lax.all_to_all(qb_send, GROUP, 0, 0, tiled=True)  10.9 us
    ppermute x4, waiting for transfers between devices, shift(): lax.ppermute(block, RING, [(spots[t], spots[(t + step) % 16]) for t in ra...  8.61 us
    ppermute x6, starting transfers between devices, swap_near(): return lax.ppermute(block, axes, [(i, i ^ step) for i in range(4)])  7.87 us
    all_to_all x1, starting transfers between devices, local(): near = lax.all_to_all(share, CHIPS, 0, 0, tiled=True)  7.46 us
    all_to_all x1, starting transfers between devices, local(): own = lax.all_to_all(kv_send, GROUP, 0, 0, tiled=True)  7.34 us
    ppermute x4, starting transfers between devices, shift(): lax.ppermute(block, RING, [(spots[t], spots[(t + step) % 16]) for t in ra...  6.99 us
  transfers between devices with their start and end apart: 18, of which 8 were waited for; matrix products, arithmetic and copies ran while one was open for 2% of the time, Pallas kernels for 24%

profile of v5, /device:TPU:1, one launch (start us, length us, event | category | flops | bytes accessed | tf_op | source)
XLA Modules:
  0.0 157.3 jit_solution(3193075806940178490)
XLA Ops:
  0.6 4.0 %shard_map.161 = (bf16[16,128,128]{2,1,0:T(8,128)(2,1)}, f32[256,128]{1,0:T(8,128)}) custom-call(bf16[256,512]{1,0:T(8,128)(2,1)} %bitcast.24, f32[1,512]{1,0:T(1,128)} %bitcast.19, bf16[512,512]{1,0:T(8,128)(2,1)} %wk.5, bf16[512,512]{1,0:T(8,128)(2,1)} %wv.5), custom_call_target="tpu_custom_call" | custom-call | flops 3000000000 | bytes 3000000 | tf_op jit(solution)/shard_map/pallas_call | solution.py:409
  4.6 7.3 %all-to-all-start = ((bf16[16,128,128]{2,1,0:T(8,128)(2,1)}), bf16[16,128,128]{2,1,0:T(8,128)(2,1)S(1)}, u32[]{:S(2)}, u32[]{:S(2)}) async-start(bf16[16,128,128]{2,1,0:T(8,128)(2,1)} %get-tuple-element.49), calls=%async_computation | async-start | bytes 1048576 | tf_op jit(solution)/shard_map/all_to_all | solution.py:425
  11.9 5.1 %shard_map.162 = (bf16[16,136,128]{2,1,0:T(8,128)(2,1)}, bf16[8,128,1024]{2,1,0:T(8,128)(2,1)}) custom-call(bf16[256,512]{1,0:T(8,128)(2,1)} %bitcast.25, f32[1,512]{1,0:T(1,128)} %bitcast.20, bf16[256,512]{1,0:T(8,128)(2,1)} %bitcast.23, s32[2,27]{1,0:T(2,128)} %bitcast.27, s32[2,27]{1,0:T(2,128)} %bitcast.28, f32[256,128]{1,0:T(8,128)} %get-tuple-element.46.factors_in, ...), custom_call_target="tpu_custom_call" | custom-call | flops 4000000000 | bytes 4000000 | tf_op jit(solution)/shard_map/pallas_call | solution.py:415
  17.0 4.6 %all-to-all-done.own.kv = bf16[16,128,128]{2,1,0:T(8,128)(2,1)S(1)} async-done(((bf16[16,128,128]{2,1,0:T(8,128)(2,1)}), bf16[16,128,128]{2,1,0:T(8,128)(2,1)S(1)}, u32[]{:S(2)}, u32[]{:S(2)}) %all-to-all-start) | async-done | bytes 524320 | tf_op jit(solution)/shard_map/all_to_all | solution.py:425
  21.6 5.5 %collective-permute-start.1 = (bf16[16,128,128]{2,1,0:T(8,128)(2,1)S(1)}, bf16[16,128,128]{2,1,0:T(8,128)(2,1)S(1)}, u32[]{:S(2)}, u32[]{:S(2)}) collective-permute-start(bf16[16,128,128]{2,1,0:T(8,128)(2,1)S(1)} %all-to-all-done.own.kv), channel_id=1, source_target_pairs={{0,23},{16,0},{1,16},{17,1},{2,17},{18,2},{3,18},{19,3},{4,19},{20... | collective-permute-start | bytes 1572872 | tf_op jit(solution)/shard_map/ppermute | solution.py:384
  27.1 3.9 %all-to-all-start.1 = ((bf16[16,136,128]{2,1,0:T(8,128)(2,1)}), bf16[16,136,128]{2,1,0:T(8,128)(2,1)S(1)}, u32[]{:S(2)}, u32[]{:S(2)}) async-start(bf16[16,136,128]{2,1,0:T(8,128)(2,1)} %get-tuple-element.50), calls=%async_computation.1 | async-start | bytes 1114112 | tf_op jit(solution)/shard_map/all_to_all | solution.py:429
  31.0 0.6 dynamic_slice.3
  32.9 0.6 pad_maximum_fusion.4.coef
  33.4 10.9 %all-to-all-done.1.qb = bf16[16,136,128]{2,1,0:T(8,128)(2,1)S(1)} async-done(((bf16[16,136,128]{2,1,0:T(8,128)(2,1)}), bf16[16,136,128]{2,1,0:T(8,128)(2,1)S(1)}, u32[]{:S(2)}, u32[]{:S(2)}) %all-to-all-start.1) | async-done | bytes 557088 | tf_op jit(solution)/shard_map/all_to_all | solution.py:429
  44.3 0.0 copy-start.12
  44.3 0.8 copy-done.11
  45.1 0.2 copy-done.12
  45.3 0.1 copy-done.9
  45.4 4.0 %all-to-all-start.2 = ((bf16[8,128,1024]{2,1,0:T(8,128)(2,1)}), bf16[8,128,1024]{2,1,0:T(8,128)(2,1)S(1)}, u32[]{:S(2)}, u32[]{:S(2)}) async-start(bf16[8,128,1024]{2,1,0:T(8,128)(2,1)} %get-tuple-element.52), calls=%async_computation.2 | async-start | bytes 4194304 | tf_op jit(solution)/shard_map/all_to_all | solution.py:431
  49.5 26.9 %shard_map.163 = (bf16[16,136,128]{2,1,0:T(8,128)(2,1)}, bf16[16,128,128]{2,1,0:T(8,128)(2,1)}, f32[16,128,128]{2,1,0:T(8,128)}, bf16[16,128,128]{2,1,0:T(8,128)(2,1)}, bf16[16,128,128]{2,1,0:T(8,128)(2,1)}) custom-call(f32[2]{0:T(128)} %pad_maximum_fusion.4.coef, bf16[16,128,128]{2,1,0:T(8,128)(2,1)} %copy-done.10, bf16[16,128,128]{2,1,0:T(8,128)(2,1)} %copy-done.12, ...), custom_call_target="tpu_custom_call" | custom-call | flops 35999997952 | bytes 36000000 | tf_op jit(solution)/shard_map/pallas_call | solution.py:436
  76.4 3.1 %all-to-all-done.2.near = bf16[8,128,1024]{2,1,0:T(8,128)(2,1)S(1)} async-done(((bf16[8,128,1024]{2,1,0:T(8,128)(2,1)}), bf16[8,128,1024]{2,1,0:T(8,128)(2,1)S(1)}, u32[]{:S(2)}, u32[]{:S(2)}) %all-to-all-start.2) | async-done | bytes 2097184 | tf_op jit(solution)/shard_map/all_to_all | solution.py:431
  79.4 1.8 %collective-permute-start.4 = (bf16[8,128,1024]{2,1,0:T(8,128)(2,1)S(1)}, bf16[8,128,1024]{2,1,0:T(8,128)(2,1)}, u32[]{:S(2)}, u32[]{:S(2)}) collective-permute-start(bf16[8,128,1024]{2,1,0:T(8,128)(2,1)S(1)} %all-to-all-done.2.near), channel_id=1, source_target_pairs={{0,8},{8,0},{1,9},{9,1},{2,10},{10,2},{3,11},{11,3},{4,12},{12,4},... | collective-permute-start | bytes 6291464 | tf_op jit(solution)/shard_map/ppermute | solution.py:388
  81.2 0.3 collective-permute-start.2
  81.6 1.1 collective-permute-start.3
  82.7 3.9 %all-to-all-start.3 = ((bf16[16,136,128]{2,1,0:T(8,128)(2,1)}), bf16[16,136,128]{2,1,0:T(8,128)(2,1)S(1)}, u32[]{:S(2)}, u32[]{:S(2)}) async-start(bf16[16,136,128]{2,1,0:T(8,128)(2,1)} %get-tuple-element.57), calls=%async_computation.3 | async-start | bytes 1114112 | tf_op jit(solution)/shard_map/all_to_all | solution.py:465
  86.6 0.1 pad_add_fusion.site
  86.7 1.0 copy-done.6
  87.8 2.4 %shard_map.164.early = bf16[128,512]{1,0:T(8,128)(2,1)S(1)} custom-call(s32[3]{0:T(128)S(1)} %pad_add_fusion.site, bf16[16,128,128]{2,1,0:T(8,128)(2,1)S(1)} %copy-done.6, bf16[8,128,1024]{2,1,0:T(8,128)(2,1)S(1)} %all-to-all-done.2.near, bf16[8,128,1024]{2,1,0:T(8,128)(2,1)} %collective-permute-done.4.far), custom_call_target="tpu_custom_call" | custom-call | flops 3000000000 | bytes 3000000 | tf_op jit(solution)/shard_map/pallas_call | solution.py:467
  90.2 0.6 copy-done.7
  90.9 8.6 %collective-permute-done.2.low = bf16[16,128,128]{2,1,0:T(8,128)(2,1)S(1)} collective-permute-done((bf16[16,128,128]{2,1,0:T(8,128)(2,1)}, bf16[16,128,128]{2,1,0:T(8,128)(2,1)S(1)}, u32[]{:S(2)}, u32[]{:S(2)}) %collective-permute-start.2) | collective-permute-done | bytes 524320 | tf_op jit(solution)/shard_map/ppermute | solution.py:384
  99.5 1.6 %all-to-all-done.3.mq = bf16[16,136,128]{2,1,0:T(8,128)(2,1)S(1)} async-done(((bf16[16,136,128]{2,1,0:T(8,128)(2,1)}), bf16[16,136,128]{2,1,0:T(8,128)(2,1)S(1)}, u32[]{:S(2)}, u32[]{:S(2)}) %all-to-all-start.3) | async-done | bytes 557088 | tf_op jit(solution)/shard_map/all_to_all | solution.py:465
  101.1 0.8 copy-done.8
  101.9 4.9 %shard_map.165 = (bf16[4,4,128,128]{3,2,1,0:T(8,128)(2,1)}, bf16[16,24,512]{2,1,0:T(8,128)(2,1)}) custom-call(s32[3]{0:T(128)} %copy-done.1, f32[16,128,128]{2,1,0:T(8,128)} %get-tuple-element.58.own, bf16[16,128,128]{2,1,0:T(8,128)(2,1)} %copy-done.13, bf16[16,128,128]{2,1,0:T(8,128)(2,1)} %collective-permute-done.3.high, bf16[16,128,128]{2,1,0:T(8,128)(2,1)} %copy-done.10, ...), custom_call_target="tpu_custom_call" | custom-call | flops 7000000000 | bytes 7000000 | tf_op jit(solution)/shard_map/pallas_call | solution.py:479
  106.8 3.7 %all-to-all-start.4 = ((bf16[16,24,512]{2,1,0:T(8,128)(2,1)}), bf16[16,24,512]{2,1,0:T(8,128)(2,1)S(1)}, u32[]{:S(2)}, u32[]{:S(2)}) async-start(bf16[16,24,512]{2,1,0:T(8,128)(2,1)} %get-tuple-element.63), calls=%async_computation.4 | async-start | bytes 786432 | tf_op jit(solution)/shard_map/all_to_all | solution.py:490
  110.4 1.1 slice_bitcast_fusion
  111.6 0.1 collective-permute-start.7
  111.7 0.9 collective-permute-start.6
  112.6 2.3 %collective-permute-start.5 = (bf16[4,128,128]{2,1,0:T(8,128)(2,1)S(1)}, bf16[4,128,128]{2,1,0:T(8,128)(2,1)S(1)}, u32[]{:S(2)}, u32[]{:S(2)}) collective-permute-start(bf16[4,128,128]{2,1,0:T(8,128)(2,1)S(1)} %get-tuple-element.86), channel_id=1, source_target_pairs={{0,32},{32,0},{64,96},{96,64},{1,33},{33,1},{65,97},{97,65},{2,34}... | collective-permute-start | bytes 393224 | tf_op jit(solution)/shard_map/ppermute | solution.py:392
  114.9 5.7 %collective-permute-done.7 = bf16[4,128,128]{2,1,0:T(8,128)(2,1)S(1)} collective-permute-done((bf16[4,128,128]{2,1,0:T(8,128)(2,1)S(1)}, bf16[4,128,128]{2,1,0:T(8,128)(2,1)S(1)}, u32[]{:S(2)}, u32[]{:S(2)}) %collective-permute-start.7) | collective-permute-done | bytes 131104 | tf_op jit(solution)/shard_map/ppermute | solution.py:392
  120.6 1.1 shard_map.166
  121.8 7.5 %all-to-all-start.5 = ((bf16[64,16,512]{2,1,0:T(8,128)(2,1)}), bf16[64,16,512]{2,1,0:T(8,128)(2,1)S(1)}, u32[]{:S(2)}, u32[]{:S(2)}) async-start(bf16[64,16,512]{2,1,0:T(8,128)(2,1)} %get-tuple-element.66), calls=%async_computation.5 | async-start | bytes 2097152 | tf_op jit(solution)/shard_map/all_to_all | solution.py:499
  129.3 2.7 %collective-permute-start.8 = (bf16[4,128,128]{2,1,0:T(8,128)(2,1)S(1)}, bf16[4,128,128]{2,1,0:T(8,128)(2,1)S(1)}, u32[]{:S(2)}, u32[]{:S(2)}) collective-permute-start(bf16[4,128,128]{2,1,0:T(8,128)(2,1)S(1)} %pad_maximum_fusion.1), channel_id=1, source_target_pairs={{0,8},{8,0},{16,24},{24,16},{1,9},{9,1},{17,25},{25,17},{2,10},{10... | collective-permute-start | bytes 393224 | tf_op jit(solution)/shard_map/ppermute | solution.py:392
  132.1 1.4 collective-permute-start.9
  133.5 0.4 collective-permute-start.10
  133.9 0.7 pad_maximum_fusion.kv0
  134.6 12.1 %collective-permute-done.9.kv2 = bf16[4,128,128]{2,1,0:T(8,128)(2,1)S(1)} collective-permute-done((bf16[4,128,128]{2,1,0:T(8,128)(2,1)S(1)}, bf16[4,128,128]{2,1,0:T(8,128)(2,1)S(1)}, u32[]{:S(2)}, u32[]{:S(2)}) %collective-permute-start.9) | collective-permute-done | bytes 131104 | tf_op jit(solution)/shard_map/ppermute | solution.py:392
  146.6 2.9 %collective-permute-done.10.kv3 = bf16[4,128,128]{2,1,0:T(8,128)(2,1)S(1)} collective-permute-done((bf16[4,128,128]{2,1,0:T(8,128)(2,1)S(1)}, bf16[4,128,128]{2,1,0:T(8,128)(2,1)S(1)}, u32[]{:S(2)}, u32[]{:S(2)}) %collective-permute-start.10) | collective-permute-done | bytes 131104 | tf_op jit(solution)/shard_map/ppermute | solution.py:392
  149.6 0.4 collective-permute-start.11
  150.0 0.1 slice_reduce_fusion
  150.1 0.5 multiply_divide_fusion
  150.6 0.0 copy-start.3
  150.7 3.7 %shard_map.167 = (bf16[256,512]{1,0:T(8,128)(2,1)}, f32[256,512]{1,0:T(8,128)}) custom-call(s32[3]{0:T(128)} %copy-done.1, bf16[256,512]{1,0:T(8,128)(2,1)} %bitcast.26, f32[1,512]{1,0:T(1,128)} %bitcast.21, bf16[16,136,128]{2,1,0:T(8,128)(2,1)} %copy-done.8, bf16[4,128,128]{2,1,0:T(8,128)(2,1)} %pad_maximum_fusion.kv0, bf16[4,128,128]{2,1,0:T(8,128)(2,1)} %copy-done.14, ...), custom_call_target="tpu_custom_call" | custom-call | flops 4000000000 | bytes 4000000 | tf_op jit(solution)/shard_map/pallas_call | solution.py:503
  154.5 2.8 %shard_map.168 = (f32[512,512]{1,0:T(8,128)}, f32[512,512]{1,0:T(8,128)}, f32[512,512]{1,0:T(8,128)}, f32[512,512]{1,0:T(8,128)}, f32[1,512]{1,0:T(1,128)}) custom-call(s32[1]{0:T(128)} %bitcast.core, bf16[64,16,512]{2,1,0:T(8,128)(2,1)S(1)} %all-to-all-done.5.near, bf16[64,16,512]{2,1,0:T(8,128)(2,1)S(1)} %collective-permute-done.11.far, ...), custom_call_target="tpu_custom_call" | custom-call | flops 5000000000 | bytes 5000000 | tf_op jit(solution)/shard_map/pallas_call | solution.py:513
  (44 shorter events, 0.2 us)
Async XLA Ops:
  4.6 17.0 %all-to-all-start = ((bf16[16,128,128]{2,1,0:T(8,128)(2,1)}), bf16[16,128,128]{2,1,0:T(8,128)(2,1)S(1)}, u32[]{:S(2)}, u32[]{:S(2)}) async-start(bf16[16,128,128]{2,1,0:T(8,128)(2,1)} %get-tuple-element.49), calls=%async_computation | async-start | bytes 1048576 | tf_op jit(solution)/shard_map/all_to_all | solution.py:425
  11.9 19.0 %copy-start.17 = (f32[8]{0:T(128)S(1)}, f32[8]{0:T(128)}, u32[]{:S(2)}) copy-start(f32[8]{0:T(128)} %param.16) | copy-start | bytes 100
  21.6 23.7 %copy-start.10 = (bf16[16,128,128]{2,1,0:T(8,128)(2,1)}, bf16[16,128,128]{2,1,0:T(8,128)(2,1)S(1)}, u32[]{:S(2)}) copy-start(bf16[16,128,128]{2,1,0:T(8,128)(2,1)S(1)} %all-to-all-done.own.kv) | copy-start | bytes 1572868
  21.6 22.7 %collective-permute-start.1 = (bf16[16,128,128]{2,1,0:T(8,128)(2,1)S(1)}, bf16[16,128,128]{2,1,0:T(8,128)(2,1)S(1)}, u32[]{:S(2)}, u32[]{:S(2)}) collective-permute-start(bf16[16,128,128]{2,1,0:T(8,128)(2,1)S(1)} %all-to-all-done.own.kv), channel_id=1, source_target_pairs={{0,23},{16,0},{1,16},{17,1},{2,17},{18,2},{3,18},{19,3},{4,19},{20... | collective-permute-start | bytes 1572872 | tf_op jit(solution)/shard_map/ppermute | solution.py:384
  27.1 17.2 %collective-permute-start = (bf16[16,128,128]{2,1,0:T(8,128)(2,1)S(1)}, bf16[16,128,128]{2,1,0:T(8,128)(2,1)S(1)}, u32[]{:S(2)}, u32[]{:S(2)}) collective-permute-start(bf16[16,128,128]{2,1,0:T(8,128)(2,1)S(1)} %all-to-all-done.own.kv), channel_id=1, source_target_pairs={{0,16},{16,1},{1,17},{17,2},{2,18},{18,3},{3,19},{19,4},{4,20},{20... | collective-permute-start | bytes 1572872 | tf_op jit(solution)/shard_map/ppermute | solution.py:384
  27.1 17.2 %all-to-all-start.1 = ((bf16[16,136,128]{2,1,0:T(8,128)(2,1)}), bf16[16,136,128]{2,1,0:T(8,128)(2,1)S(1)}, u32[]{:S(2)}, u32[]{:S(2)}) async-start(bf16[16,136,128]{2,1,0:T(8,128)(2,1)} %get-tuple-element.50), calls=%async_computation.1 | async-start | bytes 1114112 | tf_op jit(solution)/shard_map/all_to_all | solution.py:429
  44.3 1.1 copy-start.9
  44.3 0.8 copy-start.11
  44.3 1.0 copy-start.12
  45.4 34.0 %all-to-all-start.2 = ((bf16[8,128,1024]{2,1,0:T(8,128)(2,1)}), bf16[8,128,1024]{2,1,0:T(8,128)(2,1)S(1)}, u32[]{:S(2)}, u32[]{:S(2)}) async-start(bf16[8,128,1024]{2,1,0:T(8,128)(2,1)} %get-tuple-element.52), calls=%async_computation.2 | async-start | bytes 4194304 | tf_op jit(solution)/shard_map/all_to_all | solution.py:431
  79.4 10.8 %copy-start = (bf16[8,128,1024]{2,1,0:T(8,128)(2,1)}, bf16[8,128,1024]{2,1,0:T(8,128)(2,1)S(1)}, u32[]{:S(2)}) copy-start(bf16[8,128,1024]{2,1,0:T(8,128)(2,1)S(1)} %all-to-all-done.2.near) | copy-start | bytes 6291460
  79.4 7.3 %collective-permute-start.4 = (bf16[8,128,1024]{2,1,0:T(8,128)(2,1)S(1)}, bf16[8,128,1024]{2,1,0:T(8,128)(2,1)}, u32[]{:S(2)}, u32[]{:S(2)}) collective-permute-start(bf16[8,128,1024]{2,1,0:T(8,128)(2,1)S(1)} %all-to-all-done.2.near), channel_id=1, source_target_pairs={{0,8},{8,0},{1,9},{9,1},{2,10},{10,2},{3,11},{11,3},{4,12},{12,4},... | collective-permute-start | bytes 6291464 | tf_op jit(solution)/shard_map/ppermute | solution.py:388
  81.2 18.2 %collective-permute-start.2 = (bf16[16,128,128]{2,1,0:T(8,128)(2,1)}, bf16[16,128,128]{2,1,0:T(8,128)(2,1)S(1)}, u32[]{:S(2)}, u32[]{:S(2)}) collective-permute-start(bf16[16,128,128]{2,1,0:T(8,128)(2,1)} %get-tuple-element.59), channel_id=1, source_target_pairs={{0,23},{16,0},{1,16},{17,1},{2,17},{18,2},{3,18},{19,3},{4,19},{20... | collective-permute-start | bytes 1572872 | tf_op jit(solution)/shard_map/ppermute | solution.py:384
  81.6 17.9 %collective-permute-start.3 = (bf16[16,128,128]{2,1,0:T(8,128)(2,1)}, bf16[16,128,128]{2,1,0:T(8,128)(2,1)}, u32[]{:S(2)}, u32[]{:S(2)}) collective-permute-start(bf16[16,128,128]{2,1,0:T(8,128)(2,1)} %get-tuple-element.60), channel_id=1, source_target_pairs={{0,16},{16,1},{1,17},{17,2},{2,18},{18,3},{3,19},{19,4},{4,20},{20... | collective-permute-start | bytes 1572872 | tf_op jit(solution)/shard_map/ppermute | solution.py:384
  82.7 18.4 %all-to-all-start.3 = ((bf16[16,136,128]{2,1,0:T(8,128)(2,1)}), bf16[16,136,128]{2,1,0:T(8,128)(2,1)S(1)}, u32[]{:S(2)}, u32[]{:S(2)}) async-start(bf16[16,136,128]{2,1,0:T(8,128)(2,1)} %get-tuple-element.57), calls=%async_computation.3 | async-start | bytes 1114112 | tf_op jit(solution)/shard_map/all_to_all | solution.py:465
  86.7 3.5 %copy-start.1 = (s32[3]{0:T(128)}, s32[3]{0:T(128)S(1)}, u32[]{:S(2)}) copy-start(s32[3]{0:T(128)S(1)} %pad_add_fusion.site) | copy-start | bytes 40
  86.7 1.0 copy-start.6
  90.2 0.7 copy-start.7
  99.5 1.6 %copy-start.13 = (bf16[16,128,128]{2,1,0:T(8,128)(2,1)}, bf16[16,128,128]{2,1,0:T(8,128)(2,1)S(1)}, u32[]{:S(2)}) copy-start(bf16[16,128,128]{2,1,0:T(8,128)(2,1)S(1)} %collective-permute-done.2.low) | copy-start | bytes 1572868
  101.1 0.8 copy-start.8
  106.8 13.9 %all-to-all-start.4 = ((bf16[16,24,512]{2,1,0:T(8,128)(2,1)}), bf16[16,24,512]{2,1,0:T(8,128)(2,1)S(1)}, u32[]{:S(2)}, u32[]{:S(2)}) async-start(bf16[16,24,512]{2,1,0:T(8,128)(2,1)} %get-tuple-element.63), calls=%async_computation.4 | async-start | bytes 786432 | tf_op jit(solution)/shard_map/all_to_all | solution.py:490
  111.6 9.1 %collective-permute-start.7 = (bf16[4,128,128]{2,1,0:T(8,128)(2,1)S(1)}, bf16[4,128,128]{2,1,0:T(8,128)(2,1)S(1)}, u32[]{:S(2)}, u32[]{:S(2)}) collective-permute-start(bf16[4,128,128]{2,1,0:T(8,128)(2,1)S(1)} %get-tuple-element.84), channel_id=1, source_target_pairs={{0,96},{32,64},{64,32},{96,0},{1,97},{33,65},{65,33},{97,1},{2,98}... | collective-permute-start | bytes 393224 | tf_op jit(solution)/shard_map/ppermute | solution.py:392
  111.7 9.0 %collective-permute-start.6 = (bf16[4,128,128]{2,1,0:T(8,128)(2,1)S(1)}, bf16[4,128,128]{2,1,0:T(8,128)(2,1)S(1)}, u32[]{:S(2)}, u32[]{:S(2)}) collective-permute-start(bf16[4,128,128]{2,1,0:T(8,128)(2,1)S(1)} %get-tuple-element.85), channel_id=1, source_target_pairs={{0,64},{32,96},{64,0},{96,32},{1,65},{33,97},{65,1},{97,33},{2,66}... | collective-permute-start | bytes 393224 | tf_op jit(solution)/shard_map/ppermute | solution.py:392
  112.6 8.1 %collective-permute-start.5 = (bf16[4,128,128]{2,1,0:T(8,128)(2,1)S(1)}, bf16[4,128,128]{2,1,0:T(8,128)(2,1)S(1)}, u32[]{:S(2)}, u32[]{:S(2)}) collective-permute-start(bf16[4,128,128]{2,1,0:T(8,128)(2,1)S(1)} %get-tuple-element.86), channel_id=1, source_target_pairs={{0,32},{32,0},{64,96},{96,64},{1,33},{33,1},{65,97},{97,65},{2,34}... | collective-permute-start | bytes 393224 | tf_op jit(solution)/shard_map/ppermute | solution.py:392
  121.8 27.8 %all-to-all-start.5 = ((bf16[64,16,512]{2,1,0:T(8,128)(2,1)}), bf16[64,16,512]{2,1,0:T(8,128)(2,1)S(1)}, u32[]{:S(2)}, u32[]{:S(2)}) async-start(bf16[64,16,512]{2,1,0:T(8,128)(2,1)} %get-tuple-element.66), calls=%async_computation.5 | async-start | bytes 2097152 | tf_op jit(solution)/shard_map/all_to_all | solution.py:499
  129.3 5.3 %collective-permute-start.8 = (bf16[4,128,128]{2,1,0:T(8,128)(2,1)S(1)}, bf16[4,128,128]{2,1,0:T(8,128)(2,1)S(1)}, u32[]{:S(2)}, u32[]{:S(2)}) collective-permute-start(bf16[4,128,128]{2,1,0:T(8,128)(2,1)S(1)} %pad_maximum_fusion.1), channel_id=1, source_target_pairs={{0,8},{8,0},{16,24},{24,16},{1,9},{9,1},{17,25},{25,17},{2,10},{10... | collective-permute-start | bytes 393224 | tf_op jit(solution)/shard_map/ppermute | solution.py:392
  132.1 14.6 %collective-permute-start.9 = (bf16[4,128,128]{2,1,0:T(8,128)(2,1)S(1)}, bf16[4,128,128]{2,1,0:T(8,128)(2,1)S(1)}, u32[]{:S(2)}, u32[]{:S(2)}) collective-permute-start(bf16[4,128,128]{2,1,0:T(8,128)(2,1)S(1)} %pad_maximum_fusion.2), channel_id=1, source_target_pairs={{0,16},{8,24},{16,0},{24,8},{1,17},{9,25},{17,1},{25,9},{2,18},{10... | collective-permute-start | bytes 393224 | tf_op jit(solution)/shard_map/ppermute | solution.py:392
  133.5 16.1 %collective-permute-start.10 = (bf16[4,128,128]{2,1,0:T(8,128)(2,1)S(1)}, bf16[4,128,128]{2,1,0:T(8,128)(2,1)S(1)}, u32[]{:S(2)}, u32[]{:S(2)}) collective-permute-start(bf16[4,128,128]{2,1,0:T(8,128)(2,1)S(1)} %pad_maximum_fusion.3), channel_id=1, source_target_pairs={{0,24},{8,16},{16,8},{24,0},{1,25},{9,17},{17,9},{25,1},{2,26},{10... | collective-permute-start | bytes 393224 | tf_op jit(solution)/shard_map/ppermute | solution.py:392
  134.6 16.1 %copy-start.14 = (bf16[4,128,128]{2,1,0:T(8,128)(2,1)}, bf16[4,128,128]{2,1,0:T(8,128)(2,1)S(1)}, u32[]{:S(2)}) copy-start(bf16[4,128,128]{2,1,0:T(8,128)(2,1)S(1)} %collective-permute-done.8.kv1) | copy-start | bytes 393220
  146.6 4.0 %copy-start.15 = (bf16[4,128,128]{2,1,0:T(8,128)(2,1)}, bf16[4,128,128]{2,1,0:T(8,128)(2,1)S(1)}, u32[]{:S(2)}) copy-start(bf16[4,128,128]{2,1,0:T(8,128)(2,1)S(1)} %collective-permute-done.9.kv2) | copy-start | bytes 393220
  149.6 1.0 copy-start.16
  149.6 4.8 %collective-permute-start.11 = (bf16[64,16,512]{2,1,0:T(8,128)(2,1)S(1)}, bf16[64,16,512]{2,1,0:T(8,128)(2,1)S(1)}, u32[]{:S(2)}, u32[]{:S(2)}) collective-permute-start(bf16[64,16,512]{2,1,0:T(8,128)(2,1)S(1)} %all-to-all-done.5.near), channel_id=1, source_target_pairs={{0,8},{8,0},{1,9},{9,1},{2,10},{10,2},{3,11},{11,3},{4,12},{12,4},... | collective-permute-start | bytes 3145736 | tf_op jit(solution)/shard_map/ppermute | solution.py:388
  150.6 3.8 %copy-start.2 = (bf16[512,512]{1,0:T(8,128)(2,1)S(1)}, bf16[512,512]{1,0:T(8,128)(2,1)}, u32[]{:S(2)}) copy-start(bf16[512,512]{1,0:T(8,128)(2,1)} %wk.5) | copy-start | bytes 1572868
  150.6 3.8 %copy-start.3 = (bf16[512,512]{1,0:T(8,128)(2,1)S(1)}, bf16[512,512]{1,0:T(8,128)(2,1)}, u32[]{:S(2)}) copy-start(bf16[512,512]{1,0:T(8,128)(2,1)} %wv.5) | copy-start | bytes 1572868
  150.7 3.8 %copy-start.4 = (bf16[512,512]{1,0:T(8,128)(2,1)S(1)}, bf16[512,512]{1,0:T(8,128)(2,1)}, u32[]{:S(2)}) copy-start(bf16[512,512]{1,0:T(8,128)(2,1)} %wq.5) | copy-start | bytes 1572868
  150.7 3.8 %copy-start.5 = (f32[512]{0:T(512)S(1)}, f32[512]{0:T(512)}, u32[]{:S(2)}) copy-start(f32[512]{0:T(512)} %param.11) | copy-start | bytes 6148

commit v6 on v5

--- a/solution.py
+++ b/solution.py
@@ -213,11 +213,12 @@
         inverse = 1.0 / jnp.sum(sums[0], axis=0, keepdims=True)
         inner_row = jnp.sum(sums[1], axis=0, keepdims=True) * inverse
         spread = spread_of(number)
-        next_spread = spread_of(following)
+        next_spread = None if following is None else spread_of(following)
         next_sums = (zero, zero)
         out = jnp.zeros((2 * DH, 2 * BLK), F32)
         for g in range(9):
-            next_sums = first_group(following, g, next_spread, next_sums, other)
+            if following is not None:
+                next_sums = first_group(following, g, next_spread, next_sums, other)
             turned, mixed, heat = second_group(
                 number, g, spread, inverse, inner_row, heat, buffer
             )
@@ -240,10 +241,11 @@
         sums, heat = carry
         number = index * 2
         sums, heat = step(number, number + 1, sums, heat, wbuf, wbuf2)
-        following = jnp.minimum(number + 2, 15)
-        return step(number + 1, following, sums, heat, wbuf2, wbuf)
-
-    _, heat = lax.fori_loop(0, 8, two_blocks, (sums, zero))
+        return step(number + 1, number + 2, sums, heat, wbuf2, wbuf)
+
+    sums, heat = lax.fori_loop(0, 7, two_blocks, (sums, zero))
+    sums, heat = step(14, 15, sums, heat, wbuf, wbuf2)
+    _, heat = step(15, None, sums, heat, wbuf2, wbuf)
     heat = jnp.sum(jnp.sum(heat, axis=0, keepdims=True), axis=1, keepdims=True)
     upper, lower = high_low(jnp.broadcast_to(heat, (1, BLK)))
     tail = jnp.concatenate([upper, lower, jnp.zeros((6, BLK), F32)], axis=0).astype(BF)
@@ -313,20 +315,23 @@
         lines.append(0.5 * jnp.concatenate(pairs, axis=0))
     whole_sum = lines[0] + lines[1]
     upper, lower = high_low(whole_sum)
-    extra = jnp.concatenate([upper, lower, upper, lower], axis=1).astype(BF)
+    extra = jnp.concatenate([upper[:, :DH], lower[:, DH:]], axis=1).astype(BF)
     query_part, proj_part = early[:DH], early[DH:]
     joined = jnp.concatenate([query_part, both_part.astype(BF), proj_part], axis=0)
     for g in range(16):
-        parts_out[g, :16] = joined[g * 16 : (g + 1) * 16]
-        parts_out[g, 16:] = extra
+        for c in range(4):
+            parts_out[g, c * 16 : (c + 1) * 16] = joined[
+                g * 16 : (g + 1) * 16, c * 128 : (c + 1) * 128
+            ]
+        parts_out[g, 64:] = extra
 
 
 def sum_kernel(arrived, share_out, temper_out):
-    total = jnp.zeros((24, D), F32)
+    total = jnp.zeros((72, 128), F32)
     for g in range(16):
         total = total + arrived[g].astype(F32)
-    temper_out[...] = total[16:, :128] + total[16:, 128:256]
-    share = total[:16].astype(BF)
+    temper_out[...] = jnp.broadcast_to(total[64:, :1] + total[64:, DH : DH + 1], (H, 128))
+    share = jnp.concatenate([total[c * 16 : (c + 1) * 16] for c in range(4)], axis=1).astype(BF)
     for k in range(64):
         share_out[k] = share
 
@@ -456,7 +461,7 @@
             pltpu.SMEM((16, 128), F32),
             pltpu.SemaphoreType.DMA((9,)),
         ],
-        compiler_params=params(56),
+        compiler_params=params(60),
     )(coef, own, before, after, qb)
     from_after = shift(before_grad, -1)
     from_before = shift(after_grad, 1)
@@ -479,7 +484,7 @@
     kv_back, parts = pl.pallas_call(
         head_kernel,
         cost_estimate=cost(7),
-        out_shape=(whole((4, 4, BLK, 2 * DH), BF), whole((16, 24, D), BF)),
+        out_shape=(whole((4, 4, BLK, 2 * DH), BF), whole((16, 72, 128), BF)),
         grid=(1,),
         in_specs=[smem]
         + [one_spec(a) for a in (own_grad, from_after, from_before, own, qb, early, mq)]
@@ -489,7 +494,6 @@
     )(site, own_grad, from_after, from_before, own, qb, early, mq, rows_near, rows_far)
     arrived = lax.all_to_all(parts, RING, 0, 0, tiled=True)
     turn = [kv_back[0]] + [swap_near(kv_back[step], "gx", step) for step in range(1, 4)]
-    arrived, *turn = lax.optimization_barrier((arrived, *turn))
     share, temper_sum = pl.pallas_call(
         sum_kernel,
         cost_estimate=cost(2),

time: 158 us -> 154 us (0.975)
  starting transfers between devices: 47.4 us -> 44.9 us
  waiting for transfers between devices: 49.4 us -> 47.1 us
    ppermute x6, waiting for transfers between devices: 20.7 us -> 15.2 us  [swap_near(): return lax.ppermute(block, axes, [(i, i ^ step) for i in range(4)])]
    all_to_all x1, waiting for transfers between devices: 0.01 us -> 2.65 us  [local(): arrived = lax.all_to_all(parts, RING, 0, 0, tiled=True)]
    all_to_all x1, starting transfers between devices: 7.46 us -> 5.25 us  [local(): near = lax.all_to_all(share, CHIPS, 0, 0, tiled=True)]
  transfers between devices with their start and end apart: 18 -> 18, of which waited for: 8 -> 8; matrix products, arithmetic and copies ran while one was open for 2% -> 3% of each run, Pallas kernels for 24% -> 25%
where the time goes in v6:
time: 154 us; the launch traced here: 153 us
  Pallas kernels  50.3 us (33%)
  waiting for transfers between devices  47.1 us (31%)
  starting transfers between devices  44.9 us (29%)
  local copies, waits for them, and re-layouts  6.28 us (4%)
  between operations  2.18 us (1%)
  other arithmetic  1.92 us (1%)
    pallas_call x1, Pallas kernels, local(): pl.pallas_call(attend_kernel, cost_estimate=cost(36), out_shape=(whole(wi...  26.3 us
    ppermute x6, waiting for transfers between devices, swap_near(): return lax.ppermute(block, axes, [(i, i ^ step) for i in range(4)])  15.2 us
    all_to_all x1, waiting for transfers between devices, local(): qb = lax.all_to_all(qb_send, GROUP, 0, 0, tiled=True)  10.9 us
    ppermute x4, waiting for transfers between devices, shift(): lax.ppermute(block, RING, [(spots[t], spots[(t + step) % 16]) for t in ra...  8.61 us
    ppermute x6, starting transfers between devices, swap_near(): return lax.ppermute(block, axes, [(i, i ^ step) for i in range(4)])  7.58 us
    all_to_all x1, starting transfers between devices, local(): own = lax.all_to_all(kv_send, GROUP, 0, 0, tiled=True)  7.34 us
    ppermute x4, starting transfers between devices, shift(): lax.ppermute(block, RING, [(spots[t], spots[(t + step) % 16]) for t in ra...  6.99 us
    all_to_all x1, starting transfers between devices, local(): near = lax.all_to_all(share, CHIPS, 0, 0, tiled=True)  5.25 us
  transfers between devices with their start and end apart: 18, of which 8 were waited for; matrix products, arithmetic and copies ran while one was open for 3% of the time, Pallas kernels for 25%

profile of v6, /device:TPU:1, one launch (start us, length us, event | category | flops | bytes accessed | tf_op | source)
XLA Modules:
  0.0 152.6 jit_solution(7473259193686433727)
XLA Ops:
  0.6 4.0 %shard_map.161 = (bf16[16,128,128]{2,1,0:T(8,128)(2,1)}, f32[256,128]{1,0:T(8,128)}) custom-call(bf16[256,512]{1,0:T(8,128)(2,1)} %bitcast.30, f32[1,512]{1,0:T(1,128)} %bitcast.25, bf16[512,512]{1,0:T(8,128)(2,1)} %wk.5, bf16[512,512]{1,0:T(8,128)(2,1)} %wv.5), custom_call_target="tpu_custom_call" | custom-call | flops 3000000000 | bytes 3000000 | tf_op jit(solution)/shard_map/pallas_call | solution.py:414
  4.6 7.3 %all-to-all-start = ((bf16[16,128,128]{2,1,0:T(8,128)(2,1)}), bf16[16,128,128]{2,1,0:T(8,128)(2,1)S(1)}, u32[]{:S(2)}, u32[]{:S(2)}) async-start(bf16[16,128,128]{2,1,0:T(8,128)(2,1)} %get-tuple-element.44), calls=%async_computation | async-start | bytes 1048576 | tf_op jit(solution)/shard_map/all_to_all | solution.py:430
  11.9 5.1 %shard_map.162 = (bf16[16,136,128]{2,1,0:T(8,128)(2,1)}, bf16[8,128,1024]{2,1,0:T(8,128)(2,1)}) custom-call(bf16[256,512]{1,0:T(8,128)(2,1)} %bitcast.31, f32[1,512]{1,0:T(1,128)} %bitcast.26, bf16[256,512]{1,0:T(8,128)(2,1)} %bitcast.29, s32[2,27]{1,0:T(2,128)} %bitcast.33, s32[2,27]{1,0:T(2,128)} %bitcast.34, f32[256,128]{1,0:T(8,128)} %get-tuple-element.41.factors_in, ...), custom_call_target="tpu_custom_call" | custom-call | flops 4000000000 | bytes 4000000 | tf_op jit(solution)/shard_map/pallas_call | solution.py:420
  17.0 4.6 %all-to-all-done.own.kv = bf16[16,128,128]{2,1,0:T(8,128)(2,1)S(1)} async-done(((bf16[16,128,128]{2,1,0:T(8,128)(2,1)}), bf16[16,128,128]{2,1,0:T(8,128)(2,1)S(1)}, u32[]{:S(2)}, u32[]{:S(2)}) %all-to-all-start) | async-done | bytes 524320 | tf_op jit(solution)/shard_map/all_to_all | solution.py:430
  21.6 5.5 %collective-permute-start.1 = (bf16[16,128,128]{2,1,0:T(8,128)(2,1)S(1)}, bf16[16,128,128]{2,1,0:T(8,128)(2,1)S(1)}, u32[]{:S(2)}, u32[]{:S(2)}) collective-permute-start(bf16[16,128,128]{2,1,0:T(8,128)(2,1)S(1)} %all-to-all-done.own.kv), channel_id=1, source_target_pairs={{0,23},{16,0},{1,16},{17,1},{2,17},{18,2},{3,18},{19,3},{4,19},{20... | collective-permute-start | bytes 1572872 | tf_op jit(solution)/shard_map/ppermute | solution.py:389
  27.1 3.9 %all-to-all-start.1 = ((bf16[16,136,128]{2,1,0:T(8,128)(2,1)}), bf16[16,136,128]{2,1,0:T(8,128)(2,1)S(1)}, u32[]{:S(2)}, u32[]{:S(2)}) async-start(bf16[16,136,128]{2,1,0:T(8,128)(2,1)} %get-tuple-element.45), calls=%async_computation.1 | async-start | bytes 1114112 | tf_op jit(solution)/shard_map/all_to_all | solution.py:434
  31.0 0.6 dynamic_slice.3
  32.9 0.6 pad_maximum_fusion.4.coef
  33.4 10.9 %all-to-all-done.1.qb = bf16[16,136,128]{2,1,0:T(8,128)(2,1)S(1)} async-done(((bf16[16,136,128]{2,1,0:T(8,128)(2,1)}), bf16[16,136,128]{2,1,0:T(8,128)(2,1)S(1)}, u32[]{:S(2)}, u32[]{:S(2)}) %all-to-all-start.1) | async-done | bytes 557088 | tf_op jit(solution)/shard_map/all_to_all | solution.py:434
  44.3 0.8 copy-done.11
  45.1 0.2 copy-done.12
  45.3 0.2 copy-done.9
  45.4 4.0 %all-to-all-start.2 = ((bf16[8,128,1024]{2,1,0:T(8,128)(2,1)}), bf16[8,128,1024]{2,1,0:T(8,128)(2,1)S(1)}, u32[]{:S(2)}, u32[]{:S(2)}) async-start(bf16[8,128,1024]{2,1,0:T(8,128)(2,1)} %get-tuple-element.47), calls=%async_computation.2 | async-start | bytes 4194304 | tf_op jit(solution)/shard_map/all_to_all | solution.py:436
  49.5 26.3 %shard_map.163 = (bf16[16,136,128]{2,1,0:T(8,128)(2,1)}, bf16[16,128,128]{2,1,0:T(8,128)(2,1)}, f32[16,128,128]{2,1,0:T(8,128)}, bf16[16,128,128]{2,1,0:T(8,128)(2,1)}, bf16[16,128,128]{2,1,0:T(8,128)(2,1)}) custom-call(f32[2]{0:T(128)} %pad_maximum_fusion.4.coef, bf16[16,128,128]{2,1,0:T(8,128)(2,1)} %copy-done.10, bf16[16,128,128]{2,1,0:T(8,128)(2,1)} %copy-done.12, ...), custom_call_target="tpu_custom_call" | custom-call | flops 35999997952 | bytes 36000000 | tf_op jit(solution)/shard_map/pallas_call | solution.py:441
  75.7 3.7 %all-to-all-done.2.near = bf16[8,128,1024]{2,1,0:T(8,128)(2,1)S(1)} async-done(((bf16[8,128,1024]{2,1,0:T(8,128)(2,1)}), bf16[8,128,1024]{2,1,0:T(8,128)(2,1)S(1)}, u32[]{:S(2)}, u32[]{:S(2)}) %all-to-all-start.2) | async-done | bytes 2097184 | tf_op jit(solution)/shard_map/all_to_all | solution.py:436
  79.4 1.8 %collective-permute-start.4 = (bf16[8,128,1024]{2,1,0:T(8,128)(2,1)S(1)}, bf16[8,128,1024]{2,1,0:T(8,128)(2,1)}, u32[]{:S(2)}, u32[]{:S(2)}) collective-permute-start(bf16[8,128,1024]{2,1,0:T(8,128)(2,1)S(1)} %all-to-all-done.2.near), channel_id=1, source_target_pairs={{0,8},{8,0},{1,9},{9,1},{2,10},{10,2},{3,11},{11,3},{4,12},{12,4},... | collective-permute-start | bytes 6291464 | tf_op jit(solution)/shard_map/ppermute | solution.py:393
  81.2 0.3 collective-permute-start.2
  81.6 1.1 collective-permute-start.3
  82.7 3.9 %all-to-all-start.3 = ((bf16[16,136,128]{2,1,0:T(8,128)(2,1)}), bf16[16,136,128]{2,1,0:T(8,128)(2,1)S(1)}, u32[]{:S(2)}, u32[]{:S(2)}) async-start(bf16[16,136,128]{2,1,0:T(8,128)(2,1)} %get-tuple-element.52), calls=%async_computation.3 | async-start | bytes 1114112 | tf_op jit(solution)/shard_map/all_to_all | solution.py:470
  86.6 0.1 pad_add_fusion.site
  86.7 1.0 copy-done.6
  87.8 2.4 %shard_map.164.early = bf16[128,512]{1,0:T(8,128)(2,1)S(1)} custom-call(s32[3]{0:T(128)S(1)} %pad_add_fusion.site, bf16[16,128,128]{2,1,0:T(8,128)(2,1)S(1)} %copy-done.6, bf16[8,128,1024]{2,1,0:T(8,128)(2,1)S(1)} %all-to-all-done.2.near, bf16[8,128,1024]{2,1,0:T(8,128)(2,1)} %collective-permute-done.4.far), custom_call_target="tpu_custom_call" | custom-call | flops 3000000000 | bytes 3000000 | tf_op jit(solution)/shard_map/pallas_call | solution.py:472
  90.2 0.0 copy-start.7
  90.2 0.6 copy-done.7
  90.9 8.6 %collective-permute-done.2.low = bf16[16,128,128]{2,1,0:T(8,128)(2,1)S(1)} collective-permute-done((bf16[16,128,128]{2,1,0:T(8,128)(2,1)}, bf16[16,128,128]{2,1,0:T(8,128)(2,1)S(1)}, u32[]{:S(2)}, u32[]{:S(2)}) %collective-permute-start.2) | collective-permute-done | bytes 524320 | tf_op jit(solution)/shard_map/ppermute | solution.py:389
  99.5 1.6 %all-to-all-done.3.mq = bf16[16,136,128]{2,1,0:T(8,128)(2,1)S(1)} async-done(((bf16[16,136,128]{2,1,0:T(8,128)(2,1)}), bf16[16,136,128]{2,1,0:T(8,128)(2,1)S(1)}, u32[]{:S(2)}, u32[]{:S(2)}) %all-to-all-start.3) | async-done | bytes 557088 | tf_op jit(solution)/shard_map/all_to_all | solution.py:470
  101.1 0.8 copy-done.8
  101.9 4.8 %shard_map.165 = (bf16[4,4,128,128]{3,2,1,0:T(8,128)(2,1)}, bf16[16,72,128]{2,1,0:T(8,128)(2,1)}) custom-call(s32[3]{0:T(128)} %copy-done.1, f32[16,128,128]{2,1,0:T(8,128)} %get-tuple-element.53.own, bf16[16,128,128]{2,1,0:T(8,128)(2,1)} %copy-done.13, bf16[16,128,128]{2,1,0:T(8,128)(2,1)} %collective-permute-done.3.high, bf16[16,128,128]{2,1,0:T(8,128)(2,1)} %copy-done.10, ...), custom_call_target="tpu_custom_call" | custom-call | flops 7000000000 | bytes 7000000 | tf_op jit(solution)/shard_map/pallas_call | solution.py:484
  106.7 3.7 %all-to-all-start.4 = ((bf16[16,72,128]{2,1,0:T(8,128)(2,1)}), bf16[16,72,128]{2,1,0:T(8,128)(2,1)S(1)}, u32[]{:S(2)}, u32[]{:S(2)}) async-start(bf16[16,72,128]{2,1,0:T(8,128)(2,1)} %get-tuple-element.58), calls=%async_computation.4 | async-start | bytes 589824 | tf_op jit(solution)/shard_map/all_to_all | solution.py:495
  110.4 1.1 slice_bitcast_fusion.2
  111.5 0.1 collective-permute-start.5
  111.6 0.1 collective-permute-start.7
  111.6 3.1 %collective-permute-start.6 = (bf16[4,128,128]{2,1,0:T(8,128)(2,1)S(1)}, bf16[4,128,128]{2,1,0:T(8,128)(2,1)S(1)}, u32[]{:S(2)}, u32[]{:S(2)}) collective-permute-start(bf16[4,128,128]{2,1,0:T(8,128)(2,1)S(1)} %get-tuple-element.80), channel_id=1, source_target_pairs={{0,64},{32,96},{64,0},{96,32},{1,65},{33,97},{65,1},{97,33},{2,66}... | collective-permute-start | bytes 393224 | tf_op jit(solution)/shard_map/ppermute | solution.py:397
  114.8 0.8 slice_bitcast_fusion.3
  115.6 2.6 %all-to-all-done.4.arrived = bf16[16,72,128]{2,1,0:T(8,128)(2,1)S(1)} async-done(((bf16[16,72,128]{2,1,0:T(8,128)(2,1)}), bf16[16,72,128]{2,1,0:T(8,128)(2,1)S(1)}, u32[]{:S(2)}, u32[]{:S(2)}) %all-to-all-start.4) | async-done | bytes 294944 | tf_op jit(solution)/shard_map/all_to_all | solution.py:495
  118.3 1.2 shard_map.166
  119.4 5.2 %all-to-all-start.5 = ((bf16[64,16,512]{2,1,0:T(8,128)(2,1)}), bf16[64,16,512]{2,1,0:T(8,128)(2,1)S(1)}, u32[]{:S(2)}, u32[]{:S(2)}) async-start(bf16[64,16,512]{2,1,0:T(8,128)(2,1)} %get-tuple-element.59), calls=%async_computation.5 | async-start | bytes 2097152 | tf_op jit(solution)/shard_map/all_to_all | solution.py:503
  124.8 2.5 %collective-permute-start.8 = (bf16[4,128,128]{2,1,0:T(8,128)(2,1)S(1)}, bf16[4,128,128]{2,1,0:T(8,128)(2,1)S(1)}, u32[]{:S(2)}, u32[]{:S(2)}) collective-permute-start(bf16[4,128,128]{2,1,0:T(8,128)(2,1)S(1)} %pad_maximum_fusion.1), channel_id=1, source_target_pairs={{0,8},{8,0},{16,24},{24,16},{1,9},{9,1},{17,25},{25,17},{2,10},{10... | collective-permute-start | bytes 393224 | tf_op jit(solution)/shard_map/ppermute | solution.py:397
  127.3 1.4 collective-permute-start.9
  128.7 0.4 collective-permute-start.10
  129.1 0.7 pad_maximum_fusion.kv0
  129.8 12.2 %collective-permute-done.9.kv2 = bf16[4,128,128]{2,1,0:T(8,128)(2,1)S(1)} collective-permute-done((bf16[4,128,128]{2,1,0:T(8,128)(2,1)S(1)}, bf16[4,128,128]{2,1,0:T(8,128)(2,1)S(1)}, u32[]{:S(2)}, u32[]{:S(2)}) %collective-permute-start.9) | collective-permute-done | bytes 131104 | tf_op jit(solution)/shard_map/ppermute | solution.py:397
  142.0 3.0 %collective-permute-done.10.kv3 = bf16[4,128,128]{2,1,0:T(8,128)(2,1)S(1)} collective-permute-done((bf16[4,128,128]{2,1,0:T(8,128)(2,1)S(1)}, bf16[4,128,128]{2,1,0:T(8,128)(2,1)S(1)}, u32[]{:S(2)}, u32[]{:S(2)}) %collective-permute-start.10) | collective-permute-done | bytes 131104 | tf_op jit(solution)/shard_map/ppermute | solution.py:397
  145.0 0.4 collective-permute-start.11
  145.4 0.1 slice_reduce_fusion
  145.5 0.5 multiply_divide_fusion
  146.1 3.7 %shard_map.167 = (bf16[256,512]{1,0:T(8,128)(2,1)}, f32[256,512]{1,0:T(8,128)}) custom-call(s32[3]{0:T(128)} %copy-done.1, bf16[256,512]{1,0:T(8,128)(2,1)} %bitcast.32, f32[1,512]{1,0:T(1,128)} %bitcast.27, bf16[16,136,128]{2,1,0:T(8,128)(2,1)} %copy-done.8, bf16[4,128,128]{2,1,0:T(8,128)(2,1)} %pad_maximum_fusion.kv0, bf16[4,128,128]{2,1,0:T(8,128)(2,1)} %copy-done.14, ...), custom_call_target="tpu_custom_call" | custom-call | flops 4000000000 | bytes 4000000 | tf_op jit(solution)/shard_map/pallas_call | solution.py:507
  149.8 2.8 %shard_map.168 = (f32[512,512]{1,0:T(8,128)}, f32[512,512]{1,0:T(8,128)}, f32[512,512]{1,0:T(8,128)}, f32[512,512]{1,0:T(8,128)}, f32[1,512]{1,0:T(1,128)}) custom-call(s32[1]{0:T(128)} %bitcast.core, bf16[64,16,512]{2,1,0:T(8,128)(2,1)S(1)} %all-to-all-done.5.near, bf16[64,16,512]{2,1,0:T(8,128)(2,1)S(1)} %collective-permute-done.11.far, ...), custom_call_target="tpu_custom_call" | custom-call | flops 5000000000 | bytes 5000000 | tf_op jit(solution)/shard_map/pallas_call | solution.py:517
  (46 shorter events, 0.2 us)
Async XLA Ops:
  4.6 17.0 %all-to-all-start = ((bf16[16,128,128]{2,1,0:T(8,128)(2,1)}), bf16[16,128,128]{2,1,0:T(8,128)(2,1)S(1)}, u32[]{:S(2)}, u32[]{:S(2)}) async-start(bf16[16,128,128]{2,1,0:T(8,128)(2,1)} %get-tuple-element.44), calls=%async_computation | async-start | bytes 1048576 | tf_op jit(solution)/shard_map/all_to_all | solution.py:430
  11.9 19.0 %copy-start.17 = (f32[8]{0:T(128)S(1)}, f32[8]{0:T(128)}, u32[]{:S(2)}) copy-start(f32[8]{0:T(128)} %param.16) | copy-start | bytes 100
  21.6 23.7 %copy-start.10 = (bf16[16,128,128]{2,1,0:T(8,128)(2,1)}, bf16[16,128,128]{2,1,0:T(8,128)(2,1)S(1)}, u32[]{:S(2)}) copy-start(bf16[16,128,128]{2,1,0:T(8,128)(2,1)S(1)} %all-to-all-done.own.kv) | copy-start | bytes 1572868
  21.6 22.7 %collective-permute-start.1 = (bf16[16,128,128]{2,1,0:T(8,128)(2,1)S(1)}, bf16[16,128,128]{2,1,0:T(8,128)(2,1)S(1)}, u32[]{:S(2)}, u32[]{:S(2)}) collective-permute-start(bf16[16,128,128]{2,1,0:T(8,128)(2,1)S(1)} %all-to-all-done.own.kv), channel_id=1, source_target_pairs={{0,23},{16,0},{1,16},{17,1},{2,17},{18,2},{3,18},{19,3},{4,19},{20... | collective-permute-start | bytes 1572872 | tf_op jit(solution)/shard_map/ppermute | solution.py:389
  27.1 17.2 %collective-permute-start = (bf16[16,128,128]{2,1,0:T(8,128)(2,1)S(1)}, bf16[16,128,128]{2,1,0:T(8,128)(2,1)S(1)}, u32[]{:S(2)}, u32[]{:S(2)}) collective-permute-start(bf16[16,128,128]{2,1,0:T(8,128)(2,1)S(1)} %all-to-all-done.own.kv), channel_id=1, source_target_pairs={{0,16},{16,1},{1,17},{17,2},{2,18},{18,3},{3,19},{19,4},{4,20},{20... | collective-permute-start | bytes 1572872 | tf_op jit(solution)/shard_map/ppermute | solution.py:389
  27.1 17.2 %all-to-all-start.1 = ((bf16[16,136,128]{2,1,0:T(8,128)(2,1)}), bf16[16,136,128]{2,1,0:T(8,128)(2,1)S(1)}, u32[]{:S(2)}, u32[]{:S(2)}) async-start(bf16[16,136,128]{2,1,0:T(8,128)(2,1)} %get-tuple-element.45), calls=%async_computation.1 | async-start | bytes 1114112 | tf_op jit(solution)/shard_map/all_to_all | solution.py:434
  44.3 1.1 copy-start.9
  44.3 0.8 copy-start.11
  44.3 1.0 copy-start.12
  45.4 34.0 %all-to-all-start.2 = ((bf16[8,128,1024]{2,1,0:T(8,128)(2,1)}), bf16[8,128,1024]{2,1,0:T(8,128)(2,1)S(1)}, u32[]{:S(2)}, u32[]{:S(2)}) async-start(bf16[8,128,1024]{2,1,0:T(8,128)(2,1)} %get-tuple-element.47), calls=%async_computation.2 | async-start | bytes 4194304 | tf_op jit(solution)/shard_map/all_to_all | solution.py:436
  79.4 10.8 %copy-start = (bf16[8,128,1024]{2,1,0:T(8,128)(2,1)}, bf16[8,128,1024]{2,1,0:T(8,128)(2,1)S(1)}, u32[]{:S(2)}) copy-start(bf16[8,128,1024]{2,1,0:T(8,128)(2,1)S(1)} %all-to-all-done.2.near) | copy-start | bytes 6291460
  79.4 7.3 %collective-permute-start.4 = (bf16[8,128,1024]{2,1,0:T(8,128)(2,1)S(1)}, bf16[8,128,1024]{2,1,0:T(8,128)(2,1)}, u32[]{:S(2)}, u32[]{:S(2)}) collective-permute-start(bf16[8,128,1024]{2,1,0:T(8,128)(2,1)S(1)} %all-to-all-done.2.near), channel_id=1, source_target_pairs={{0,8},{8,0},{1,9},{9,1},{2,10},{10,2},{3,11},{11,3},{4,12},{12,4},... | collective-permute-start | bytes 6291464 | tf_op jit(solution)/shard_map/ppermute | solution.py:393
  81.2 18.2 %collective-permute-start.2 = (bf16[16,128,128]{2,1,0:T(8,128)(2,1)}, bf16[16,128,128]{2,1,0:T(8,128)(2,1)S(1)}, u32[]{:S(2)}, u32[]{:S(2)}) collective-permute-start(bf16[16,128,128]{2,1,0:T(8,128)(2,1)} %get-tuple-element.54), channel_id=1, source_target_pairs={{0,23},{16,0},{1,16},{17,1},{2,17},{18,2},{3,18},{19,3},{4,19},{20... | collective-permute-start | bytes 1572872 | tf_op jit(solution)/shard_map/ppermute | solution.py:389
  81.6 17.9 %collective-permute-start.3 = (bf16[16,128,128]{2,1,0:T(8,128)(2,1)}, bf16[16,128,128]{2,1,0:T(8,128)(2,1)}, u32[]{:S(2)}, u32[]{:S(2)}) collective-permute-start(bf16[16,128,128]{2,1,0:T(8,128)(2,1)} %get-tuple-element.55), channel_id=1, source_target_pairs={{0,16},{16,1},{1,17},{17,2},{2,18},{18,3},{3,19},{19,4},{4,20},{20... | collective-permute-start | bytes 1572872 | tf_op jit(solution)/shard_map/ppermute | solution.py:389
  82.7 18.4 %all-to-all-start.3 = ((bf16[16,136,128]{2,1,0:T(8,128)(2,1)}), bf16[16,136,128]{2,1,0:T(8,128)(2,1)S(1)}, u32[]{:S(2)}, u32[]{:S(2)}) async-start(bf16[16,136,128]{2,1,0:T(8,128)(2,1)} %get-tuple-element.52), calls=%async_computation.3 | async-start | bytes 1114112 | tf_op jit(solution)/shard_map/all_to_all | solution.py:470
  86.7 3.5 %copy-start.1 = (s32[3]{0:T(128)}, s32[3]{0:T(128)S(1)}, u32[]{:S(2)}) copy-start(s32[3]{0:T(128)S(1)} %pad_add_fusion.site) | copy-start | bytes 40
  86.7 1.0 copy-start.6
  90.2 0.7 copy-start.7
  99.5 1.6 %copy-start.13 = (bf16[16,128,128]{2,1,0:T(8,128)(2,1)}, bf16[16,128,128]{2,1,0:T(8,128)(2,1)S(1)}, u32[]{:S(2)}) copy-start(bf16[16,128,128]{2,1,0:T(8,128)(2,1)S(1)} %collective-permute-done.2.low) | copy-start | bytes 1572868
  101.1 0.8 copy-start.8
  106.7 11.5 %all-to-all-start.4 = ((bf16[16,72,128]{2,1,0:T(8,128)(2,1)}), bf16[16,72,128]{2,1,0:T(8,128)(2,1)S(1)}, u32[]{:S(2)}, u32[]{:S(2)}) async-start(bf16[16,72,128]{2,1,0:T(8,128)(2,1)} %get-tuple-element.58), calls=%async_computation.4 | async-start | bytes 589824 | tf_op jit(solution)/shard_map/all_to_all | solution.py:495
  111.5 13.2 %collective-permute-start.5 = (bf16[4,128,128]{2,1,0:T(8,128)(2,1)S(1)}, bf16[4,128,128]{2,1,0:T(8,128)(2,1)S(1)}, u32[]{:S(2)}, u32[]{:S(2)}) collective-permute-start(bf16[4,128,128]{2,1,0:T(8,128)(2,1)S(1)} %get-tuple-element.78), channel_id=1, source_target_pairs={{0,32},{32,0},{64,96},{96,64},{1,33},{33,1},{65,97},{97,65},{2,34}... | collective-permute-start | bytes 393224 | tf_op jit(solution)/shard_map/ppermute | solution.py:397
  111.6 13.2 %collective-permute-start.7 = (bf16[4,128,128]{2,1,0:T(8,128)(2,1)S(1)}, bf16[4,128,128]{2,1,0:T(8,128)(2,1)S(1)}, u32[]{:S(2)}, u32[]{:S(2)}) collective-permute-start(bf16[4,128,128]{2,1,0:T(8,128)(2,1)S(1)} %get-tuple-element.79), channel_id=1, source_target_pairs={{0,96},{32,64},{64,32},{96,0},{1,97},{33,65},{65,33},{97,1},{2,98}... | collective-permute-start | bytes 393224 | tf_op jit(solution)/shard_map/ppermute | solution.py:397
  111.6 13.1 %collective-permute-start.6 = (bf16[4,128,128]{2,1,0:T(8,128)(2,1)S(1)}, bf16[4,128,128]{2,1,0:T(8,128)(2,1)S(1)}, u32[]{:S(2)}, u32[]{:S(2)}) collective-permute-start(bf16[4,128,128]{2,1,0:T(8,128)(2,1)S(1)} %get-tuple-element.80), channel_id=1, source_target_pairs={{0,64},{32,96},{64,0},{96,32},{1,65},{33,97},{65,1},{97,33},{2,66}... | collective-permute-start | bytes 393224 | tf_op jit(solution)/shard_map/ppermute | solution.py:397
  119.4 25.5 %all-to-all-start.5 = ((bf16[64,16,512]{2,1,0:T(8,128)(2,1)}), bf16[64,16,512]{2,1,0:T(8,128)(2,1)S(1)}, u32[]{:S(2)}, u32[]{:S(2)}) async-start(bf16[64,16,512]{2,1,0:T(8,128)(2,1)} %get-tuple-element.59), calls=%async_computation.5 | async-start | bytes 2097152 | tf_op jit(solution)/shard_map/all_to_all | solution.py:503
  124.8 5.0 %collective-permute-start.8 = (bf16[4,128,128]{2,1,0:T(8,128)(2,1)S(1)}, bf16[4,128,128]{2,1,0:T(8,128)(2,1)S(1)}, u32[]{:S(2)}, u32[]{:S(2)}) collective-permute-start(bf16[4,128,128]{2,1,0:T(8,128)(2,1)S(1)} %pad_maximum_fusion.1), channel_id=1, source_target_pairs={{0,8},{8,0},{16,24},{24,16},{1,9},{9,1},{17,25},{25,17},{2,10},{10... | collective-permute-start | bytes 393224 | tf_op jit(solution)/shard_map/ppermute | solution.py:397
  127.3 14.7 %collective-permute-start.9 = (bf16[4,128,128]{2,1,0:T(8,128)(2,1)S(1)}, bf16[4,128,128]{2,1,0:T(8,128)(2,1)S(1)}, u32[]{:S(2)}, u32[]{:S(2)}) collective-permute-start(bf16[4,128,128]{2,1,0:T(8,128)(2,1)S(1)} %pad_maximum_fusion.2), channel_id=1, source_target_pairs={{0,16},{8,24},{16,0},{24,8},{1,17},{9,25},{17,1},{25,9},{2,18},{10... | collective-permute-start | bytes 393224 | tf_op jit(solution)/shard_map/ppermute | solution.py:397
  128.7 16.3 %collective-permute-start.10 = (bf16[4,128,128]{2,1,0:T(8,128)(2,1)S(1)}, bf16[4,128,128]{2,1,0:T(8,128)(2,1)S(1)}, u32[]{:S(2)}, u32[]{:S(2)}) collective-permute-start(bf16[4,128,128]{2,1,0:T(8,128)(2,1)S(1)} %pad_maximum_fusion.3), channel_id=1, source_target_pairs={{0,24},{8,16},{16,8},{24,0},{1,25},{9,17},{17,9},{25,1},{2,26},{10... | collective-permute-start | bytes 393224 | tf_op jit(solution)/shard_map/ppermute | solution.py:397
  129.8 16.2 %copy-start.14 = (bf16[4,128,128]{2,1,0:T(8,128)(2,1)}, bf16[4,128,128]{2,1,0:T(8,128)(2,1)S(1)}, u32[]{:S(2)}) copy-start(bf16[4,128,128]{2,1,0:T(8,128)(2,1)S(1)} %collective-permute-done.8.kv1) | copy-start | bytes 393220
  142.0 4.0 %copy-start.15 = (bf16[4,128,128]{2,1,0:T(8,128)(2,1)}, bf16[4,128,128]{2,1,0:T(8,128)(2,1)S(1)}, u32[]{:S(2)}) copy-start(bf16[4,128,128]{2,1,0:T(8,128)(2,1)S(1)} %collective-permute-done.9.kv2) | copy-start | bytes 393220
  145.0 1.0 copy-start.16
  145.0 4.8 %collective-permute-start.11 = (bf16[64,16,512]{2,1,0:T(8,128)(2,1)S(1)}, bf16[64,16,512]{2,1,0:T(8,128)(2,1)S(1)}, u32[]{:S(2)}, u32[]{:S(2)}) collective-permute-start(bf16[64,16,512]{2,1,0:T(8,128)(2,1)S(1)} %all-to-all-done.5.near), channel_id=1, source_target_pairs={{0,8},{8,0},{1,9},{9,1},{2,10},{10,2},{3,11},{11,3},{4,12},{12,4},... | collective-permute-start | bytes 3145736 | tf_op jit(solution)/shard_map/ppermute | solution.py:393
  146.0 3.8 %copy-start.2 = (bf16[512,512]{1,0:T(8,128)(2,1)S(1)}, bf16[512,512]{1,0:T(8,128)(2,1)}, u32[]{:S(2)}) copy-start(bf16[512,512]{1,0:T(8,128)(2,1)} %wk.5) | copy-start | bytes 1572868
  146.0 3.8 %copy-start.3 = (bf16[512,512]{1,0:T(8,128)(2,1)S(1)}, bf16[512,512]{1,0:T(8,128)(2,1)}, u32[]{:S(2)}) copy-start(bf16[512,512]{1,0:T(8,128)(2,1)} %wv.5) | copy-start | bytes 1572868
  146.0 3.8 %copy-start.4 = (bf16[512,512]{1,0:T(8,128)(2,1)S(1)}, bf16[512,512]{1,0:T(8,128)(2,1)}, u32[]{:S(2)}) copy-start(bf16[512,512]{1,0:T(8,128)(2,1)} %wq.5) | copy-start | bytes 1572868
  146.0 3.8 %copy-start.5 = (f32[512]{0:T(512)S(1)}, f32[512]{0:T(512)}, u32[]{:S(2)}) copy-start(f32[512]{0:T(512)} %param.11) | copy-start | bytes 6148

commit v7 on v6

--- a/solution.py
+++ b/solution.py
@@ -502,6 +502,8 @@
     )(arrived)
     near = lax.all_to_all(share, CHIPS, 0, 0, tiled=True)
     kv = [jnp.stack([piece[step] for piece in turn]) for step in range(4)]
+    grad_temper = temper_sum[:, 0] / (temper * math.log2(math.e))
+    kv[1], grad_temper = lax.optimization_barrier((kv[1], grad_temper))
     kv = [kv[0]] + [swap_near(kv[step], ("zl", "cr"), step) for step in range(1, 4)]
     near, *kv = lax.optimization_barrier((near, *kv))
     layer_out, grad_tokens = pl.pallas_call(
@@ -522,7 +524,6 @@
         scratch_shapes=[pltpu.VMEM((4, D, D), BF)],
         compiler_params=params(16),
     )(core.reshape(1), near, far, gain, w_query, w_key, w_value)
-    grad_temper = temper_sum[:, 0] / (temper * math.log2(math.e))
     return (
         layer_out.reshape(tokens.shape),
         grad_tokens.reshape(tokens.shape),

time: 154 us -> 156 us (1.013)
    ppermute x6, waiting for transfers between devices: 15.2 us -> 18.7 us  [swap_near(): return lax.ppermute(block, axes, [(i, i ^ step) for i in range(4)])]
    all_to_all x1, waiting for transfers between devices: 2.65 us -> 0.01 us  [local(): arrived = lax.all_to_all(parts, RING, 0, 0, tiled=True)]
    all_to_all x1, starting transfers between devices: 5.25 us -> 7.31 us  [local(): near = lax.all_to_all(share, CHIPS, 0, 0, tiled=True)]
where the time goes in v7:
time: 156 us; the launch traced here: 155 us
  Pallas kernels  50.2 us (32%)
  waiting for transfers between devices  48 us (31%)
  starting transfers between devices  46.4 us (30%)
  local copies, waits for them, and re-layouts  6.55 us (4%)
  between operations  2.14 us (1%)
  other arithmetic  1.92 us (1%)
    pallas_call x1, Pallas kernels, local(): pl.pallas_call(attend_kernel, cost_estimate=cost(36), out_shape=(whole(wi...  26.3 us
    ppermute x6, waiting for transfers between devices, swap_near(): return lax.ppermute(block, axes, [(i, i ^ step) for i in range(4)])  18.7 us
    all_to_all x1, waiting for transfers between devices, local(): qb = lax.all_to_all(qb_send, GROUP, 0, 0, tiled=True)  10.9 us
    ppermute x4, waiting for transfers between devices, shift(): lax.ppermute(block, RING, [(spots[t], spots[(t + step) % 16]) for t in ra...  8.61 us
    all_to_all x1, starting transfers between devices, local(): own = lax.all_to_all(kv_send, GROUP, 0, 0, tiled=True)  7.34 us
    all_to_all x1, starting transfers between devices, local(): near = lax.all_to_all(share, CHIPS, 0, 0, tiled=True)  7.31 us
    ppermute x6, starting transfers between devices, swap_near(): return lax.ppermute(block, axes, [(i, i ^ step) for i in range(4)])  7.06 us
    ppermute x4, starting transfers between devices, shift(): lax.ppermute(block, RING, [(spots[t], spots[(t + step) % 16]) for t in ra...  6.99 us
  transfers between devices with their start and end apart: 18, of which 8 were waited for; matrix products, arithmetic and copies ran while one was open for 3% of the time, Pallas kernels for 25%

profile of v7, /device:TPU:1, one launch (start us, length us, event | category | flops | bytes accessed | tf_op | source)
XLA Modules:
  0.0 155.2 jit_solution(1808760431030046170)
XLA Ops:
  0.6 4.0 %shard_map.161 = (bf16[16,128,128]{2,1,0:T(8,128)(2,1)}, f32[256,128]{1,0:T(8,128)}) custom-call(bf16[256,512]{1,0:T(8,128)(2,1)} %bitcast.30, f32[1,512]{1,0:T(1,128)} %bitcast.25, bf16[512,512]{1,0:T(8,128)(2,1)} %wk.5, bf16[512,512]{1,0:T(8,128)(2,1)} %wv.5), custom_call_target="tpu_custom_call" | custom-call | flops 3000000000 | bytes 3000000 | tf_op jit(solution)/shard_map/pallas_call | solution.py:414
  4.6 7.3 %all-to-all-start = ((bf16[16,128,128]{2,1,0:T(8,128)(2,1)}), bf16[16,128,128]{2,1,0:T(8,128)(2,1)S(1)}, u32[]{:S(2)}, u32[]{:S(2)}) async-start(bf16[16,128,128]{2,1,0:T(8,128)(2,1)} %get-tuple-element.46), calls=%async_computation | async-start | bytes 1048576 | tf_op jit(solution)/shard_map/all_to_all | solution.py:430
  11.9 5.1 %shard_map.162 = (bf16[16,136,128]{2,1,0:T(8,128)(2,1)}, bf16[8,128,1024]{2,1,0:T(8,128)(2,1)}) custom-call(bf16[256,512]{1,0:T(8,128)(2,1)} %bitcast.31, f32[1,512]{1,0:T(1,128)} %bitcast.26, bf16[256,512]{1,0:T(8,128)(2,1)} %bitcast.29, s32[2,27]{1,0:T(2,128)} %bitcast.33, s32[2,27]{1,0:T(2,128)} %bitcast.34, f32[256,128]{1,0:T(8,128)} %get-tuple-element.43.factors_in, ...), custom_call_target="tpu_custom_call" | custom-call | flops 4000000000 | bytes 4000000 | tf_op jit(solution)/shard_map/pallas_call | solution.py:420
  17.0 4.6 %all-to-all-done.own.kv = bf16[16,128,128]{2,1,0:T(8,128)(2,1)S(1)} async-done(((bf16[16,128,128]{2,1,0:T(8,128)(2,1)}), bf16[16,128,128]{2,1,0:T(8,128)(2,1)S(1)}, u32[]{:S(2)}, u32[]{:S(2)}) %all-to-all-start) | async-done | bytes 524320 | tf_op jit(solution)/shard_map/all_to_all | solution.py:430
  21.6 5.5 %collective-permute-start.1 = (bf16[16,128,128]{2,1,0:T(8,128)(2,1)S(1)}, bf16[16,128,128]{2,1,0:T(8,128)(2,1)S(1)}, u32[]{:S(2)}, u32[]{:S(2)}) collective-permute-start(bf16[16,128,128]{2,1,0:T(8,128)(2,1)S(1)} %all-to-all-done.own.kv), channel_id=1, source_target_pairs={{0,23},{16,0},{1,16},{17,1},{2,17},{18,2},{3,18},{19,3},{4,19},{20... | collective-permute-start | bytes 1572872 | tf_op jit(solution)/shard_map/ppermute | solution.py:389
  27.1 3.9 %all-to-all-start.1 = ((bf16[16,136,128]{2,1,0:T(8,128)(2,1)}), bf16[16,136,128]{2,1,0:T(8,128)(2,1)S(1)}, u32[]{:S(2)}, u32[]{:S(2)}) async-start(bf16[16,136,128]{2,1,0:T(8,128)(2,1)} %get-tuple-element.47), calls=%async_computation.1 | async-start | bytes 1114112 | tf_op jit(solution)/shard_map/all_to_all | solution.py:434
  31.0 0.6 dynamic_slice.3
  32.9 0.6 pad_maximum_fusion.4.coef
  33.4 10.9 %all-to-all-done.1.qb = bf16[16,136,128]{2,1,0:T(8,128)(2,1)S(1)} async-done(((bf16[16,136,128]{2,1,0:T(8,128)(2,1)}), bf16[16,136,128]{2,1,0:T(8,128)(2,1)S(1)}, u32[]{:S(2)}, u32[]{:S(2)}) %all-to-all-start.1) | async-done | bytes 557088 | tf_op jit(solution)/shard_map/all_to_all | solution.py:434
  44.3 0.8 copy-done.11
  45.1 0.2 copy-done.12
  45.3 0.2 copy-done.9
  45.4 4.0 %all-to-all-start.2 = ((bf16[8,128,1024]{2,1,0:T(8,128)(2,1)}), bf16[8,128,1024]{2,1,0:T(8,128)(2,1)S(1)}, u32[]{:S(2)}, u32[]{:S(2)}) async-start(bf16[8,128,1024]{2,1,0:T(8,128)(2,1)} %get-tuple-element.49), calls=%async_computation.2 | async-start | bytes 4194304 | tf_op jit(solution)/shard_map/all_to_all | solution.py:436
  49.5 26.3 %shard_map.163 = (bf16[16,136,128]{2,1,0:T(8,128)(2,1)}, bf16[16,128,128]{2,1,0:T(8,128)(2,1)}, f32[16,128,128]{2,1,0:T(8,128)}, bf16[16,128,128]{2,1,0:T(8,128)(2,1)}, bf16[16,128,128]{2,1,0:T(8,128)(2,1)}) custom-call(f32[2]{0:T(128)} %pad_maximum_fusion.4.coef, bf16[16,128,128]{2,1,0:T(8,128)(2,1)} %copy-done.10, bf16[16,128,128]{2,1,0:T(8,128)(2,1)} %copy-done.12, ...), custom_call_target="tpu_custom_call" | custom-call | flops 35999997952 | bytes 36000000 | tf_op jit(solution)/shard_map/pallas_call | solution.py:441
  75.7 3.7 %all-to-all-done.2.near = bf16[8,128,1024]{2,1,0:T(8,128)(2,1)S(1)} async-done(((bf16[8,128,1024]{2,1,0:T(8,128)(2,1)}), bf16[8,128,1024]{2,1,0:T(8,128)(2,1)S(1)}, u32[]{:S(2)}, u32[]{:S(2)}) %all-to-all-start.2) | async-done | bytes 2097184 | tf_op jit(solution)/shard_map/all_to_all | solution.py:436
  79.4 1.8 %collective-permute-start.4 = (bf16[8,128,1024]{2,1,0:T(8,128)(2,1)S(1)}, bf16[8,128,1024]{2,1,0:T(8,128)(2,1)}, u32[]{:S(2)}, u32[]{:S(2)}) collective-permute-start(bf16[8,128,1024]{2,1,0:T(8,128)(2,1)S(1)} %all-to-all-done.2.near), channel_id=1, source_target_pairs={{0,8},{8,0},{1,9},{9,1},{2,10},{10,2},{3,11},{11,3},{4,12},{12,4},... | collective-permute-start | bytes 6291464 | tf_op jit(solution)/shard_map/ppermute | solution.py:393
  81.2 0.3 collective-permute-start.2
  81.6 1.1 collective-permute-start.3
  82.7 3.9 %all-to-all-start.3 = ((bf16[16,136,128]{2,1,0:T(8,128)(2,1)}), bf16[16,136,128]{2,1,0:T(8,128)(2,1)S(1)}, u32[]{:S(2)}, u32[]{:S(2)}) async-start(bf16[16,136,128]{2,1,0:T(8,128)(2,1)} %get-tuple-element.54), calls=%async_computation.3 | async-start | bytes 1114112 | tf_op jit(solution)/shard_map/all_to_all | solution.py:470
  86.6 0.1 pad_add_fusion.site
  86.7 1.0 copy-done.6
  87.8 2.4 %shard_map.164.early = bf16[128,512]{1,0:T(8,128)(2,1)S(1)} custom-call(s32[3]{0:T(128)S(1)} %pad_add_fusion.site, bf16[16,128,128]{2,1,0:T(8,128)(2,1)S(1)} %copy-done.6, bf16[8,128,1024]{2,1,0:T(8,128)(2,1)S(1)} %all-to-all-done.2.near, bf16[8,128,1024]{2,1,0:T(8,128)(2,1)} %collective-permute-done.4.far), custom_call_target="tpu_custom_call" | custom-call | flops 3000000000 | bytes 3000000 | tf_op jit(solution)/shard_map/pallas_call | solution.py:472
  90.2 0.6 copy-done.7
  90.9 8.6 %collective-permute-done.2.low = bf16[16,128,128]{2,1,0:T(8,128)(2,1)S(1)} collective-permute-done((bf16[16,128,128]{2,1,0:T(8,128)(2,1)}, bf16[16,128,128]{2,1,0:T(8,128)(2,1)S(1)}, u32[]{:S(2)}, u32[]{:S(2)}) %collective-permute-start.2) | collective-permute-done | bytes 524320 | tf_op jit(solution)/shard_map/ppermute | solution.py:389
  99.5 1.6 %all-to-all-done.3.mq = bf16[16,136,128]{2,1,0:T(8,128)(2,1)S(1)} async-done(((bf16[16,136,128]{2,1,0:T(8,128)(2,1)}), bf16[16,136,128]{2,1,0:T(8,128)(2,1)S(1)}, u32[]{:S(2)}, u32[]{:S(2)}) %all-to-all-start.3) | async-done | bytes 557088 | tf_op jit(solution)/shard_map/all_to_all | solution.py:470
  101.1 0.8 copy-done.8
  101.9 4.8 %shard_map.165 = (bf16[4,4,128,128]{3,2,1,0:T(8,128)(2,1)}, bf16[16,72,128]{2,1,0:T(8,128)(2,1)}) custom-call(s32[3]{0:T(128)} %copy-done.1, f32[16,128,128]{2,1,0:T(8,128)} %get-tuple-element.55.own, bf16[16,128,128]{2,1,0:T(8,128)(2,1)} %copy-done.13, bf16[16,128,128]{2,1,0:T(8,128)(2,1)} %collective-permute-done.3.high, bf16[16,128,128]{2,1,0:T(8,128)(2,1)} %copy-done.10, ...), custom_call_target="tpu_custom_call" | custom-call | flops 7000000000 | bytes 7000000 | tf_op jit(solution)/shard_map/pallas_call | solution.py:484
  106.7 3.7 %all-to-all-start.4 = ((bf16[16,72,128]{2,1,0:T(8,128)(2,1)}), bf16[16,72,128]{2,1,0:T(8,128)(2,1)S(1)}, u32[]{:S(2)}, u32[]{:S(2)}) async-start(bf16[16,72,128]{2,1,0:T(8,128)(2,1)} %get-tuple-element.60), calls=%async_computation.4 | async-start | bytes 589824 | tf_op jit(solution)/shard_map/all_to_all | solution.py:495
  110.4 1.1 slice_bitcast_fusion.2
  111.5 0.1 collective-permute-start.5
  111.6 0.1 collective-permute-start.7
  111.6 3.1 %collective-permute-start.6 = (bf16[4,128,128]{2,1,0:T(8,128)(2,1)S(1)}, bf16[4,128,128]{2,1,0:T(8,128)(2,1)S(1)}, u32[]{:S(2)}, u32[]{:S(2)}) collective-permute-start(bf16[4,128,128]{2,1,0:T(8,128)(2,1)S(1)} %get-tuple-element.84), channel_id=1, source_target_pairs={{0,64},{32,96},{64,0},{96,32},{1,65},{33,97},{65,1},{97,33},{2,66}... | collective-permute-start | bytes 393224 | tf_op jit(solution)/shard_map/ppermute | solution.py:397
  114.8 0.8 slice_bitcast_fusion.3
  115.7 4.5 %collective-permute-done.7 = bf16[4,128,128]{2,1,0:T(8,128)(2,1)S(1)} collective-permute-done((bf16[4,128,128]{2,1,0:T(8,128)(2,1)S(1)}, bf16[4,128,128]{2,1,0:T(8,128)(2,1)S(1)}, u32[]{:S(2)}, u32[]{:S(2)}) %collective-permute-start.7) | collective-permute-done | bytes 131104 | tf_op jit(solution)/shard_map/ppermute | solution.py:397
  120.2 1.2 shard_map.166
  121.3 7.3 %all-to-all-start.5 = ((bf16[64,16,512]{2,1,0:T(8,128)(2,1)}), bf16[64,16,512]{2,1,0:T(8,128)(2,1)S(1)}, u32[]{:S(2)}, u32[]{:S(2)}) async-start(bf16[64,16,512]{2,1,0:T(8,128)(2,1)} %get-tuple-element.61), calls=%async_computation.5 | async-start | bytes 2097152 | tf_op jit(solution)/shard_map/all_to_all | solution.py:503
  128.7 1.1 collective-permute-start.9
  129.8 2.6 %collective-permute-start.10 = (bf16[4,128,128]{2,1,0:T(8,128)(2,1)S(1)}, bf16[4,128,128]{2,1,0:T(8,128)(2,1)S(1)}, u32[]{:S(2)}, u32[]{:S(2)}) collective-permute-start(bf16[4,128,128]{2,1,0:T(8,128)(2,1)S(1)} %pad_maximum_fusion.3), channel_id=1, source_target_pairs={{0,24},{8,16},{16,8},{24,0},{1,25},{9,17},{17,9},{25,1},{2,26},{10... | collective-permute-start | bytes 393224 | tf_op jit(solution)/shard_map/ppermute | solution.py:397
  132.5 0.1 slice_reduce_fusion
  132.6 0.5 multiply_divide_fusion
  133.1 0.7 pad_maximum_fusion.kv0
  133.8 5.7 %collective-permute-done.9.kv2 = bf16[4,128,128]{2,1,0:T(8,128)(2,1)S(1)} collective-permute-done((bf16[4,128,128]{2,1,0:T(8,128)(2,1)S(1)}, bf16[4,128,128]{2,1,0:T(8,128)(2,1)S(1)}, u32[]{:S(2)}, u32[]{:S(2)}) %collective-permute-start.9) | collective-permute-done | bytes 131104 | tf_op jit(solution)/shard_map/ppermute | solution.py:397
  139.5 8.5 %collective-permute-done.10.kv3 = bf16[4,128,128]{2,1,0:T(8,128)(2,1)S(1)} collective-permute-done((bf16[4,128,128]{2,1,0:T(8,128)(2,1)S(1)}, bf16[4,128,128]{2,1,0:T(8,128)(2,1)S(1)}, u32[]{:S(2)}, u32[]{:S(2)}) %collective-permute-start.10) | collective-permute-done | bytes 131104 | tf_op jit(solution)/shard_map/ppermute | solution.py:397
  148.0 0.4 collective-permute-start.11
  148.4 0.2 copy-done.15
  148.6 0.0 copy-done.16
  148.7 3.6 %shard_map.167 = (bf16[256,512]{1,0:T(8,128)(2,1)}, f32[256,512]{1,0:T(8,128)}) custom-call(s32[3]{0:T(128)} %copy-done.1, bf16[256,512]{1,0:T(8,128)(2,1)} %bitcast.32, f32[1,512]{1,0:T(1,128)} %bitcast.27, bf16[16,136,128]{2,1,0:T(8,128)(2,1)} %copy-done.8, bf16[4,128,128]{2,1,0:T(8,128)(2,1)} %pad_maximum_fusion.kv0, bf16[4,128,128]{2,1,0:T(8,128)(2,1)} %copy-done.16, ...), custom_call_target="tpu_custom_call" | custom-call | flops 4000000000 | bytes 4000000 | tf_op jit(solution)/shard_map/pallas_call | solution.py:509
  152.4 2.8 %shard_map.168 = (f32[512,512]{1,0:T(8,128)}, f32[512,512]{1,0:T(8,128)}, f32[512,512]{1,0:T(8,128)}, f32[512,512]{1,0:T(8,128)}, f32[1,512]{1,0:T(1,128)}) custom-call(s32[1]{0:T(128)} %bitcast.core, bf16[64,16,512]{2,1,0:T(8,128)(2,1)S(1)} %all-to-all-done.5.near, bf16[64,16,512]{2,1,0:T(8,128)(2,1)S(1)} %collective-permute-done.11.far, ...), custom_call_target="tpu_custom_call" | custom-call | flops 5000000000 | bytes 5000000 | tf_op jit(solution)/shard_map/pallas_call | solution.py:519
  (46 shorter events, 0.2 us)
Async XLA Ops:
  4.6 17.0 %all-to-all-start = ((bf16[16,128,128]{2,1,0:T(8,128)(2,1)}), bf16[16,128,128]{2,1,0:T(8,128)(2,1)S(1)}, u32[]{:S(2)}, u32[]{:S(2)}) async-start(bf16[16,128,128]{2,1,0:T(8,128)(2,1)} %get-tuple-element.46), calls=%async_computation | async-start | bytes 1048576 | tf_op jit(solution)/shard_map/all_to_all | solution.py:430
  11.9 19.0 %copy-start.17 = (f32[8]{0:T(128)S(1)}, f32[8]{0:T(128)}, u32[]{:S(2)}) copy-start(f32[8]{0:T(128)} %param.16) | copy-start | bytes 100
  21.6 23.7 %copy-start.10 = (bf16[16,128,128]{2,1,0:T(8,128)(2,1)}, bf16[16,128,128]{2,1,0:T(8,128)(2,1)S(1)}, u32[]{:S(2)}) copy-start(bf16[16,128,128]{2,1,0:T(8,128)(2,1)S(1)} %all-to-all-done.own.kv) | copy-start | bytes 1572868
  21.6 22.7 %collective-permute-start.1 = (bf16[16,128,128]{2,1,0:T(8,128)(2,1)S(1)}, bf16[16,128,128]{2,1,0:T(8,128)(2,1)S(1)}, u32[]{:S(2)}, u32[]{:S(2)}) collective-permute-start(bf16[16,128,128]{2,1,0:T(8,128)(2,1)S(1)} %all-to-all-done.own.kv), channel_id=1, source_target_pairs={{0,23},{16,0},{1,16},{17,1},{2,17},{18,2},{3,18},{19,3},{4,19},{20... | collective-permute-start | bytes 1572872 | tf_op jit(solution)/shard_map/ppermute | solution.py:389
  27.1 17.2 %collective-permute-start = (bf16[16,128,128]{2,1,0:T(8,128)(2,1)S(1)}, bf16[16,128,128]{2,1,0:T(8,128)(2,1)S(1)}, u32[]{:S(2)}, u32[]{:S(2)}) collective-permute-start(bf16[16,128,128]{2,1,0:T(8,128)(2,1)S(1)} %all-to-all-done.own.kv), channel_id=1, source_target_pairs={{0,16},{16,1},{1,17},{17,2},{2,18},{18,3},{3,19},{19,4},{4,20},{20... | collective-permute-start | bytes 1572872 | tf_op jit(solution)/shard_map/ppermute | solution.py:389
  27.1 17.2 %all-to-all-start.1 = ((bf16[16,136,128]{2,1,0:T(8,128)(2,1)}), bf16[16,136,128]{2,1,0:T(8,128)(2,1)S(1)}, u32[]{:S(2)}, u32[]{:S(2)}) async-start(bf16[16,136,128]{2,1,0:T(8,128)(2,1)} %get-tuple-element.47), calls=%async_computation.1 | async-start | bytes 1114112 | tf_op jit(solution)/shard_map/all_to_all | solution.py:434
  44.3 1.1 copy-start.9
  44.3 0.8 copy-start.11
  44.3 1.0 copy-start.12
  45.4 34.0 %all-to-all-start.2 = ((bf16[8,128,1024]{2,1,0:T(8,128)(2,1)}), bf16[8,128,1024]{2,1,0:T(8,128)(2,1)S(1)}, u32[]{:S(2)}, u32[]{:S(2)}) async-start(bf16[8,128,1024]{2,1,0:T(8,128)(2,1)} %get-tuple-element.49), calls=%async_computation.2 | async-start | bytes 4194304 | tf_op jit(solution)/shard_map/all_to_all | solution.py:436
  79.4 10.8 %copy-start = (bf16[8,128,1024]{2,1,0:T(8,128)(2,1)}, bf16[8,128,1024]{2,1,0:T(8,128)(2,1)S(1)}, u32[]{:S(2)}) copy-start(bf16[8,128,1024]{2,1,0:T(8,128)(2,1)S(1)} %all-to-all-done.2.near) | copy-start | bytes 6291460
  79.4 7.3 %collective-permute-start.4 = (bf16[8,128,1024]{2,1,0:T(8,128)(2,1)S(1)}, bf16[8,128,1024]{2,1,0:T(8,128)(2,1)}, u32[]{:S(2)}, u32[]{:S(2)}) collective-permute-start(bf16[8,128,1024]{2,1,0:T(8,128)(2,1)S(1)} %all-to-all-done.2.near), channel_id=1, source_target_pairs={{0,8},{8,0},{1,9},{9,1},{2,10},{10,2},{3,11},{11,3},{4,12},{12,4},... | collective-permute-start | bytes 6291464 | tf_op jit(solution)/shard_map/ppermute | solution.py:393
  81.2 18.2 %collective-permute-start.2 = (bf16[16,128,128]{2,1,0:T(8,128)(2,1)}, bf16[16,128,128]{2,1,0:T(8,128)(2,1)S(1)}, u32[]{:S(2)}, u32[]{:S(2)}) collective-permute-start(bf16[16,128,128]{2,1,0:T(8,128)(2,1)} %get-tuple-element.56), channel_id=1, source_target_pairs={{0,23},{16,0},{1,16},{17,1},{2,17},{18,2},{3,18},{19,3},{4,19},{20... | collective-permute-start | bytes 1572872 | tf_op jit(solution)/shard_map/ppermute | solution.py:389
  81.6 17.9 %collective-permute-start.3 = (bf16[16,128,128]{2,1,0:T(8,128)(2,1)}, bf16[16,128,128]{2,1,0:T(8,128)(2,1)}, u32[]{:S(2)}, u32[]{:S(2)}) collective-permute-start(bf16[16,128,128]{2,1,0:T(8,128)(2,1)} %get-tuple-element.57), channel_id=1, source_target_pairs={{0,16},{16,1},{1,17},{17,2},{2,18},{18,3},{3,19},{19,4},{4,20},{20... | collective-permute-start | bytes 1572872 | tf_op jit(solution)/shard_map/ppermute | solution.py:389
  82.7 18.4 %all-to-all-start.3 = ((bf16[16,136,128]{2,1,0:T(8,128)(2,1)}), bf16[16,136,128]{2,1,0:T(8,128)(2,1)S(1)}, u32[]{:S(2)}, u32[]{:S(2)}) async-start(bf16[16,136,128]{2,1,0:T(8,128)(2,1)} %get-tuple-element.54), calls=%async_computation.3 | async-start | bytes 1114112 | tf_op jit(solution)/shard_map/all_to_all | solution.py:470
  86.7 3.5 %copy-start.1 = (s32[3]{0:T(128)}, s32[3]{0:T(128)S(1)}, u32[]{:S(2)}) copy-start(s32[3]{0:T(128)S(1)} %pad_add_fusion.site) | copy-start | bytes 40
  86.7 1.0 copy-start.6
  90.2 0.7 copy-start.7
  99.5 1.6 %copy-start.13 = (bf16[16,128,128]{2,1,0:T(8,128)(2,1)}, bf16[16,128,128]{2,1,0:T(8,128)(2,1)S(1)}, u32[]{:S(2)}) copy-start(bf16[16,128,128]{2,1,0:T(8,128)(2,1)S(1)} %collective-permute-done.2.low) | copy-start | bytes 1572868
  101.1 0.8 copy-start.8
  106.7 13.4 %all-to-all-start.4 = ((bf16[16,72,128]{2,1,0:T(8,128)(2,1)}), bf16[16,72,128]{2,1,0:T(8,128)(2,1)S(1)}, u32[]{:S(2)}, u32[]{:S(2)}) async-start(bf16[16,72,128]{2,1,0:T(8,128)(2,1)} %get-tuple-element.60), calls=%async_computation.4 | async-start | bytes 589824 | tf_op jit(solution)/shard_map/all_to_all | solution.py:495
  111.5 4.2 %collective-permute-start.5 = (bf16[4,128,128]{2,1,0:T(8,128)(2,1)S(1)}, bf16[4,128,128]{2,1,0:T(8,128)(2,1)S(1)}, u32[]{:S(2)}, u32[]{:S(2)}) collective-permute-start(bf16[4,128,128]{2,1,0:T(8,128)(2,1)S(1)} %get-tuple-element.82), channel_id=1, source_target_pairs={{0,32},{32,0},{64,96},{96,64},{1,33},{33,1},{65,97},{97,65},{2,34}... | collective-permute-start | bytes 393224 | tf_op jit(solution)/shard_map/ppermute | solution.py:397
  111.6 8.6 %collective-permute-start.7 = (bf16[4,128,128]{2,1,0:T(8,128)(2,1)S(1)}, bf16[4,128,128]{2,1,0:T(8,128)(2,1)S(1)}, u32[]{:S(2)}, u32[]{:S(2)}) collective-permute-start(bf16[4,128,128]{2,1,0:T(8,128)(2,1)S(1)} %get-tuple-element.83), channel_id=1, source_target_pairs={{0,96},{32,64},{64,32},{96,0},{1,97},{33,65},{65,33},{97,1},{2,98}... | collective-permute-start | bytes 393224 | tf_op jit(solution)/shard_map/ppermute | solution.py:397
  111.6 17.0 %collective-permute-start.6 = (bf16[4,128,128]{2,1,0:T(8,128)(2,1)S(1)}, bf16[4,128,128]{2,1,0:T(8,128)(2,1)S(1)}, u32[]{:S(2)}, u32[]{:S(2)}) collective-permute-start(bf16[4,128,128]{2,1,0:T(8,128)(2,1)S(1)} %get-tuple-element.84), channel_id=1, source_target_pairs={{0,64},{32,96},{64,0},{96,32},{1,65},{33,97},{65,1},{97,33},{2,66}... | collective-permute-start | bytes 393224 | tf_op jit(solution)/shard_map/ppermute | solution.py:397
  121.3 26.7 %all-to-all-start.5 = ((bf16[64,16,512]{2,1,0:T(8,128)(2,1)}), bf16[64,16,512]{2,1,0:T(8,128)(2,1)S(1)}, u32[]{:S(2)}, u32[]{:S(2)}) async-start(bf16[64,16,512]{2,1,0:T(8,128)(2,1)} %get-tuple-element.61), calls=%async_computation.5 | async-start | bytes 2097152 | tf_op jit(solution)/shard_map/all_to_all | solution.py:503
  128.7 10.8 %collective-permute-start.9 = (bf16[4,128,128]{2,1,0:T(8,128)(2,1)S(1)}, bf16[4,128,128]{2,1,0:T(8,128)(2,1)S(1)}, u32[]{:S(2)}, u32[]{:S(2)}) collective-permute-start(bf16[4,128,128]{2,1,0:T(8,128)(2,1)S(1)} %pad_maximum_fusion.2), channel_id=1, source_target_pairs={{0,16},{8,24},{16,0},{24,8},{1,17},{9,25},{17,1},{25,9},{2,18},{10... | collective-permute-start | bytes 393224 | tf_op jit(solution)/shard_map/ppermute | solution.py:397
  129.8 18.2 %collective-permute-start.10 = (bf16[4,128,128]{2,1,0:T(8,128)(2,1)S(1)}, bf16[4,128,128]{2,1,0:T(8,128)(2,1)S(1)}, u32[]{:S(2)}, u32[]{:S(2)}) collective-permute-start(bf16[4,128,128]{2,1,0:T(8,128)(2,1)S(1)} %pad_maximum_fusion.3), channel_id=1, source_target_pairs={{0,24},{8,16},{16,8},{24,0},{1,25},{9,17},{17,9},{25,1},{2,26},{10... | collective-permute-start | bytes 393224 | tf_op jit(solution)/shard_map/ppermute | solution.py:397
  133.1 14.9 %collective-permute-start.8 = (bf16[4,128,128]{2,1,0:T(8,128)(2,1)S(1)}, bf16[4,128,128]{2,1,0:T(8,128)(2,1)S(1)}, u32[]{:S(2)}, u32[]{:S(2)}) collective-permute-start(bf16[4,128,128]{2,1,0:T(8,128)(2,1)S(1)} %pad_maximum_fusion.1), channel_id=1, source_target_pairs={{0,8},{8,0},{16,24},{24,16},{1,9},{9,1},{17,25},{25,17},{2,10},{10... | collective-permute-start | bytes 393224 | tf_op jit(solution)/shard_map/ppermute | solution.py:397
  133.8 18.5 %copy-start.2 = (bf16[512,512]{1,0:T(8,128)(2,1)S(1)}, bf16[512,512]{1,0:T(8,128)(2,1)}, u32[]{:S(2)}) copy-start(bf16[512,512]{1,0:T(8,128)(2,1)} %wk.5) | copy-start | bytes 1572868
  133.8 18.5 %copy-start.3 = (bf16[512,512]{1,0:T(8,128)(2,1)S(1)}, bf16[512,512]{1,0:T(8,128)(2,1)}, u32[]{:S(2)}) copy-start(bf16[512,512]{1,0:T(8,128)(2,1)} %wv.5) | copy-start | bytes 1572868
  133.8 18.5 %copy-start.4 = (bf16[512,512]{1,0:T(8,128)(2,1)S(1)}, bf16[512,512]{1,0:T(8,128)(2,1)}, u32[]{:S(2)}) copy-start(bf16[512,512]{1,0:T(8,128)(2,1)} %wq.5) | copy-start | bytes 1572868
  133.8 18.5 %copy-start.5 = (f32[512]{0:T(512)S(1)}, f32[512]{0:T(512)}, u32[]{:S(2)}) copy-start(f32[512]{0:T(512)} %param.11) | copy-start | bytes 6148
  139.5 8.9 %copy-start.14 = (bf16[4,128,128]{2,1,0:T(8,128)(2,1)}, bf16[4,128,128]{2,1,0:T(8,128)(2,1)S(1)}, u32[]{:S(2)}) copy-start(bf16[4,128,128]{2,1,0:T(8,128)(2,1)S(1)} %collective-permute-done.9.kv2) | copy-start | bytes 393220
  148.0 0.7 copy-start.15
  148.0 0.7 copy-start.16
  148.0 4.3 %collective-permute-start.11 = (bf16[64,16,512]{2,1,0:T(8,128)(2,1)S(1)}, bf16[64,16,512]{2,1,0:T(8,128)(2,1)S(1)}, u32[]{:S(2)}, u32[]{:S(2)}) collective-permute-start(bf16[64,16,512]{2,1,0:T(8,128)(2,1)S(1)} %all-to-all-done.5.near), channel_id=1, source_target_pairs={{0,8},{8,0},{1,9},{9,1},{2,10},{10,2},{3,11},{11,3},{4,12},{12,4},... | collective-permute-start | bytes 3145736 | tf_op jit(solution)/shard_map/ppermute | solution.py:393
